TPU v7x, 32 devices: a whole 2x2x4 slice. The times are simulated.
32 devices in a mesh: batch: 4 (over y, x), seq: 8 (over z, core).
Axes of the slice: x: 2, y: 2, z: 4, core: 2. Of those that a mesh axis runs over, the one named last changes fastest.
Arguments:
- tokens_in: bfloat16 [4, 4096, 1024], P('batch', 'seq'), may hold values from -6 to 6
- skip_in: bfloat16 [4, 4096, 1024], P('batch', 'seq'), may hold values from -6 to 6
- condition: bfloat16 [4, 4096, 1024], P('batch', 'seq'), may hold values from -3 to 3
- cotangent: bfloat16 [4, 4096, 1024], P('batch', 'seq'), may hold values from -6 to 6
- time_embed: float32 [4, 8, 1024], P('batch'), may hold values from -6 to 6
- lengths: int32 [4, 8], P('batch'), may hold values from 1 to 2048, 4096 in all within a row
- key_mask: int32 [4, 4096], P('batch'), may hold values 0 or 1
- drop_mask: int32 [4, 8], P('batch'), may hold values 0 or 1
- loss_mask: int32 [4, 4096], P('batch', 'seq'), may hold values from 0 to 1, as said below
- w_skip: bfloat16 [2048, 1024], replicated, may hold values from -0.125 to 0.125
- b_skip: bfloat16 [1024], replicated, may hold values from -2 to 2
- w_ada: bfloat16 [1024, 6144], replicated, may hold values from -0.1875 to 0.1875
- b_ada: bfloat16 [6144], replicated, may hold values from -3 to 3
- w_qkv: bfloat16 [1024, 3072], replicated, may hold values from -0.1875 to 0.1875
- b_qkv: bfloat16 [3072], replicated, may hold values from -2 to 2
- w_out: bfloat16 [1024, 1024], replicated, may hold values from -1.5 to 1.5
- b_out: bfloat16 [1024], replicated, may hold values from -2 to 2
- w_up: bfloat16 [1024, 4096], replicated, may hold values from -0.1875 to 0.1875
- b_up: bfloat16 [4096], replicated, may hold values from -2 to 2
- w_down: bfloat16 [4096, 1024], replicated, may hold values from -0.09375 to 0.09375
- b_down: bfloat16 [1024], replicated, may hold values from -2 to 2
Outputs:
- output: bfloat16 [4, 4096, 1024], P('batch', 'seq')
- grad_tokens: float32 [4, 4096, 1024], P('batch', 'seq')
- grad_skip: float32 [4, 4096, 1024], P('batch', 'seq')
- grad_w_skip: float32 [2048, 1024], P('seq')
- grad_b_skip: float32 [1024], P('seq')
- grad_w_ada: float32 [1024, 6144], P('seq')
- grad_b_ada: float32 [6144], P('seq')
- grad_w_qkv: float32 [1024, 3072], P('seq')
- grad_b_qkv: float32 [3072], P('seq')
- grad_w_out: float32 [1024, 1024], P('seq')
- grad_b_out: float32 [1024], P('seq')
- grad_w_up: float32 [1024, 4096], P('seq')
- grad_b_up: float32 [4096], P('seq')
- grad_w_down: float32 [4096, 1024], P('seq')
- grad_b_down: float32 [1024], P('seq')
Inputs may be any that keep to these rules, and one draw needn't show every extreme that they name: Each group's 8 lengths sum to 4096; in every group the longest is exactly 2048. `loss_mask`: the last frame of every group is a loss frame.
All inputs are finite; a program needn't handle non-finite values. No bound on the sum of `key_mask` or of `drop_mask` on one device may be relied on, other than what follows from the above.
Results may differ from a plain program's by a relative error of at most 0.02.
Values may be sent and summed in bfloat16 or wider, within the bound.
No kernel may reach another device: no remote copies, remote signals or barrier semaphores. Data moves between devices by JAX's collectives and lax.ppermute only.
A program may use at most 320 MiB of HBM per device.

v0:
```python
import jax
import jax.numpy as jnp
from jax import lax
from jax.sharding import PartitionSpec as P

HEADS = 16


epsilon = 1e-06
masked_score = -1e30


def norm_rows(tensor):
    centred = tensor - jnp.mean(tensor, axis=-1, keepdims=True)
    spread = jnp.mean(centred * centred, axis=-1, keepdims=True)
    return centred * lax.rsqrt(spread + epsilon)


def modulate(hidden, shift_in, scale_in):
    return norm_rows(hidden) * (1.0 + scale_in) + shift_in


def gelu_tanh(tensor):
    return jax.nn.gelu(tensor, approximate=True)


def rotary_tables(position, head_size):
    halfway = head_size // 2
    inverse = 10000.0 ** (-(2.0 * jnp.arange(halfway, dtype=jnp.float32)) / head_size)
    angles = position.astype(jnp.float32)[:, None] * inverse[None, :]
    return (jnp.cos(angles)[:, None, :], jnp.sin(angles)[:, None, :])


def rotate(tensor, cosine_table, sine_table):
    halfway = tensor.shape[-1] // 2
    first_half = tensor[..., :halfway]
    second_half = tensor[..., halfway:]
    return jnp.concatenate(
        [
            first_half * cosine_table - second_half * sine_table,
            second_half * cosine_table + first_half * sine_table,
        ],
        axis=-1,
    )


def group_layout(lengths_row, frame_ids):
    ends_at = jnp.cumsum(lengths_row)
    starts_at = ends_at - lengths_row
    member = (frame_ids[:, None] >= starts_at[None, :]) & (frame_ids[:, None] < ends_at[None, :])
    utter_ids = jnp.arange(lengths_row.shape[0], dtype=jnp.int32)
    segment = jnp.sum(jnp.where(member, utter_ids[None, :], 0), axis=1)
    position = frame_ids - jnp.sum(jnp.where(member, starts_at[None, :], 0), axis=1)
    return (member, segment, position)


def block_mask(segment_all, key_ok, row_start, block_rows):
    key_ids = jnp.arange(segment_all.shape[0], dtype=jnp.int32)
    row_ids = row_start + jnp.arange(block_rows, dtype=jnp.int32)
    row_segment = lax.dynamic_slice_in_dim(segment_all, row_start, block_rows)
    return (row_segment[:, None] == segment_all[None, :]) & (
        (key_ok[None, :] > 0) | (row_ids[:, None] == key_ids[None, :])
    )


def transpose_dot(left_op, right_op):
    return lax.dot_general(
        left_op, right_op, (((0,), (0,)), ((), ())), preferred_element_type=jnp.float32
    )


def back_dot(left_op, right_op):
    return lax.dot_general(
        left_op, right_op, (((1,), (1,)), ((), ())), preferred_element_type=jnp.float32
    )


def precise_dot(left_op, right_op):
    return jnp.dot(left_op, right_op, precision=lax.Precision.HIGHEST)


def shards(
    tokens_in,
    skip_in,
    condition,
    cotangent,
    time_embed,
    lengths,
    key_mask,
    drop_mask,
    loss_mask,
    w_skip,
    b_skip,
    w_ada,
    b_ada,
    w_qkv,
    b_qkv,
    w_out,
    b_out,
    w_up,
    b_up,
    w_down,
    b_down,
):
    seq_ways = lax.axis_size("seq")
    seq_rank = lax.axis_index("seq")
    frames = tokens_in.shape[1]
    model_width = tokens_in.shape[2]
    group_frames = frames * seq_ways
    local_heads = HEADS // seq_ways
    head_size = model_width // HEADS
    lengths_row = lengths[0]
    key_ok = key_mask[0]
    local_ids = seq_rank * frames + jnp.arange(frames, dtype=jnp.int32)
    member, segment_local, position = group_layout(lengths_row, local_ids)
    onehot = member.astype(jnp.float32)
    segment_all = group_layout(lengths_row, jnp.arange(group_frames, dtype=jnp.int32))[1]
    keep_frame = precise_dot(onehot, (1 - drop_mask[0]).astype(jnp.float32))
    mixed_in = tokens_in[0].astype(jnp.float32) + keep_frame[:, None] * condition[0].astype(
        jnp.float32
    )
    joined = jnp.concatenate([mixed_in.astype(jnp.bfloat16), skip_in[0]], axis=1)
    hidden = jnp.dot(joined, w_skip, preferred_element_type=jnp.float32) + b_skip.astype(
        jnp.float32
    )
    time_act = jax.nn.silu(time_embed[0]).astype(jnp.bfloat16)
    modulation = jnp.dot(time_act, w_ada, preferred_element_type=jnp.float32) + b_ada.astype(
        jnp.float32
    )
    frame_mods = precise_dot(onehot, modulation)
    shift_a, scale_a, gate_a, shift_f, scale_f, gate_f = jnp.split(frame_mods, 6, axis=1)
    normed_a, pull_norm_a = jax.vjp(modulate, hidden, shift_a, scale_a)
    normed_a = normed_a.astype(jnp.bfloat16)
    projected = jnp.dot(normed_a, w_qkv, preferred_element_type=jnp.float32) + b_qkv.astype(
        jnp.float32
    )
    query_raw, key_raw, value_raw = jnp.split(projected, 3, axis=1)
    cosine_table, sine_table = rotary_tables(position, head_size)

    def rotate_pair(query_in, key_in):
        query_out = rotate(
            query_in.reshape(frames, HEADS, head_size), cosine_table, sine_table
        ).reshape(frames, model_width)
        key_out = rotate(
            key_in.reshape(frames, HEADS, head_size), cosine_table, sine_table
        ).reshape(frames, model_width)
        return (query_out, key_out)

    (query_rot, key_rot), pull_rotary = jax.vjp(rotate_pair, query_raw, key_raw)
    packed = jnp.stack([query_rot, key_rot, value_raw], axis=1).astype(jnp.bfloat16)
    heads_packed = lax.all_to_all(packed, "seq", split_axis=2, concat_axis=0, tiled=True)
    queries = heads_packed[:, 0].reshape(group_frames, local_heads, head_size)
    keys_all = heads_packed[:, 1].reshape(group_frames, local_heads, head_size)
    values_all = heads_packed[:, 2].reshape(group_frames, local_heads, head_size)
    block_rows = min(512, group_frames)
    blocks = group_frames // block_rows
    block_starts = jnp.arange(blocks, dtype=jnp.int32) * block_rows
    query_blocks = queries.reshape(blocks, block_rows, local_heads, head_size)

    def block_scores(query_block, row_start):
        allowed = block_mask(segment_all, key_ok, row_start, block_rows)
        scores = (
            jnp.einsum("qhd,khd->hqk", query_block, keys_all, preferred_element_type=jnp.float32)
            * 0.125
        )
        return jnp.where(allowed[None], scores, masked_score)

    def attend_block(block_args):
        query_block, row_start = block_args
        scores = block_scores(query_block, row_start)
        row_peak = jnp.max(scores, axis=-1, keepdims=True)
        log_total = row_peak + jnp.log(jnp.sum(jnp.exp(scores - row_peak), axis=-1, keepdims=True))
        attn_probs = jnp.exp(scores - log_total).astype(jnp.bfloat16)
        mixed_block = jnp.einsum(
            "hqk,khd->qhd", attn_probs, values_all, preferred_element_type=jnp.float32
        )
        return (
            mixed_block.astype(jnp.bfloat16).reshape(block_rows, local_heads * head_size),
            log_total,
        )

    head_out, log_totals = lax.map(attend_block, (query_blocks, block_starts))
    head_out = head_out.reshape(group_frames, local_heads * head_size)
    attended = lax.all_to_all(head_out, "seq", split_axis=0, concat_axis=1, tiled=True)
    attn_proj = jnp.dot(attended, w_out, preferred_element_type=jnp.float32) + b_out.astype(
        jnp.float32
    )
    after_attn = hidden + gate_a * attn_proj
    normed_f, pull_norm_f = jax.vjp(modulate, after_attn, shift_f, scale_f)
    normed_f = normed_f.astype(jnp.bfloat16)
    up_proj = jnp.dot(normed_f, w_up, preferred_element_type=jnp.float32) + b_up.astype(jnp.float32)
    activated, pull_gelu = jax.vjp(gelu_tanh, up_proj)
    activated = activated.astype(jnp.bfloat16)
    ff_out = jnp.dot(activated, w_down, preferred_element_type=jnp.float32) + b_down.astype(
        jnp.float32
    )
    output = after_attn + gate_f * ff_out
    frame_count = lax.psum(jnp.sum(loss_mask[0].astype(jnp.float32)), ("batch", "seq"))
    grad_scale = group_frames * lax.axis_size("batch") / frame_count
    grad_out = (
        cotangent[0].astype(jnp.float32) * loss_mask[0].astype(jnp.float32)[:, None] * grad_scale
    )
    grad_ff = (grad_out * gate_f).astype(jnp.bfloat16)
    grad_gate_f = grad_out * ff_out
    grad_w_down = transpose_dot(activated, grad_ff)
    grad_b_down = jnp.sum(grad_ff.astype(jnp.float32), axis=0)
    grad_act = back_dot(grad_ff, w_down)
    grad_up = pull_gelu(grad_act)[0].astype(jnp.bfloat16)
    grad_w_up = transpose_dot(normed_f, grad_up)
    grad_b_up = jnp.sum(grad_up.astype(jnp.float32), axis=0)
    grad_normed_f = back_dot(grad_up, w_up)
    grad_after_norm, grad_shift_f, grad_scale_f = pull_norm_f(grad_normed_f)
    grad_after = grad_out + grad_after_norm
    grad_attn = (grad_after * gate_a).astype(jnp.bfloat16)
    grad_gate_a = grad_after * attn_proj
    grad_w_out = transpose_dot(attended, grad_attn)
    grad_b_out = jnp.sum(grad_attn.astype(jnp.float32), axis=0)
    grad_attended = back_dot(grad_attn, w_out).astype(jnp.bfloat16)
    grad_heads = lax.all_to_all(grad_attended, "seq", split_axis=1, concat_axis=0, tiled=True)
    grad_blocks = grad_heads.reshape(blocks, block_rows, local_heads, head_size)

    def back_block(running, block_args):
        grad_key_sum, grad_value_sum = running
        query_block, grad_block, log_total, row_start = block_args
        scores = block_scores(query_block, row_start)
        attn_probs = jnp.exp(scores - log_total)
        grad_probs = jnp.einsum(
            "qhd,khd->hqk", grad_block, values_all, preferred_element_type=jnp.float32
        )
        row_delta = jnp.sum(attn_probs * grad_probs, axis=-1, keepdims=True)
        grad_scores = (attn_probs * (grad_probs - row_delta)).astype(jnp.bfloat16)
        grad_query = (
            jnp.einsum("hqk,khd->qhd", grad_scores, keys_all, preferred_element_type=jnp.float32)
            * 0.125
        )
        grad_key_sum = (
            grad_key_sum
            + jnp.einsum(
                "hqk,qhd->khd", grad_scores, query_block, preferred_element_type=jnp.float32
            )
            * 0.125
        )
        grad_value_sum = grad_value_sum + jnp.einsum(
            "hqk,qhd->khd",
            attn_probs.astype(jnp.bfloat16),
            grad_block,
            preferred_element_type=jnp.float32,
        )
        return (
            (grad_key_sum, grad_value_sum),
            grad_query.astype(jnp.bfloat16).reshape(block_rows, local_heads * head_size),
        )

    zero_grads = jnp.zeros((group_frames, local_heads, head_size), jnp.float32)
    (grad_keys, grad_values), grad_queries = lax.scan(
        back_block, (zero_grads, zero_grads), (query_blocks, grad_blocks, log_totals, block_starts)
    )
    grad_packed = jnp.stack(
        [
            grad_queries.reshape(group_frames, local_heads * head_size),
            grad_keys.reshape(group_frames, local_heads * head_size).astype(jnp.bfloat16),
            grad_values.reshape(group_frames, local_heads * head_size).astype(jnp.bfloat16),
        ],
        axis=1,
    )
    grad_local = lax.all_to_all(grad_packed, "seq", split_axis=0, concat_axis=2, tiled=True)
    grad_query_raw, grad_key_raw = pull_rotary(
        (grad_local[:, 0].astype(jnp.float32), grad_local[:, 1].astype(jnp.float32))
    )
    grad_projected = jnp.concatenate(
        [grad_query_raw, grad_key_raw, grad_local[:, 2].astype(jnp.float32)], axis=1
    ).astype(jnp.bfloat16)
    grad_w_qkv = transpose_dot(normed_a, grad_projected)
    grad_b_qkv = jnp.sum(grad_projected.astype(jnp.float32), axis=0)
    grad_normed_a = back_dot(grad_projected, w_qkv)
    grad_hidden_norm, grad_shift_a, grad_scale_a = pull_norm_a(grad_normed_a)
    grad_hidden = (grad_after + grad_hidden_norm).astype(jnp.bfloat16)
    grad_w_skip = transpose_dot(joined, grad_hidden)
    grad_b_skip = jnp.sum(grad_hidden.astype(jnp.float32), axis=0)
    grad_joined = back_dot(grad_hidden, w_skip)
    grad_tokens = grad_joined[:, :model_width]
    grad_skip = grad_joined[:, model_width:]
    grad_frame_mods = jnp.concatenate(
        [grad_shift_a, grad_scale_a, grad_gate_a, grad_shift_f, grad_scale_f, grad_gate_f], axis=1
    )
    grad_modulation = lax.dot_general(
        onehot, grad_frame_mods, (((0,), (0,)), ((), ())), precision=lax.Precision.HIGHEST
    )
    grad_w_ada = lax.dot_general(
        time_act.astype(jnp.float32),
        grad_modulation,
        (((0,), (0,)), ((), ())),
        precision=lax.Precision.HIGHEST,
    )
    grad_b_ada = jnp.sum(grad_modulation, axis=0)
    grad_shards = (
        lax.psum_scatter(
            grad_w_skip.astype(jnp.bfloat16), "seq", scatter_dimension=0, tiled=True
        ).astype(jnp.float32),
        lax.psum_scatter(
            grad_b_skip.astype(jnp.bfloat16), "seq", scatter_dimension=0, tiled=True
        ).astype(jnp.float32),
        lax.psum_scatter(
            grad_w_ada.astype(jnp.bfloat16), "seq", scatter_dimension=0, tiled=True
        ).astype(jnp.float32),
        lax.psum_scatter(
            grad_b_ada.astype(jnp.bfloat16), "seq", scatter_dimension=0, tiled=True
        ).astype(jnp.float32),
        lax.psum_scatter(
            grad_w_qkv.astype(jnp.bfloat16), "seq", scatter_dimension=0, tiled=True
        ).astype(jnp.float32),
        lax.psum_scatter(
            grad_b_qkv.astype(jnp.bfloat16), "seq", scatter_dimension=0, tiled=True
        ).astype(jnp.float32),
        lax.psum_scatter(
            grad_w_out.astype(jnp.bfloat16), "seq", scatter_dimension=0, tiled=True
        ).astype(jnp.float32),
        lax.psum_scatter(
            grad_b_out.astype(jnp.bfloat16), "seq", scatter_dimension=0, tiled=True
        ).astype(jnp.float32),
        lax.psum_scatter(
            grad_w_up.astype(jnp.bfloat16), "seq", scatter_dimension=0, tiled=True
        ).astype(jnp.float32),
        lax.psum_scatter(
            grad_b_up.astype(jnp.bfloat16), "seq", scatter_dimension=0, tiled=True
        ).astype(jnp.float32),
        lax.psum_scatter(
            grad_w_down.astype(jnp.bfloat16), "seq", scatter_dimension=0, tiled=True
        ).astype(jnp.float32),
        lax.psum_scatter(
            grad_b_down.astype(jnp.bfloat16), "seq", scatter_dimension=0, tiled=True
        ).astype(jnp.float32),
    )
    reduced = (
        lax.psum(grad_shards[0].astype(jnp.bfloat16), "batch").astype(jnp.float32),
        lax.psum(grad_shards[1].astype(jnp.bfloat16), "batch").astype(jnp.float32),
        lax.psum(grad_shards[2].astype(jnp.bfloat16), "batch").astype(jnp.float32),
        lax.psum(grad_shards[3].astype(jnp.bfloat16), "batch").astype(jnp.float32),
        lax.psum(grad_shards[4].astype(jnp.bfloat16), "batch").astype(jnp.float32),
        lax.psum(grad_shards[5].astype(jnp.bfloat16), "batch").astype(jnp.float32),
        lax.psum(grad_shards[6].astype(jnp.bfloat16), "batch").astype(jnp.float32),
        lax.psum(grad_shards[7].astype(jnp.bfloat16), "batch").astype(jnp.float32),
        lax.psum(grad_shards[8].astype(jnp.bfloat16), "batch").astype(jnp.float32),
        lax.psum(grad_shards[9].astype(jnp.bfloat16), "batch").astype(jnp.float32),
        lax.psum(grad_shards[10].astype(jnp.bfloat16), "batch").astype(jnp.float32),
        lax.psum(grad_shards[11].astype(jnp.bfloat16), "batch").astype(jnp.float32),
    )
    return (
        output.astype(jnp.bfloat16)[None],
        grad_tokens[None],
        grad_skip[None],
        reduced[0],
        reduced[1],
        reduced[2],
        reduced[3],
        reduced[4],
        reduced[5],
        reduced[6],
        reduced[7],
        reduced[8],
        reduced[9],
        reduced[10],
        reduced[11],
    )


def solution(mesh):
    in_specs = (
        P("batch", "seq", None),
        P("batch", "seq", None),
        P("batch", "seq", None),
        P("batch", "seq", None),
        P("batch", None, None),
        P("batch", None),
        P("batch", None),
        P("batch", None),
        P("batch", "seq"),
        P(),
        P(),
        P(),
        P(),
        P(),
        P(),
        P(),
        P(),
        P(),
        P(),
        P(),
        P(),
    )
    out_specs = (
        P("batch", "seq", None),
        P("batch", "seq", None),
        P("batch", "seq", None),
        P("seq", None),
        P("seq"),
        P("seq", None),
        P("seq"),
        P("seq", None),
        P("seq"),
        P("seq", None),
        P("seq"),
        P("seq", None),
        P("seq"),
        P("seq", None),
        P("seq"),
    )
    return jax.shard_map(shards, mesh=mesh, in_specs=in_specs, out_specs=out_specs, check_vma=False)
```

profile of v0, /device:TPU:0, one launch (start us, length us, event | category | flops | bytes accessed | tf_op | source)
XLA Modules:
  0.0 1702.7 jit_solution(16372457305609374927)
XLA Ops:
  68.5 94.0 %all-to-all-done = bf16[512,3,1024]{0,1,2:T(4,128)(2,1)} async-done(((bf16[512,3,1024]{0,1,2:T(4,128)(2,1)}), bf16[512,3,1024]{0,1,2:T(4,128)(2,1)}, u32[]{:S(2)}, u32[]{:S(2)}) %all-to-all-start) | async-done | bytes 3145760 | tf_op jit(solution)/shard_map/all_to_all | solution.py:151
  188.8 178.2 %while.27 = (s32[]{:T(128)}, bf16[8,512,128]{1,2,0:T(8,128)(2,1)}, f32[8,2,512,1]{2,1,3,0:T(2,128)S(1)}, s32[8]{0:T(128)S(1)}, s32[4096]{0:T(1024)S(1)}, /*index...) while((s32[]{:T(128)}, bf16[8,512,128]{1,2,0:T(8,128)(2,1)}, ...), condition=%wide.region_8.9_spmd, body=%wide.region_5.8_spmd.sunk | while | flops 1128336896 | bytes 61425856 | solution.py:182
  371.9 46.2 %psum.91 = f32[]{:T(128)} all-reduce(f32[]{:T(128)} %convert_reduce_fusion), channel_id=1, replica_groups=mesh['batch'=4,'seq'=8] {'batch','seq'}, use_global_device_ids=true, to_apply=%region_12.13 | all-reduce | flops 1 | bytes 8 | tf_op jit(solution)/shard_map/psum | solution.py:198
  453.4 16.7 fusion.88
  492.2 26.6 %all-to-all-done.2 = bf16[512,8,128]{2,0,1:T(8,128)(2,1)S(1)} async-done(((bf16[512,8,128]{2,0,1:T(8,128)(2,1)}), bf16[512,8,128]{2,0,1:T(8,128)(2,1)S(1)}, u32[]{:S(2)}, u32[]{:S(2)}) %all-to-all-start.2) | async-done | bytes 1048608 | tf_op jit(solution)/shard_map/all_to_all | solution.py:219
  520.1 430.2 %while.28 = (s32[]{:T(128)}, f32[4096,2,64]{0,2,1:T(8,128)}, f32[4096,2,64]{0,2,1:T(8,128)}, bf16[8,512,128]{2,1,0:T(8,128)(2,1)}, bf16[8,512,2,64]{1,3,2,0:T(8,...) while((s32[]{:T(128)}, f32[4096,2,64]{0,2,1:T(8,128)}, ...), condition=%wide.region_17.18_spmd.clone, body=%wide.region_15.17_spmd.clone.sunk | while | flops 2758413824 | bytes 251869584 | solution.py:255
  541.6 13.3 multiply_reduce_fusion.6
  595.4 13.3 multiply_reduce_fusion.6
  649.1 13.3 multiply_reduce_fusion.6
  702.8 13.3 multiply_reduce_fusion.6
  756.5 13.3 multiply_reduce_fusion.6
  810.2 13.3 multiply_reduce_fusion.6
  863.9 13.3 multiply_reduce_fusion.6
  917.6 13.3 multiply_reduce_fusion.6
  957.2 20.5 %copy.123 = bf16[4096,3,128]{2,1,0:T(4,128)(2,1)} copy(bf16[4096,3,128]{2,0,1:T(8,128)(2,1)S(1)} %pad_maximum_fusion.1) | data formatting | bytes 6291456 | tf_op jit(solution)/shard_map/stack | solution.py:258
  986.4 109.7 %all-to-all-done.3 = bf16[4096,3,128]{2,1,0:T(4,128)(2,1)} async-done(((bf16[4096,3,128]{2,1,0:T(4,128)(2,1)}), bf16[4096,3,128]{2,1,0:T(4,128)(2,1)}, u32[]{:S(2)}, u32[]{:S(2)}) %all-to-all-start.3) | async-done | bytes 3145760 | tf_op jit(solution)/shard_map/all_to_all | solution.py:266
  1129.5 13.0 convolution_convert_fusion.1
  1181.0 12.5 convolution_convert_fusion
  1193.7 73.8 %reduce-scatter.17.cloned.1.call-done = bf16[512,1024]{1,0:T(8,128)(2,1)} async-done(((bf16[4096,1024]{1,0:T(8,128)(2,1)}), bf16[512,1024]{1,0:T(8,128)(2,1)}) %reduce-scatter.17.cloned.1.call-update) | async-done | bytes 1048592 | tf_op jit(solution)/shard_map/reduce_scatter | solution.py:327
  1267.4 90.1 %reduce-scatter.15.cloned.1.call-done = bf16[128,4096]{1,0:T(8,128)(2,1)} async-done(((bf16[1024,4096]{1,0:T(8,128)(2,1)}), bf16[128,4096]{1,0:T(8,128)(2,1)}) %reduce-scatter.15.cloned.1.call-update) | async-done | bytes 1048592 | tf_op jit(solution)/shard_map/reduce_scatter | solution.py:321
  1357.6 70.3 %reduce-scatter.11.cloned.1.call-done = bf16[128,3072]{1,0:T(8,128)(2,1)} async-done(((bf16[1024,3072]{1,0:T(8,128)(2,1)}), bf16[128,3072]{1,0:T(8,128)(2,1)}) %reduce-scatter.11.cloned.1.call-update) | async-done | bytes 786448 | tf_op jit(solution)/shard_map/reduce_scatter | solution.py:309
  1427.9 129.8 %reduce-scatter.9.cloned.1.call-done = bf16[128,6144]{1,0:T(8,128)(2,1)} async-done(((bf16[1024,6144]{1,0:T(8,128)(2,1)}), bf16[128,6144]{1,0:T(8,128)(2,1)}) %reduce-scatter.9.cloned.1.call-update) | async-done | bytes 1572880 | tf_op jit(solution)/shard_map/reduce_scatter | solution.py:303
  1562.0 26.1 %all-reduce.10 = (bf16[1024]{0:T(1024)(128)(2,1)S(1)}, bf16[6144]{0:T(1024)(128)(2,1)S(1)}, bf16[3072]{0:T(1024)(128)(2,1)S(1)}, bf16[1024]{0:T(1024)(128)(2,1)S...) all-reduce(bf16[1024]{0:T(1024)(128)(2,1)S(1)} %get-tuple-element.3, ...), channel_id=3, replica_groups=mesh['batch'=4,'seq'=8] {'seq'}, use_global_device_ids=true, to_apply=%region_23.24.clone | all-reduce | flops 16384 | bytes 65536
  1609.8 74.2 %all-reduce.15.cloned.1.call-done = (bf16[256,1024]{1,0:T(8,128)(2,1)}, bf16[128,6144]{1,0:T(8,128)(2,1)}, bf16[128,3072]{1,0:T(8,128)(2,1)}, bf16[128,1024]{1,0...) async-done(((bf16[256,1024]{1,0:T(8,128)(2,1)}, bf16[128,6144]{1,0:T(8,128)(2,1)}, bf16[128,3072]{1,0:T(8,128)(2,1)}, bf16[128,1024]{1,0:T(8,128)(2,1)}, ...) | async-done | bytes 5242896 | tf_op jit(solution)/shard_map/psum | solution.py:335
  (598 shorter events, 742.9 us)
Async XLA Ops:
  7.2 415.6 %copy-start = (bf16[1024,1024]{1,0:T(8,128)(2,1)S(1)}, bf16[1024,1024]{1,0:T(8,128)(2,1)}, u32[]{:S(2)}) copy-start(bf16[1024,1024]{1,0:T(8,128)(2,1)} %param.40) | copy-start | bytes 6291460
  8.2 60.2 %copy-start.75 = (s32[8,1]{0,1:T(1,128)}, s32[8,1]{0,1:T(1,128)S(1)}, u32[]{:S(2)}) copy-start(s32[8,1]{0,1:T(1,128)S(1)} %reduce-window.4) | copy-start | bytes 100
  10.6 412.3 %copy-start.51 = (f32[1024]{0:T(1024)}, f32[1024]{0:T(1024)S(1)}, u32[]{:S(2)}) copy-start(f32[1024]{0:T(1024)S(1)} %convert_element_type.260) | copy-start | bytes 12292
  62.0 100.4 %all-to-all-start = ((bf16[512,3,1024]{0,1,2:T(4,128)(2,1)}), bf16[512,3,1024]{0,1,2:T(4,128)(2,1)}, u32[]{:S(2)}, u32[]{:S(2)}) async-start(bf16[512,3,1024]{0,1,2:T(4,128)(2,1)} %copy.110), calls=%async_computation | async-start | bytes 8388608 | tf_op jit(solution)/shard_map/all_to_all | solution.py:151
  188.8 182.5 %copy-start.82 = (s32[1,512]{1,0:T(1,128)S(1)}, s32[1,512]{1,0:T(1,128)}, u32[]{:S(2)}) copy-start(s32[1,512]{1,0:T(1,128)} %param.33) | copy-start | bytes 6148
  188.8 229.4 %copy-start.84 = (bf16[1024]{0:T(1024)(128)(2,1)S(1)}, bf16[1024]{0:T(1024)(128)(2,1)}, u32[]{:S(2)}) copy-start(bf16[1024]{0:T(1024)(128)(2,1)} %param.41) | copy-start | bytes 6148
  188.8 229.4 %copy-start.85 = (bf16[1024]{0:T(1024)(128)(2,1)S(1)}, bf16[1024]{0:T(1024)(128)(2,1)}, u32[]{:S(2)}) copy-start(bf16[1024]{0:T(1024)(128)(2,1)} %param.45) | copy-start | bytes 6148
  188.8 229.4 %copy-start.81 = (bf16[4096]{0:T(1024)(128)(2,1)S(1)}, bf16[4096]{0:T(1024)(128)(2,1)}, u32[]{:S(2)}) copy-start(bf16[4096]{0:T(1024)(128)(2,1)} %param.43) | copy-start | bytes 24580
  367.1 55.8 %all-to-all-start.1 = ((bf16[8,512,128]{1,2,0:T(8,128)(2,1)}), bf16[8,512,128]{1,2,0:T(8,128)(2,1)}, u32[]{:S(2)}, u32[]{:S(2)}) async-start(bf16[8,512,128]{1,2,0:T(8,128)(2,1)} %get-tuple-element.127), calls=%async_computation.1 | async-start | bytes 2097152 | tf_op jit(solution)/shard_map/all_to_all | solution.py:184
  418.2 66.6 %copy-start.55 = (f32[1,512]{1,0:T(1,128)}, f32[1,512]{1,0:T(1,128)S(1)}, u32[]{:S(2)}) copy-start(f32[1,512]{1,0:T(1,128)S(1)} %convert_element_type.274) | copy-start | bytes 6148
  418.2 62.7 %copy-start.61 = (f32[1024]{0:T(1024)}, f32[1024]{0:T(1024)S(1)}, u32[]{:S(2)}) copy-start(f32[1024]{0:T(1024)S(1)} %convert_element_type.270) | copy-start | bytes 12292
  488.6 30.2 %all-to-all-start.2 = ((bf16[512,8,128]{2,0,1:T(8,128)(2,1)}), bf16[512,8,128]{2,0,1:T(8,128)(2,1)S(1)}, u32[]{:S(2)}, u32[]{:S(2)}) async-start(bf16[512,8,128]{2,0,1:T(8,128)(2,1)} %bitcast.170), calls=%async_computation.2 | async-start | bytes 2097152 | tf_op jit(solution)/shard_map/all_to_all | solution.py:219
  977.7 118.4 %all-to-all-start.3 = ((bf16[4096,3,128]{2,1,0:T(4,128)(2,1)}), bf16[4096,3,128]{2,1,0:T(4,128)(2,1)}, u32[]{:S(2)}, u32[]{:S(2)}) async-start(bf16[4096,3,128]{2,1,0:T(4,128)(2,1)} %copy.123), calls=%async_computation.3 | async-start | bytes 8388608 | tf_op jit(solution)/shard_map/all_to_all | solution.py:266
  982.4 211.2 %reduce-scatter.13.cloned.1.call-start = ((), (), s32[]{:S(2)}) async-start(), calls=%async_computation.13 | async-start | bytes 2359296 | tf_op jit(solution)/shard_map/reduce_scatter | solution.py:315
  986.3 207.3 %reduce-scatter.7.cloned.1.call-start = ((), (), s32[]{:S(2)}) async-start(), calls=%async_computation.10 | async-start | bytes 4718592 | tf_op jit(solution)/shard_map/reduce_scatter | solution.py:297
  1128.3 139.2 %reduce-scatter.17.cloned.1.call-start = ((), (), s32[]{:S(2)}) async-start(), calls=%async_computation.15 | async-start | bytes 9437184 | tf_op jit(solution)/shard_map/reduce_scatter | solution.py:327
  1142.5 215.1 %reduce-scatter.15.cloned.1.call-start = ((), (), s32[]{:S(2)}) async-start(), calls=%async_computation.14 | async-start | bytes 9437184 | tf_op jit(solution)/shard_map/reduce_scatter | solution.py:321
  1152.8 275.1 %reduce-scatter.11.cloned.1.call-start = ((), (), s32[]{:S(2)}) async-start(), calls=%async_computation.12 | async-start | bytes 7077888 | tf_op jit(solution)/shard_map/reduce_scatter | solution.py:309
  1162.1 395.6 %reduce-scatter.9.cloned.1.call-start = ((), (), s32[]{:S(2)}) async-start(), calls=%async_computation.11 | async-start | bytes 14155776 | tf_op jit(solution)/shard_map/reduce_scatter | solution.py:303
  1193.5 364.2 %copy-start.88 = (u32[32]{0:T(128)S(1)}, u32[32]{0:T(128)}, u32[]{:S(2)}) copy-start(u32[32]{0:T(128)} %constant.128) | copy-start | bytes 388
  1193.5 367.4 %copy-start.22 = (bf16[512,16,64]{0,2,1:T(8,128)(2,1)S(1)}, bf16[512,16,64]{0,2,1:T(8,128)(2,1)}, u32[]{:S(2)}) copy-start(bf16[512,16,64]{0,2,1:T(8,128)(2,1)} %copy-done.20) | copy-start | bytes 3145732
  1193.5 367.4 %copy-start.25 = (bf16[512,16,64]{0,2,1:T(8,128)(2,1)S(1)}, bf16[512,16,64]{0,2,1:T(8,128)(2,1)}, u32[]{:S(2)}) copy-start(bf16[512,16,64]{0,2,1:T(8,128)(2,1)} %copy-done.23) | copy-start | bytes 3145732
  1193.5 367.4 %copy-start.27 = (bf16[512,1024]{0,1:T(8,128)(2,1)S(1)}, bf16[512,1024]{0,1:T(8,128)(2,1)}, u32[]{:S(2)}) copy-start(bf16[512,1024]{0,1:T(8,128)(2,1)} %copy-done.26) | copy-start | bytes 3145732
  1193.6 490.4 %all-reduce.15.cloned.1.call-start = ((), (), s32[]{:S(2)}) async-start(), calls=%async_computation.16 | async-start | bytes 10485760 | tf_op jit(solution)/shard_map/psum | solution.py:335
  (125 other events, 946.6 us)
Sparse Core Ops, SparseCore 0:
  986.4 69.7 reduce-scatter.12
  1128.4 48.8 reduce-scatter.6
  1179.6 87.7 reduce-scatter.16
  1269.6 87.9 reduce-scatter.14
  1359.7 68.1 reduce-scatter.10
  1430.0 127.5 reduce-scatter.8
  1562.1 121.8 all-reduce.14
where the time goes:
time: 1710 us; the launch traced here: 1700 us
  waiting for transfers between devices  669 us (39%)
  matrix products  456 us (27%)
  other arithmetic  252 us (15%)
  local copies, waits for them, and re-layouts  175 us (10%)
  blocking collectives  82.5 us (5%)
  loops' own time  30.8 us (2%)
  starting transfers between devices  19.5 us (1%)
  between operations  18.7 us (1%)
    reduce_scatter x1, waiting for transfers between devices, shards(): lax.psum_scatter(grad_w_ada.astype(jnp.bfloat16), 'seq', scatter_dimensio...  130 us
    all_to_all x1, waiting for transfers between devices, shards(): lax.all_to_all(grad_packed, 'seq', split_axis=0, concat_axis=2, tiled=True)  110 us
    dot_general x8, matrix products, back_block(): jnp.einsum('qhd,khd->hqk', grad_block, values_all, preferred_element_type...  107 us
    convert_element_type x8, other arithmetic, back_block(): grad_scores = (attn_probs * (grad_probs - row_delta)).astype(jnp.bfloat16)  97.9 us
    all_to_all x1, waiting for transfers between devices, shards(): lax.all_to_all(packed, 'seq', split_axis=2, concat_axis=0, tiled=True)  94 us
    reduce_scatter x1, waiting for transfers between devices, shards(): lax.psum_scatter(grad_w_up.astype(jnp.bfloat16), 'seq', scatter_dimension...  90.1 us
    psum x1, waiting for transfers between devices, shards(): lax.psum(grad_shards[0].astype(jnp.bfloat16), 'batch').astype(jnp.float32)  74.2 us
    reduce_scatter x1, waiting for transfers between devices, shards(): lax.psum_scatter(grad_w_down.astype(jnp.bfloat16), 'seq', scatter_dimensi...  73.8 us
  transfers between devices with their start and end apart: 11, of which 8 were waited for; matrix products, arithmetic and copies ran while one was open for 6% of the time, Pallas kernels for 0%

commit v1 on v0

v1 whole, which is shorter than its diff:
```python
import functools

import jax
import jax.numpy as jnp
from jax import lax
from jax.experimental import pallas as pl
from jax.experimental.pallas import tpu as pltpu
from jax.sharding import PartitionSpec as P

HEADS = 16


epsilon = 1e-06


def norm_rows(tensor):
    centred = tensor - jnp.mean(tensor, axis=-1, keepdims=True)
    spread = jnp.mean(centred * centred, axis=-1, keepdims=True)
    return centred * lax.rsqrt(spread + epsilon)


def modulate(hidden, shift_in, scale_in):
    return norm_rows(hidden) * (1.0 + scale_in) + shift_in


def gelu_tanh(tensor):
    return jax.nn.gelu(tensor, approximate=True)


def group_layout(lengths_row, frame_ids):
    ends_at = jnp.cumsum(lengths_row)
    starts_at = ends_at - lengths_row
    member = (frame_ids[:, None] >= starts_at[None, :]) & (frame_ids[:, None] < ends_at[None, :])
    utter_ids = jnp.arange(lengths_row.shape[0], dtype=jnp.int32)
    segment = jnp.sum(jnp.where(member, utter_ids[None, :], 0), axis=1)
    position = frame_ids - jnp.sum(jnp.where(member, starts_at[None, :], 0), axis=1)
    return (member, segment, position)


def transpose_dot(left_op, right_op):
    return lax.dot_general(
        left_op, right_op, (((0,), (0,)), ((), ())), preferred_element_type=jnp.float32
    )


def back_dot(left_op, right_op):
    return lax.dot_general(
        left_op, right_op, (((1,), (1,)), ((), ())), preferred_element_type=jnp.float32
    )


def precise_dot(left_op, right_op):
    return jnp.dot(left_op, right_op, precision=lax.Precision.HIGHEST)

BIG = 1e30
DH = 64
BQ = 512
BK = 512


def onehot_rows(lengths_ref, utts, rows, base, width):
    row = lax.broadcasted_iota(jnp.int32, (rows, width), 0)
    col = base + lax.broadcasted_iota(jnp.int32, (rows, width), 1)
    start = jnp.int32(0)
    hot = jnp.zeros((rows, width), jnp.float32)
    for u in range(utts):
        end = start + lengths_ref[u]
        hot = jnp.where((row == u) & (col >= start) & (col < end), 1.0, hot)
        start = end
    return hot


def key_range(lengths_ref, utts, first, last):
    start = jnp.int32(0)
    low, high = jnp.int32(0), jnp.int32(0)
    for u in range(utts):
        end = start + lengths_ref[u]
        low = jnp.where((start <= first) & (first < end), start, low)
        high = jnp.where((start <= last) & (last < end), end, high)
        start = end
    return low // BK, (high + BK - 1) // BK


def aug_rows(utts):
    return -(-utts // 16) * 16


def split3(row):
    a = row.astype(jnp.bfloat16)
    rest = row - a.astype(jnp.float32)
    b = rest.astype(jnp.bfloat16)
    c = (rest - b.astype(jnp.float32)).astype(jnp.bfloat16)
    return a, b, c


def pad_rows(parts, total):
    have = sum(p.shape[0] for p in parts)
    if have < total:
        parts = parts + [jnp.zeros((total - have, parts[0].shape[1]), parts[0].dtype)]
    return jnp.concatenate(parts, axis=0)


def rows16(rows, width):
    idx = lax.broadcasted_iota(jnp.int32, (16, width), 0)
    out = jnp.zeros((16, width), jnp.float32)
    for i, r in enumerate(rows):
        out = jnp.where(idx == i, r, out)
    return out.astype(jnp.bfloat16)


def fwd_kernel(utts, lengths_ref, qkv_ref, ok_ref, out_ref, lse_ref, kaug, vaug):
    sources, _, frames = qkv_ref.shape
    per = frames // BQ
    pad_u = aug_rows(utts)
    step = pl.program_id(0)

    @pl.when(step == 0)
    def _():
        def build(s, c):
            hot = onehot_rows(lengths_ref, utts, pad_u, s * frames, frames)
            ok = ok_ref[s].astype(jnp.float32)
            block = qkv_ref[s]
            one = jnp.ones((1, frames), jnp.float32)
            kT = pad_rows(
                [block[DH : 2 * DH], (1.0 - hot).astype(jnp.bfloat16), rows16([1.0 - ok], frames)], 128
            )
            kaug[pl.ds(pl.multiple_of(s * frames, frames), frames), :] = kT.T
            vT = jnp.concatenate([block[2 * DH :], rows16([one], frames)], axis=0)
            for t in range(frames // BK):
                vaug[s * (frames // BK) + t] = vT[:, t * BK : (t + 1) * BK]
            return c

        lax.fori_loop(0, sources, build, 0)

    block = qkv_ref[step]
    hot_q = onehot_rows(lengths_ref, utts, pad_u, step * frames, frames)
    qT = (block[:DH].astype(jnp.float32) * 0.125)
    one = jnp.ones((1, frames), jnp.float32)
    qaug = pad_rows(
        [qT.astype(jnp.bfloat16), (hot_q * -BIG).astype(jnp.bfloat16), rows16([one * -BIG], frames)], 128
    )
    kT = block[DH : 2 * DH].astype(jnp.float32)
    vT = block[2 * DH :].astype(jnp.float32)
    ok = ok_ref[step] > 0
    s_self = jnp.sum(qT * kT, axis=0, keepdims=True)
    m0 = jnp.where(ok, -3e38, s_self)
    acc0 = jnp.concatenate([jnp.where(ok, 0.0, vT), jnp.where(ok, 0.0, jnp.ones((16, frames), jnp.float32))], axis=0)
    for t in range(per):
        cols = slice(t * BQ, (t + 1) * BQ)
        low, high = key_range(lengths_ref, utts, step * frames + t * BQ, step * frames + (t + 1) * BQ - 1)
        q_b = qaug[:, cols]

        def body(j, carry):
            m, acc = carry
            s = jnp.dot(kaug[pl.ds(pl.multiple_of(j * BK, BK), BK), :], q_b, preferred_element_type=jnp.float32)
            m_new = jnp.maximum(m, jnp.max(s, axis=0, keepdims=True))
            p = jnp.exp(s - m_new).astype(jnp.bfloat16)
            alpha = jnp.exp(m - m_new)
            acc = acc * alpha + jnp.dot(vaug[j], p, preferred_element_type=jnp.float32)
            return m_new, acc

        m, acc = lax.fori_loop(low, high, body, (m0[:, cols], acc0[:, cols]))
        total = acc[DH : DH + 1]
        out_ref[0, :, cols] = (acc[:DH] / total).astype(jnp.bfloat16)
        lse_ref[0, :, cols] = m + jnp.log(total)


def attend(lengths, qkv, ok):
    sources, _, frames = qkv.shape
    total = sources * frames
    utts = lengths.shape[0]
    whole = lambda shape: pl.BlockSpec(shape, lambda i, *_: (0,) * len(shape))
    return pl.pallas_call(
        functools.partial(fwd_kernel, utts),
        out_shape=(
            jax.ShapeDtypeStruct((sources, DH, frames), jnp.bfloat16),
            jax.ShapeDtypeStruct((sources, 1, frames), jnp.float32),
        ),
        grid_spec=pltpu.PrefetchScalarGridSpec(
            num_scalar_prefetch=1,
            grid=(sources,),
            in_specs=[whole(qkv.shape), whole(ok.shape)],
            out_specs=(
                pl.BlockSpec((1, DH, frames), lambda i, *_: (i, 0, 0)),
                pl.BlockSpec((1, 1, frames), lambda i, *_: (i, 0, 0)),
            ),
            scratch_shapes=[
                pltpu.VMEM((total, 128), jnp.bfloat16),
                pltpu.VMEM((total // BK, DH + 16, BK), jnp.bfloat16),
            ],
        ),
        name="attend",
    )(lengths, qkv, ok)


def bwd_kernel(utts, lengths_ref, qkv_ref, ok_ref, o_ref, do_ref, lse_ref, out_ref, kaug, vnat, kT_s, dk, dv):
    sources, _, frames = qkv_ref.shape
    per = frames // BK
    pad_u = aug_rows(utts)
    step = pl.program_id(0)
    f32 = jnp.float32

    @pl.when(step == 0)
    def _():
        def build(s, c):
            hot = onehot_rows(lengths_ref, utts, pad_u, s * frames, frames)
            ok = ok_ref[s]
            block = qkv_ref[s]
            one = jnp.ones((1, frames), f32)
            kT = block[DH : 2 * DH]
            vT = block[2 * DH :]
            kA = pad_rows(
                [kT, (1.0 - hot).astype(jnp.bfloat16), rows16([1.0 - ok.astype(f32), one, one, one], frames)], 128
            )
            rows = pl.ds(pl.multiple_of(s * frames, frames), frames)
            kaug[rows, :] = kA.T
            vnat[rows, :] = pad_rows([vT, rows16([one, one, one], frames)], 128).T
            qT = block[:DH].astype(f32) * 0.125
            do = do_ref[s].astype(f32)
            s_self = jnp.sum(qT * kT.astype(f32), axis=0, keepdims=True)
            delta = jnp.sum(do * o_ref[s].astype(f32), axis=0, keepdims=True)
            p_self = jnp.where(ok > 0, 0.0, jnp.exp(s_self - lse_ref[s]))
            ds_self = p_self * (jnp.sum(do * vT.astype(f32), axis=0, keepdims=True) - delta)
            dk0 = ds_self * qT
            dv0 = p_self * do
            for t in range(per):
                cols = slice(t * BK, (t + 1) * BK)
                kT_s[s * per + t] = kT[:, cols]
                dk[s * per + t] = dk0[:, cols]
                dv[s * per + t] = dv0[:, cols]
            return c

        lax.fori_loop(0, sources, build, 0)

    block = qkv_ref[step]
    one = jnp.ones((1, frames), f32)
    hot_q = onehot_rows(lengths_ref, utts, pad_u, step * frames, frames)
    qT = block[:DH].astype(f32) * 0.125
    qTb = qT.astype(jnp.bfloat16)
    kT = block[DH : 2 * DH].astype(f32)
    vT = block[2 * DH :].astype(f32)
    ok = ok_ref[step]
    dob = do_ref[step]
    do = dob.astype(f32)
    lse = lse_ref[step]
    delta = jnp.sum(do * o_ref[step].astype(f32), axis=0, keepdims=True)
    l3 = [-r.astype(f32) for r in split3(lse)]
    d3 = [-r.astype(f32) for r in split3(delta)]
    qaug = pad_rows([qTb, (hot_q * -BIG).astype(jnp.bfloat16), rows16([one * -BIG] + l3, frames)], 128)
    doaug = pad_rows([dob, rows16(d3, frames)], 128)
    s_self = jnp.sum(qT * kT, axis=0, keepdims=True)
    p_self = jnp.where(ok > 0, 0.0, jnp.exp(s_self - lse))
    ds_self = p_self * (jnp.sum(do * vT, axis=0, keepdims=True) - delta)
    dq0 = ds_self * kT
    nt = (((1,), (1,)), ((), ()))
    for t in range(frames // BQ):
        cols = slice(t * BQ, (t + 1) * BQ)
        low, high = key_range(lengths_ref, utts, step * frames + t * BQ, step * frames + (t + 1) * BQ - 1)
        q_a = qaug[:, cols]
        q_b = qTb[:, cols]
        do_a = doaug[:, cols]
        do_b = dob[:, cols]

        def body(j, dq):
            rows = pl.ds(pl.multiple_of(j * BK, BK), BK)
            s = jnp.dot(kaug[rows, :], q_a, preferred_element_type=f32)
            dp = jnp.dot(vnat[rows, :], do_a, preferred_element_type=f32)
            p = jnp.exp(s)
            ds = (p * dp).astype(jnp.bfloat16)
            dv[j] += lax.dot_general(do_b, p.astype(jnp.bfloat16), nt, preferred_element_type=f32)
            dk[j] += lax.dot_general(q_b, ds, nt, preferred_element_type=f32)
            return dq + jnp.dot(kT_s[j], ds, preferred_element_type=f32)

        dq = lax.fori_loop(low, high, body, dq0[:, cols])
        out_ref[step, :DH, cols] = (dq * 0.125).astype(jnp.bfloat16)

    @pl.when(step == sources - 1)
    def _():
        def finish(s, c):
            for t in range(per):
                cols = slice(t * BK, (t + 1) * BK)
                out_ref[s, DH : 2 * DH, cols] = dk[s * per + t].astype(jnp.bfloat16)
                out_ref[s, 2 * DH :, cols] = dv[s * per + t].astype(jnp.bfloat16)
            return c

        lax.fori_loop(0, sources, finish, 0)


def attend_back(lengths, qkv, ok, out, grad, lse):
    sources, _, frames = qkv.shape
    total = sources * frames
    utts = lengths.shape[0]
    whole = lambda shape: pl.BlockSpec(shape, lambda i, *_: (0,) * len(shape))
    return pl.pallas_call(
        functools.partial(bwd_kernel, utts),
        out_shape=jax.ShapeDtypeStruct(qkv.shape, jnp.bfloat16),
        grid_spec=pltpu.PrefetchScalarGridSpec(
            num_scalar_prefetch=1,
            grid=(sources,),
            in_specs=[whole(a.shape) for a in (qkv, ok, out, grad, lse)],
            out_specs=whole(qkv.shape),
            scratch_shapes=[
                pltpu.VMEM((total, 128), jnp.bfloat16),
                pltpu.VMEM((total, 128), jnp.bfloat16),
                pltpu.VMEM((total // BK, DH, BK), jnp.bfloat16),
                pltpu.VMEM((total // BK, DH, BK), jnp.float32),
                pltpu.VMEM((total // BK, DH, BK), jnp.float32),
            ],
        ),
        name="attend_back",
    )(lengths, qkv, ok, out, grad, lse)


def shards(
    tokens_in,
    skip_in,
    condition,
    cotangent,
    time_embed,
    lengths,
    key_mask,
    drop_mask,
    loss_mask,
    w_skip,
    b_skip,
    w_ada,
    b_ada,
    w_qkv,
    b_qkv,
    w_out,
    b_out,
    w_up,
    b_up,
    w_down,
    b_down,
):
    seq_ways = lax.axis_size("seq")
    seq_rank = lax.axis_index("seq")
    frames = tokens_in.shape[1]
    model_width = tokens_in.shape[2]
    group_frames = frames * seq_ways
    local_heads = HEADS // seq_ways
    head_size = model_width // HEADS
    lengths_row = lengths[0]
    key_ok = key_mask[0]
    local_ids = seq_rank * frames + jnp.arange(frames, dtype=jnp.int32)
    member, segment_local, position = group_layout(lengths_row, local_ids)
    onehot = member.astype(jnp.float32)
    keep_frame = precise_dot(onehot, (1 - drop_mask[0]).astype(jnp.float32))
    mixed_in = tokens_in[0].astype(jnp.float32) + keep_frame[:, None] * condition[0].astype(
        jnp.float32
    )
    joined = jnp.concatenate([mixed_in.astype(jnp.bfloat16), skip_in[0]], axis=1)
    hidden = jnp.dot(joined, w_skip, preferred_element_type=jnp.float32) + b_skip.astype(
        jnp.float32
    )
    time_act = jax.nn.silu(time_embed[0]).astype(jnp.bfloat16)
    modulation = jnp.dot(time_act, w_ada, preferred_element_type=jnp.float32) + b_ada.astype(
        jnp.float32
    )
    frame_mods = precise_dot(onehot, modulation)
    shift_a, scale_a, gate_a, shift_f, scale_f, gate_f = jnp.split(frame_mods, 6, axis=1)
    normed_a, pull_norm_a = jax.vjp(modulate, hidden, shift_a, scale_a)
    normed_a = normed_a.astype(jnp.bfloat16)
    half = head_size // 2
    projected = lax.dot_general(
        w_qkv, normed_a, (((0,), (1,)), ((), ())), preferred_element_type=jnp.float32
    ) + b_qkv.astype(jnp.float32)[:, None]
    projected = projected.reshape(3, HEADS, head_size, frames)
    inverse = 10000.0 ** (-(2.0 * jnp.arange(half, dtype=jnp.float32)) / head_size)
    angles = inverse[:, None] * position.astype(jnp.float32)[None, :]
    cosine, sine = jnp.cos(angles)[None], jnp.sin(angles)[None]

    def turn(tensor, sign):
        first, second = tensor[:, :half], tensor[:, half:]
        return jnp.concatenate(
            [first * cosine - sign * second * sine, second * cosine + sign * first * sine], axis=1
        )

    packed = jnp.concatenate(
        [turn(projected[0], 1.0), turn(projected[1], 1.0), projected[2]], axis=1
    ).astype(jnp.bfloat16)
    packed = packed.reshape(seq_ways, local_heads, 3 * head_size, frames)
    ok = key_ok.reshape(seq_ways, 1, frames)
    exchange = functools.partial(
        lax.all_to_all, axis_name="seq", split_axis=0, concat_axis=0, tiled=True
    )
    received, head_out, log_totals, returned = [], [], [], []
    for h in range(local_heads):
        received.append(exchange(packed[:, h]))
    for h in range(local_heads):
        out, log_total = attend(lengths_row, received[h], ok)
        head_out.append(out)
        log_totals.append(log_total)
        returned.append(exchange(out))
    attended = jnp.stack(returned, axis=1).reshape(model_width, frames)
    attn_proj = transpose_dot(attended, w_out) + b_out.astype(jnp.float32)
    after_attn = hidden + gate_a * attn_proj
    normed_f, pull_norm_f = jax.vjp(modulate, after_attn, shift_f, scale_f)
    normed_f = normed_f.astype(jnp.bfloat16)
    up_proj = jnp.dot(normed_f, w_up, preferred_element_type=jnp.float32) + b_up.astype(jnp.float32)
    activated, pull_gelu = jax.vjp(gelu_tanh, up_proj)
    activated = activated.astype(jnp.bfloat16)
    ff_out = jnp.dot(activated, w_down, preferred_element_type=jnp.float32) + b_down.astype(
        jnp.float32
    )
    output = after_attn + gate_f * ff_out
    frame_count = lax.psum(jnp.sum(loss_mask[0].astype(jnp.float32)), ("batch", "seq"))
    grad_scale = group_frames * lax.axis_size("batch") / frame_count
    grad_out = (
        cotangent[0].astype(jnp.float32) * loss_mask[0].astype(jnp.float32)[:, None] * grad_scale
    )
    grad_ff = (grad_out * gate_f).astype(jnp.bfloat16)
    grad_gate_f = grad_out * ff_out
    grad_w_down = transpose_dot(activated, grad_ff)
    grad_b_down = jnp.sum(grad_ff.astype(jnp.float32), axis=0)
    grad_act = back_dot(grad_ff, w_down)
    grad_up = pull_gelu(grad_act)[0].astype(jnp.bfloat16)
    grad_w_up = transpose_dot(normed_f, grad_up)
    grad_b_up = jnp.sum(grad_up.astype(jnp.float32), axis=0)
    grad_normed_f = back_dot(grad_up, w_up)
    grad_after_norm, grad_shift_f, grad_scale_f = pull_norm_f(grad_normed_f)
    grad_after = grad_out + grad_after_norm
    grad_attn = (grad_after * gate_a).astype(jnp.bfloat16)
    grad_gate_a = grad_after * attn_proj
    grad_w_out = jnp.dot(attended, grad_attn, preferred_element_type=jnp.float32)
    grad_b_out = jnp.sum(grad_attn.astype(jnp.float32), axis=0)
    grad_attended = back_dot(w_out, grad_attn).astype(jnp.bfloat16)
    grad_attended = grad_attended.reshape(seq_ways, local_heads, head_size, frames)
    grad_heads = [exchange(grad_attended[:, h]) for h in range(local_heads)]
    grad_local = []
    for h in range(local_heads):
        grad_packed = attend_back(
            lengths_row, received[h], ok, head_out[h], grad_heads[h], log_totals[h]
        )
        grad_local.append(exchange(grad_packed))
    grad_local = jnp.stack(grad_local, axis=1).reshape(HEADS, 3, head_size, frames)
    grad_local = grad_local.astype(jnp.float32)
    grad_projected = jnp.stack(
        [turn(grad_local[:, 0], -1.0), turn(grad_local[:, 1], -1.0), grad_local[:, 2]]
    )
    grad_projected = grad_projected.reshape(3 * model_width, frames).astype(jnp.bfloat16)
    grad_w_qkv = lax.dot_general(
        normed_a, grad_projected, (((0,), (1,)), ((), ())), preferred_element_type=jnp.float32
    )
    grad_b_qkv = jnp.sum(grad_projected.astype(jnp.float32), axis=1)
    grad_normed_a = lax.dot_general(
        grad_projected, w_qkv, (((0,), (1,)), ((), ())), preferred_element_type=jnp.float32
    )
    grad_hidden_norm, grad_shift_a, grad_scale_a = pull_norm_a(grad_normed_a)
    grad_hidden = (grad_after + grad_hidden_norm).astype(jnp.bfloat16)
    grad_w_skip = transpose_dot(joined, grad_hidden)
    grad_b_skip = jnp.sum(grad_hidden.astype(jnp.float32), axis=0)
    grad_joined = back_dot(grad_hidden, w_skip)
    grad_tokens = grad_joined[:, :model_width]
    grad_skip = grad_joined[:, model_width:]
    grad_frame_mods = jnp.concatenate(
        [grad_shift_a, grad_scale_a, grad_gate_a, grad_shift_f, grad_scale_f, grad_gate_f], axis=1
    )
    grad_modulation = lax.dot_general(
        onehot, grad_frame_mods, (((0,), (0,)), ((), ())), precision=lax.Precision.HIGHEST
    )
    grad_modulation = lax.psum(grad_modulation, "seq")
    all_modulation = lax.all_gather(grad_modulation, "batch", axis=0, tiled=True)
    all_time = lax.all_gather(time_act, "batch", axis=0, tiled=True)
    ada_rows = model_width // seq_ways
    own_time = lax.dynamic_slice_in_dim(all_time, seq_rank * ada_rows, ada_rows, axis=1)
    grad_w_ada = lax.dot_general(
        own_time.astype(jnp.float32),
        all_modulation,
        (((0,), (0,)), ((), ())),
        precision=lax.Precision.HIGHEST,
    )
    bias_rows = all_modulation.shape[1] // seq_ways
    grad_b_ada = jnp.sum(
        lax.dynamic_slice_in_dim(all_modulation, seq_rank * bias_rows, bias_rows, axis=1), axis=0
    )
    def reduce_grad(grad):
        shard = lax.psum_scatter(
            grad.astype(jnp.bfloat16), "seq", scatter_dimension=0, tiled=True
        )
        return lax.psum(shard, "batch").astype(jnp.float32)

    reduced = [
        reduce_grad(g)
        for g in (
            grad_w_skip,
            grad_b_skip,
            grad_w_qkv,
            grad_b_qkv,
            grad_w_out,
            grad_b_out,
            grad_w_up,
            grad_b_up,
            grad_w_down,
            grad_b_down,
        )
    ]
    reduced = reduced[:2] + [grad_w_ada, grad_b_ada] + reduced[2:]
    return (
        output.astype(jnp.bfloat16)[None],
        grad_tokens[None],
        grad_skip[None],
        reduced[0],
        reduced[1],
        reduced[2],
        reduced[3],
        reduced[4],
        reduced[5],
        reduced[6],
        reduced[7],
        reduced[8],
        reduced[9],
        reduced[10],
        reduced[11],
    )


def solution(mesh):
    in_specs = (
        P("batch", "seq", None),
        P("batch", "seq", None),
        P("batch", "seq", None),
        P("batch", "seq", None),
        P("batch", None, None),
        P("batch", None),
        P("batch", None),
        P("batch", None),
        P("batch", "seq"),
        P(),
        P(),
        P(),
        P(),
        P(),
        P(),
        P(),
        P(),
        P(),
        P(),
        P(),
        P(),
    )
    out_specs = (
        P("batch", "seq", None),
        P("batch", "seq", None),
        P("batch", "seq", None),
        P("seq", None),
        P("seq"),
        P("seq", None),
        P("seq"),
        P("seq", None),
        P("seq"),
        P("seq", None),
        P("seq"),
        P("seq", None),
        P("seq"),
        P("seq", None),
        P("seq"),
    )
    return jax.shard_map(shards, mesh=mesh, in_specs=in_specs, out_specs=out_specs, check_vma=False)
```

time: 1710 us -> 943 us (0.55)
  matrix products: 456 us -> 128 us
  waiting for transfers between devices: 669 us -> 390 us
  other arithmetic: 252 us -> 50.1 us
  local copies, waits for them, and re-layouts: 175 us -> 38.7 us
  Pallas kernels: 0 us -> 119 us
  blocking collectives: 82.5 us -> 163 us
  loops' own time: 30.8 us -> 0 us
    dot_general x59 -> x5, matrix products: 335 us -> 24.7 us  [the longest x1 7.63 us: shards(): lax.dot_general(normed_a, grad_projected, (((0,), (1,)), ((), ())), prefe...]
    all_to_all x4 -> x6, waiting for transfers between devices: 230 us -> 67 us  [the longest x2 55.3 us: shards(): grad_local.append(exchange(grad_packed))]
    reduce_scatter x6 -> x5, waiting for transfers between devices: 364 us -> 244 us  [reduce_grad(): lax.psum_scatter(grad.astype(jnp.bfloat16), 'seq', scatter_dimension=0, t...]
    pallas_call x0 -> x4, Pallas kernels: none -> 119 us  [the longest x2 66.8 us: attend_back(): pl.pallas_call(functools.partial(bwd_kernel, utts), out_shape=jax.ShapeDt...]
    convert_element_type x27 -> x15, other arithmetic: 116 us -> 14.9 us  [the longest x10 11.1 us: reduce_grad(): return lax.psum(shard, 'batch').astype(jnp.float32)]
    all_to_all x0 -> x2, blocking collectives: none -> 62.9 us  [the longest x1 44.1 us: shards(): received.append(exchange(packed[:, h]))]
    while x97 -> x0, local copies, waits for them, and re-layouts: 55.7 us -> none
    and x16 -> x0, other arithmetic: 45.4 us -> none  [block_mask(): (row_segment[:, None] == segment_all[None, :]) & ((key_ok[None, :] > 0) |...]
  transfers between devices with their start and end apart: 11 -> 13, of which waited for: 8 -> 7; matrix products, arithmetic and copies ran while one was open for 6% -> 10% of each run, Pallas kernels for 0% -> 13%
where the time goes in v1:
time: 943 us; the launch traced here: 933 us
  waiting for transfers between devices  390 us (41%)
  blocking collectives  163 us (17%)
  matrix products  128 us (14%)
  Pallas kernels  119 us (13%)
  other arithmetic  50.1 us (5%)
  local copies, waits for them, and re-layouts  38.7 us (4%)
  starting transfers between devices  27.2 us (3%)
  between operations  17.7 us (2%)
    reduce_scatter x5, waiting for transfers between devices, reduce_grad(): lax.psum_scatter(grad.astype(jnp.bfloat16), 'seq', scatter_dimension=0, t...  244 us
    psum x1, waiting for transfers between devices, reduce_grad(): return lax.psum(shard, 'batch').astype(jnp.float32)  79.3 us
    pallas_call x2, Pallas kernels, attend_back(): pl.pallas_call(functools.partial(bwd_kernel, utts), out_shape=jax.ShapeDt...  66.8 us
    all_to_all x2, waiting for transfers between devices, shards(): grad_local.append(exchange(grad_packed))  55.3 us
    pallas_call x2, Pallas kernels, attend(): pl.pallas_call(functools.partial(fwd_kernel, utts), out_shape=(jax.ShapeD...  52.1 us
    all_to_all x1, blocking collectives, shards(): received.append(exchange(packed[:, h]))  44.1 us
    psum x1, blocking collectives, shards(): lax.psum(jnp.sum(loss_mask[0].astype(jnp.float32)), ('batch', 'seq'))  40 us
    dot_general x4, matrix products, back_dot(): lax.dot_general(left_op, right_op, (((1,), (1,)), ((), ())), preferred_el...  33.4 us
  transfers between devices with their start and end apart: 13, of which 7 were waited for; matrix products, arithmetic and copies ran while one was open for 10% of the time, Pallas kernels for 13%

profile of v1, /device:TPU:0, one launch (start us, length us, event | category | flops | bytes accessed | tf_op | source)
XLA Modules:
  0.0 933.0 jit_solution(10760233180463634839)
XLA Ops:
  48.6 44.1 %all_to_all.40.qkv_ref = bf16[8,192,512]{2,1,0:T(8,128)(2,1)} all-to-all(bf16[8,192,512]{2,1,0:T(8,128)(2,1)S(1)} %get-tuple-element.63), channel_id=1, replica_groups=mesh['batch'=4,'seq'=8] {'seq'}, dimensions={0} | all-to-all | bytes 3145728 | tf_op jit(solution)/shard_map/all_to_all | solution.py:390
  96.9 26.0 %attend.3 = (bf16[8,64,512]{2,1,0:T(8,128)(2,1)}, f32[8,1,512]{2,1,0:T(1,128)}) custom-call(s32[8]{0:T(128)} %bitcast.165, bf16[8,192,512]{2,1,0:T(8,128)(2,1)} %all_to_all.40.qkv_ref, s32[8,1,512]{2,1,0:T(1,128)} %bitcast.155), custom_call_target="tpu_custom_call" | custom-call | tf_op jit(solution)/shard_map/attend/pallas_call | solution.py:173
  123.0 11.8 %all-to-all-done.qkv_ref = bf16[8,192,512]{2,1,0:T(8,128)(2,1)} async-done(((bf16[8,192,512]{2,1,0:T(8,128)(2,1)}), bf16[8,192,512]{2,1,0:T(8,128)(2,1)}, u32[]{:S(2)}, u32[]{:S(2)}) %all-to-all-start) | async-done | bytes 1572896 | tf_op jit(solution)/shard_map/all_to_all | solution.py:390
  138.9 26.0 %attend.2 = (bf16[8,64,512]{2,1,0:T(8,128)(2,1)}, f32[8,1,512]{2,1,0:T(1,128)}) custom-call(s32[8]{0:T(128)} %bitcast.166, bf16[8,192,512]{2,1,0:T(8,128)(2,1)} %all-to-all-done.qkv_ref, s32[8,1,512]{2,1,0:T(1,128)} %bitcast.156), custom_call_target="tpu_custom_call" | custom-call | tf_op jit(solution)/shard_map/attend/pallas_call | solution.py:173
  170.6 40.0 %psum.84 = f32[]{:T(128)} all-reduce(f32[]{:T(128)} %convert_reduce_fusion), channel_id=1, replica_groups=mesh['batch'=4,'seq'=8] {'batch','seq'}, use_global_device_ids=true, to_apply=%region_7.8 | all-reduce | flops 1 | bytes 8 | tf_op jit(solution)/shard_map/psum | solution.py:408
  233.1 10.4 %fusion.39 = f32[512,1024]{1,0:T(8,128)} fusion(bf16[4096,1024]{1,0:T(8,128)(2,1)S(1)} %bitcast.175, f32[512,4096]{1,0:T(8,128)} %fusion.51, f32[4096]{0:T(1024)S(1)} %convert_element_type.183), kind=kOutput, calls=%fused_computation.124 | convolution fusion | flops 4315938816 | bytes 18890752 | tf_op jit(solution)/shard_map/dot_general | solution.py:404
  243.5 15.8 %fusion.42 = (bf16[4096]{0:T(1024)(128)(2,1)S(1)}, bf16[512,4096]{1,0:T(8,128)(2,1)}) fusion(f32[512,4096]{1,0:T(8,128)} %fusion.51, f32[4096]{0:T(1024)S(1)} %convert_element_type.183, bf16[512,1024]{1,0:T(8,128)(2,1)S(1)} %copy-done.22, bf16[4096,1024]{1,0:T(8,128)(2,1)} %param.40), kind=kOutput, calls=%fused_computation.126 | convolution fusion | flops 4341100544 | bytes 22044672 | tf_op jit(solution)/shard_map/dot_general | solution.py:47
  259.3 10.8 %multiply_reduce_fusion.1 = (f32[512]{0:T(512)S(1)}, f32[512,1024]{1,0:T(8,128)}) fusion(f32[512,1024]{1,0:T(8,128)S(1)} %get-tuple-element.53, f32[512]{0:T(512)S(1)} %broadcast_multiply_fusion.1, f32[512,6144]{1,0:T(8,128)S(1)} %bitcast.140, bf16[512,4096]{1,0:T(8,128)(2,1)} %get-tuple-element.41, bf16[1024,4096]{1,0:T(8,128)(2,1)} %param.38), kind=kOutput, calls=%fused_computation.51 | convolution fusion | flops 4297588224 | bytes 18878464 | tf_op jit(solution)/shard_map/dot_general | solution.py:47
  280.8 18.8 %all_to_all.41.do_ref = bf16[8,64,512]{2,1,0:T(8,128)(2,1)} all-to-all(bf16[8,64,512]{2,1,0:T(8,128)(2,1)S(1)} %get-tuple-element.74), channel_id=1, replica_groups=mesh['batch'=4,'seq'=8] {'seq'}, dimensions={0} | all-to-all | bytes 1048576 | tf_op jit(solution)/shard_map/all_to_all | solution.py:430
  303.5 33.4 %attend_back.2 = bf16[8,192,512]{2,1,0:T(8,128)(2,1)} custom-call(s32[8]{0:T(128)} %bitcast.167, bf16[8,192,512]{2,1,0:T(8,128)(2,1)} %all-to-all-done.qkv_ref, s32[8,1,512]{2,1,0:T(1,128)} %bitcast.157, bf16[8,64,512]{2,1,0:T(8,128)(2,1)} %get-tuple-element.19.o_ref, bf16[8,64,512]{2,1,0:T(8,128)(2,1)} %all_to_all.41.do_ref, ...), custom_call_target="tpu_custom_call" | custom-call | tf_op jit(solution)/shard_map/attend_back/pallas_call | solution.py:294
  342.0 33.4 %attend_back.3 = bf16[8,192,512]{2,1,0:T(8,128)(2,1)} custom-call(s32[8]{0:T(128)} %bitcast.168, bf16[8,192,512]{2,1,0:T(8,128)(2,1)} %all_to_all.40.qkv_ref, s32[8,1,512]{2,1,0:T(1,128)} %bitcast.158, bf16[8,64,512]{2,1,0:T(8,128)(2,1)} %get-tuple-element.20.o_ref, bf16[8,64,512]{2,1,0:T(8,128)(2,1)} %copy-done.19, f32[8,1,512]{2,1,0:T(1,128)} %get-tuple-element.22.lse_ref), custom_call_target="tpu_custom_call" | custom-call | tf_op jit(solution)/shard_map/attend_back/pallas_call | solution.py:294
  387.0 50.8 %all-to-all-done.7 = bf16[8,192,512]{2,1,0:T(8,128)(2,1)} async-done(((bf16[8,192,512]{2,1,0:T(8,128)(2,1)}), bf16[8,192,512]{2,1,0:T(8,128)(2,1)}, u32[]{:S(2)}, u32[]{:S(2)}) %all-to-all-start.7) | async-done | bytes 1572896 | tf_op jit(solution)/shard_map/all_to_all | solution.py:436
  466.0 7.6 convolution_convert_fusion.2
  474.9 13.2 %convolution_convert_fusion = bf16[4096,1024]{1,0:T(8,128)(2,1)} fusion(bf16[512,1024]{1,0:T(8,128)(2,1)S(1)} %copy-done.23, f32[512,4096]{1,0:T(8,128)} %fusion.51, f32[4096]{0:T(1024)S(1)} %convert_element_type.183), kind=kOutput, calls=%fused_computation.10 | convolution fusion | flops 4320133120 | bytes 17842176 | tf_op jit(solution)/shard_map/dot_general | solution.py:41
  489.3 9.0 convolution_convert_fusion.1
  510.0 8.0 fusion.37
  518.2 63.4 %reduce-scatter.8.cloned.1.call-done = bf16[128,3072]{1,0:T(8,128)(2,1)} async-done(((bf16[1024,3072]{1,0:T(8,128)(2,1)}), bf16[128,3072]{1,0:T(8,128)(2,1)}) %reduce-scatter.8.cloned.1.call-update) | async-done | bytes 786448 | tf_op jit(solution)/shard_map/reduce_scatter | solution.py:479
  581.6 90.1 %reduce-scatter.14.cloned.1.call-done = bf16[512,1024]{1,0:T(8,128)(2,1)} async-done(((bf16[4096,1024]{1,0:T(8,128)(2,1)}), bf16[512,1024]{1,0:T(8,128)(2,1)}) %reduce-scatter.14.cloned.1.call-update) | async-done | bytes 1048592 | tf_op jit(solution)/shard_map/reduce_scatter | solution.py:479
  671.7 90.2 %reduce-scatter.12.cloned.1.call-done = bf16[128,4096]{1,0:T(8,128)(2,1)} async-done(((bf16[1024,4096]{1,0:T(8,128)(2,1)}), bf16[128,4096]{1,0:T(8,128)(2,1)}) %reduce-scatter.12.cloned.1.call-update) | async-done | bytes 1048592 | tf_op jit(solution)/shard_map/reduce_scatter | solution.py:479
  764.4 8.2 all_gather.6
  772.7 26.1 %all-reduce.5 = (bf16[1024]{0:T(1024)(128)(2,1)S(1)}, bf16[3072]{0:T(1024)(128)(2,1)S(1)}, bf16[1024]{0:T(1024)(128)(2,1)S(1)}, bf16[4096]{0:T(1024)(128)(2,1)S(1)}, bf16[1024]{0:T(1024)(128)(2,1)S(1)}) all-reduce(bf16[1024]{0:T(1024)(128)(2,1)S(1)} %get-tuple-element.46, ...), channel_id=3, replica_groups=mesh['batch'=4,'seq'=8] {'seq'}, use_global_device_ids=true, to_apply=%region_15.16.clone | all-reduce | flops 10240 | bytes 40960
  799.2 9.2 all-reduce.6
  818.2 16.2 %all_gather.7 = f32[32,6144]{1,0:T(8,128)S(1)} all-gather(f32[8,6144]{1,0:T(8,128)} %all-reduce.11.cloned.1.call-done), channel_id=1, replica_groups=mesh['batch'=4,'seq'=8] {'batch'}, dimensions={0}, use_global_device_ids=true | all-gather | bytes 983040 | tf_op jit(solution)/shard_map/all_gather | solution.py:464
  838.1 79.3 %all-reduce.13.cloned.1.call-done = (bf16[256,1024]{1,0:T(8,128)(2,1)}, bf16[128,3072]{1,0:T(8,128)(2,1)}, bf16[128,1024]{1,0:T(8,128)(2,1)}, bf16[128,4096]{1,0:T(8,128)(2,1)}, bf16[512,1024]{1,0:T(8,128)(2,1)}) async-done(((bf16[256,1024]{1,0:T(8,128)(2,1)}, bf16[128,3072]{1,0:T(8,128)(2,1)}, bf16[128,1024]{1,0:T(8,128)(2,1)}, bf16[128,4096]{1,0:T(8,128)(2,1)}, bf16[512,1024]{1,0:T(8,128)(2,1)}), ...) | async-done | bytes 3670032 | tf_op jit(solution)/shard_map/psum | solution.py:482
  (244 shorter events, 173.5 us)
Async XLA Ops:
  7.2 209.3 %copy-start = (bf16[1024,1024]{1,0:T(8,128)(2,1)S(1)}, bf16[1024,1024]{1,0:T(8,128)(2,1)}, u32[]{:S(2)}) copy-start(bf16[1024,1024]{1,0:T(8,128)(2,1)} %param.36) | copy-start | bytes 6291460
  92.6 42.1 %all-to-all-start = ((bf16[8,192,512]{2,1,0:T(8,128)(2,1)}), bf16[8,192,512]{2,1,0:T(8,128)(2,1)}, u32[]{:S(2)}, u32[]{:S(2)}) async-start(bf16[8,192,512]{2,1,0:T(8,128)(2,1)} %get-tuple-element.62), calls=%async_computation | async-start | bytes 3145728 | tf_op jit(solution)/shard_map/all_to_all | solution.py:390
  123.0 47.0 %copy-start.45 = (s32[1,512]{1,0:T(1,128)S(1)}, s32[1,512]{1,0:T(1,128)}, u32[]{:S(2)}) copy-start(s32[1,512]{1,0:T(1,128)} %param.29) | copy-start | bytes 6148
  123.0 87.6 %copy-start.46 = (bf16[1024]{0:T(1024)(128)(2,1)S(1)}, bf16[1024]{0:T(1024)(128)(2,1)}, u32[]{:S(2)}) copy-start(bf16[1024]{0:T(1024)(128)(2,1)} %param.37) | copy-start | bytes 6148
  123.0 87.6 %copy-start.47 = (bf16[1024]{0:T(1024)(128)(2,1)S(1)}, bf16[1024]{0:T(1024)(128)(2,1)}, u32[]{:S(2)}) copy-start(bf16[1024]{0:T(1024)(128)(2,1)} %param.41) | copy-start | bytes 6148
  123.0 87.6 %copy-start.44 = (bf16[4096]{0:T(1024)(128)(2,1)S(1)}, bf16[4096]{0:T(1024)(128)(2,1)}, u32[]{:S(2)}) copy-start(bf16[4096]{0:T(1024)(128)(2,1)} %param.39) | copy-start | bytes 24580
  123.0 88.3 %copy-start.12 = (bf16[1,512,1024]{2,1,0:T(8,128)(2,1)S(1)}, bf16[1,512,1024]{2,1,0:T(8,128)(2,1)}, u32[]{:S(2)}) copy-start(bf16[1,512,1024]{2,1,0:T(8,128)(2,1)} %param.24) | copy-start | bytes 3145732
  134.8 30.2 %all-to-all-start.3 = ((bf16[8,64,512]{2,1,0:T(8,128)(2,1)}), bf16[8,64,512]{2,1,0:T(8,128)(2,1)}, u32[]{:S(2)}, u32[]{:S(2)}) async-start(bf16[8,64,512]{2,1,0:T(8,128)(2,1)} %get-tuple-element.20.o_ref), calls=%async_computation.3 | async-start | bytes 1048576 | tf_op jit(solution)/shard_map/all_to_all | solution.py:395
  164.9 50.0 %all-to-all-start.1 = ((bf16[8,64,512]{2,1,0:T(8,128)(2,1)}), bf16[8,64,512]{2,1,0:T(8,128)(2,1)}, u32[]{:S(2)}, u32[]{:S(2)}) async-start(bf16[8,64,512]{2,1,0:T(8,128)(2,1)} %get-tuple-element.19.o_ref), calls=%async_computation.1 | async-start | bytes 1048576 | tf_op jit(solution)/shard_map/all_to_all | solution.py:395
  221.7 48.4 %copy-start.3 = (f32[512,1024]{1,0:T(8,128)}, f32[512,1024]{1,0:T(8,128)S(1)}, u32[]{:S(2)}) copy-start(f32[512,1024]{1,0:T(8,128)S(1)} %get-tuple-element.53) | copy-start | bytes 6291460
  299.6 37.3 %all-to-all-start.6 = ((bf16[8,64,512]{2,1,0:T(8,128)(2,1)}), bf16[8,64,512]{2,1,0:T(8,128)(2,1)S(1)}, u32[]{:S(2)}, u32[]{:S(2)}) async-start(bf16[8,64,512]{2,1,0:T(8,128)(2,1)} %get-tuple-element.75), calls=%async_computation.6 | async-start | bytes 1048576 | tf_op jit(solution)/shard_map/all_to_all | solution.py:430
  336.9 43.0 %all-to-all-start.5 = ((bf16[8,192,512]{2,1,0:T(8,128)(2,1)}), bf16[8,192,512]{2,1,0:T(8,128)(2,1)}, u32[]{:S(2)}, u32[]{:S(2)}) async-start(bf16[8,192,512]{2,1,0:T(8,128)(2,1)} %attend_back.2), calls=%async_computation.5 | async-start | bytes 3145728 | tf_op jit(solution)/shard_map/all_to_all | solution.py:436
  379.9 57.8 %all-to-all-start.7 = ((bf16[8,192,512]{2,1,0:T(8,128)(2,1)}), bf16[8,192,512]{2,1,0:T(8,128)(2,1)}, u32[]{:S(2)}, u32[]{:S(2)}) async-start(bf16[8,192,512]{2,1,0:T(8,128)(2,1)} %attend_back.3), calls=%async_computation.7 | async-start | bytes 3145728 | tf_op jit(solution)/shard_map/all_to_all | solution.py:436
  384.2 134.0 %reduce-scatter.10.cloned.1.call-start = ((), (), s32[]{:S(2)}) async-start(), calls=%async_computation.16 | async-start | bytes 2359296 | tf_op jit(solution)/shard_map/reduce_scatter | solution.py:479
  386.9 131.3 %reduce-scatter.6.cloned.1.call-start = ((), (), s32[]{:S(2)}) async-start(), calls=%async_computation.13 | async-start | bytes 4718592 | tf_op jit(solution)/shard_map/reduce_scatter | solution.py:479
  464.8 116.8 %reduce-scatter.8.cloned.1.call-start = ((), (), s32[]{:S(2)}) async-start(), calls=%async_computation.15 | async-start | bytes 7077888 | tf_op jit(solution)/shard_map/reduce_scatter | solution.py:479
  473.7 198.0 %reduce-scatter.14.cloned.1.call-start = ((), (), s32[]{:S(2)}) async-start(), calls=%async_computation.18 | async-start | bytes 9437184 | tf_op jit(solution)/shard_map/reduce_scatter | solution.py:479
  488.1 273.8 %reduce-scatter.12.cloned.1.call-start = ((), (), s32[]{:S(2)}) async-start(), calls=%async_computation.17 | async-start | bytes 9437184 | tf_op jit(solution)/shard_map/reduce_scatter | solution.py:479
  498.3 319.9 %all-reduce.11.cloned.1.call-start = ((), (), s32[]{:S(2)}) async-start(), calls=%async_computation.14 | async-start | bytes 393216 | tf_op jit(solution)/shard_map/psum | solution.py:463
  518.0 243.8 %copy-start.50 = (u32[32]{0:T(128)S(1)}, u32[32]{0:T(128)}, u32[]{:S(2)}) copy-start(u32[32]{0:T(128)} %constant.80) | copy-start | bytes 388
  518.1 246.4 %copy-start.36 = (bf16[8,1024]{1,0:T(8,128)(2,1)S(1)}, bf16[8,1024]{1,0:T(8,128)(2,1)}, u32[]{:S(2)}) copy-start(bf16[8,1024]{1,0:T(8,128)(2,1)} %copy-done.35) | copy-start | bytes 49156
  518.1 254.7 %copy-start.39 = (bf16[1024]{0:T(1024)(128)(2,1)S(1)}, bf16[1024]{0:T(1024)(128)(2,1)}, u32[]{:S(2)}) copy-start(bf16[1024]{0:T(1024)(128)(2,1)} %get-tuple-element.38) | copy-start | bytes 6148
  518.1 293.0 %copy-start.21 = (bf16[512,1024]{1,0:T(8,128)(2,1)S(1)}, bf16[512,1024]{1,0:T(8,128)(2,1)}, u32[]{:S(2)}) copy-start(bf16[512,1024]{1,0:T(8,128)(2,1)} %copy-done.20) | copy-start | bytes 3145732
  518.1 399.4 %all-reduce.13.cloned.1.call-start = ((), (), s32[]{:S(2)}) async-start(), calls=%async_computation.19 | async-start | bytes 7340032 | tf_op jit(solution)/shard_map/psum | solution.py:482
  (49 other events, 313.3 us)
Sparse Core Ops, SparseCore 0:
  387.3 53.7 reduce-scatter.9
  464.9 46.3 reduce-scatter.5
  513.6 67.9 reduce-scatter.7
  583.7 87.9 reduce-scatter.13
  673.8 87.9 reduce-scatter.11
  764.6 52.9 all-reduce.10
  821.6 95.7 all-reduce.12

commit v2 on v1

--- a/solution.py
+++ b/solution.py
@@ -8,50 +8,8 @@
 from jax.sharding import PartitionSpec as P
 
 HEADS = 16
-
-
-epsilon = 1e-06
-
-
-def norm_rows(tensor):
-    centred = tensor - jnp.mean(tensor, axis=-1, keepdims=True)
-    spread = jnp.mean(centred * centred, axis=-1, keepdims=True)
-    return centred * lax.rsqrt(spread + epsilon)
-
-
-def modulate(hidden, shift_in, scale_in):
-    return norm_rows(hidden) * (1.0 + scale_in) + shift_in
-
-
-def gelu_tanh(tensor):
-    return jax.nn.gelu(tensor, approximate=True)
-
-
-def group_layout(lengths_row, frame_ids):
-    ends_at = jnp.cumsum(lengths_row)
-    starts_at = ends_at - lengths_row
-    member = (frame_ids[:, None] >= starts_at[None, :]) & (frame_ids[:, None] < ends_at[None, :])
-    utter_ids = jnp.arange(lengths_row.shape[0], dtype=jnp.int32)
-    segment = jnp.sum(jnp.where(member, utter_ids[None, :], 0), axis=1)
-    position = frame_ids - jnp.sum(jnp.where(member, starts_at[None, :], 0), axis=1)
-    return (member, segment, position)
-
-
-def transpose_dot(left_op, right_op):
-    return lax.dot_general(
-        left_op, right_op, (((0,), (0,)), ((), ())), preferred_element_type=jnp.float32
-    )
-
-
-def back_dot(left_op, right_op):
-    return lax.dot_general(
-        left_op, right_op, (((1,), (1,)), ((), ())), preferred_element_type=jnp.float32
-    )
-
-
-def precise_dot(left_op, right_op):
-    return jnp.dot(left_op, right_op, precision=lax.Precision.HIGHEST)
-
+HEAD_DIM = 64
+PARTS = 8
 BIG = 1e30
 DH = 64
 BQ = 512
@@ -311,6 +269,752 @@
     )(lengths, qkv, ok, out, grad, lse)
 
 
+FF_TILE = 512
+EPS = 1e-06
+
+
+def dot(left, right):
+    return jnp.dot(left, right, preferred_element_type=jnp.float32)
+
+
+def dot_nt(left, right):
+    return lax.dot_general(left, right, (((1,), (1,)), ((), ())), preferred_element_type=jnp.float32)
+
+
+def norm_stats(x):
+    mean = jnp.mean(x, axis=1, keepdims=True)
+    centred = x - mean
+    rstd = lax.rsqrt(jnp.mean(centred * centred, axis=1, keepdims=True) + EPS)
+    return centred * rstd, rstd
+
+
+def norm_back(grad, normed, rstd):
+    first = jnp.mean(grad, axis=1, keepdims=True)
+    second = jnp.mean(grad * normed, axis=1, keepdims=True)
+    return rstd * (grad - first - normed * second)
+
+
+def mods_operand(mods_ref):
+    rows = mods_ref[...]
+    return pad_rows(list(split3(rows)), 128)
+
+
+def sum_rows(hot, utts_pad, frames):
+    idx = lax.broadcasted_iota(jnp.int32, (16, frames), 0)
+    ones = jnp.where(idx == 0, 1.0, 0.0).astype(jnp.bfloat16)
+    return jnp.concatenate([hot.astype(jnp.bfloat16), ones], axis=0)
+
+
+def mid_kernel(
+    dims,
+    lengths_ref,
+    ids_ref,
+    scale_ref,
+    *refs,
+):
+    seq_ways, heads_local, utts = dims
+    att_refs = refs[:heads_local]
+    (
+        hidden_ref,
+        mods_ref,
+        cot_ref,
+        loss_ref,
+        w_out_ref,
+        b_out_ref,
+        w_up_ref,
+        b_up_ref,
+        w_down_ref,
+        b_down_ref,
+    ) = refs[heads_local : heads_local + 10]
+    outs = refs[heads_local + 10 :]
+    output_ref, after_grad_ref, tables_ref, b_up_grad_ref = outs[:4]
+    gatt_refs = outs[4 : 4 + heads_local]
+    keep_ref, send_ref = outs[4 + heads_local : 6 + heads_local]
+    (
+        attT,
+        attn_proj,
+        after,
+        nf,
+        nfT,
+        gff,
+        ff_acc,
+        gnf_acc,
+        sums,
+        cols,
+        madd,
+        grads,
+        sems,
+    ) = outs[6 + heads_local :]
+    f32, bf16 = jnp.float32, jnp.bfloat16
+    step = pl.program_id(0)
+    steps = pl.num_programs(0)
+    core = ids_ref[0]
+    rank = ids_ref[1]
+    frames, width = hidden_ref.shape
+    up_rows = width // seq_ways
+    down_rows = FF_TILE
+    z_ways = seq_ways // 2
+    parts = grads.shape[1]
+    ff_total = b_up_grad_ref.shape[1]
+    up_part = ff_total // width * up_rows // parts
+    down_block = ff_total // seq_ways
+    down_part = down_block // parts
+    out_part = up_rows // parts
+
+    def mod(index):
+        return dot(cols[...], madd[:, index * width : (index + 1) * width])
+
+    def grad_out():
+        loss = cols[:, 48:49].astype(f32)
+        return cot_ref[...].astype(f32) * (loss * scale_ref[0])
+
+    @pl.when(step == 0)
+    def _():
+        hot = onehot_rows(lengths_ref, utts, 16, rank * frames, frames)
+        hotb = hot.astype(bf16)
+        idx = lax.broadcasted_iota(jnp.int32, (16, frames), 0)
+        loss = jnp.where(idx == 0, loss_ref[...].astype(f32), 0.0).astype(bf16)
+        cols[...] = pad_rows([hotb, hotb, hotb, loss], 128).T
+        sums[...] = sum_rows(hot, 16, frames)
+        madd[...] = mods_operand(mods_ref)
+        for c in range(heads_local):
+            for s in range(seq_ways):
+                attT[(c * seq_ways + s) * DH : (c * seq_ways + s + 1) * DH, :] = att_refs[c][s]
+        proj = dot(attT[...].T, w_out_ref[...]) + b_out_ref[...].astype(f32)
+        attn_proj[...] = proj
+        mixed = hidden_ref[...] + mod(0) * proj
+        after[...] = mixed
+        normed, _ = norm_stats(mixed)
+        value = (normed * (1.0 + mod(2)) + mod(1)).astype(bf16)
+        nf[...] = value
+        nfT[...] = value.T
+        gff[...] = (grad_out() * mod(3)).astype(bf16)
+
+    up = dot(nf[...], w_up_ref[...]) + b_up_ref[...].astype(f32)
+    inner = 0.7978845608028654 * (up + 0.044715 * (up * up * up))
+    tanh = jnp.tanh(inner)
+    cdf = 0.5 * (1.0 + tanh)
+    act = (up * cdf).astype(bf16)
+    slope = cdf + 0.5 * up * (1.0 - tanh * tanh) * (
+        0.7978845608028654 * (1.0 + (3 * 0.044715) * (up * up))
+    )
+    ff_part = dot(act, w_down_ref[...])
+    gup = (dot_nt(gff[...], w_down_ref[...]) * slope).astype(bf16)
+    gnf_part = dot_nt(gup, w_up_ref[...])
+
+    @pl.when(step == 0)
+    def _():
+        ff_acc[...] = ff_part
+        gnf_acc[...] = gnf_part
+
+    @pl.when(step > 0)
+    def _():
+        ff_acc[...] += ff_part
+        gnf_acc[...] += gnf_part
+
+    b_up_grad_ref[:, pl.ds(pl.multiple_of(step * FF_TILE, FF_TILE), FF_TILE)] = dot(
+        sums[16:32, :], gup
+    )[:8]
+    halves = width // FF_TILE
+    chunk = step // halves
+    half = step % halves
+    col = pl.ds(pl.multiple_of(half * FF_TILE, FF_TILE), FF_TILE)
+    per_chunk = up_rows // up_part
+    grad_w_up = dot(nfT[...], gup).astype(bf16)
+    for s in range(seq_ways):
+        side = jnp.where(core == s % 2, 0, 1)
+        for h in range(per_chunk):
+            lo = s * up_rows + h * up_part
+            grads[side, chunk * per_chunk + h, s // 2, 0:up_part, col] = grad_w_up[lo : lo + up_part]
+    grad_w_down = dot(act.T, gff[...]).astype(bf16)
+    blocks = FF_TILE // down_block
+    copies = []
+    for b in range(blocks):
+        s = step * blocks + b
+        side = jnp.where(core == s % 2, 0, 1)
+        for k in range(parts):
+            lo = b * down_block + k * down_part
+            grads[side, k, s // 2, up_part : up_part + down_part, :] = grad_w_down[lo : lo + down_part]
+
+    def up_copy(side, j):
+        target = (keep_ref, send_ref)[side]
+        where = (
+            pl.ds((j // halves) * per_chunk, per_chunk),
+            slice(None),
+            pl.ds(0, up_part),
+            pl.ds(pl.multiple_of((j % halves) * FF_TILE, FF_TILE), FF_TILE),
+        )
+        return pltpu.make_async_copy(grads.at[side].at[where], target.at[where], sems.at[side, j])
+
+    def down_copy(side, z, index):
+        target = (keep_ref, send_ref)[side]
+        where = (slice(None), pl.ds(z, 1), pl.ds(up_part, down_part), slice(None))
+        return pltpu.make_async_copy(grads.at[side].at[where], target.at[where], sems.at[side, index])
+
+    def out_copy(side):
+        target = (keep_ref, send_ref)[side]
+        where = (slice(None), slice(None), pl.ds(up_part + down_part, out_part), slice(None))
+        return pltpu.make_async_copy(
+            grads.at[side].at[where], target.at[where], sems.at[side, ff_total // FF_TILE + z_ways]
+        )
+
+    base = ff_total // FF_TILE
+    for side in range(2):
+        up_copy(side, step).start()
+    for b in range(blocks):
+        s = step * blocks + b
+        for side in range(2):
+
+            @pl.when(lax.rem(s + core, 2) == side)
+            def _():
+                down_copy(side, s // 2, base + s // 2).start()
+
+    @pl.when(step == steps - 1)
+    def _():
+        ff_out = ff_acc[...] + b_down_ref[...].astype(f32)
+        mixed = after[...]
+        go = grad_out()
+        output_ref[...] = (mixed + mod(3) * ff_out).astype(bf16)
+        rows = sums[...]
+        tables_ref[:, 3 * width : 4 * width] = dot(rows, (go * ff_out).astype(bf16))
+        normed, rstd = norm_stats(mixed)
+        gnf = gnf_acc[...]
+        tables_ref[:, width : 2 * width] = dot(rows, gnf.astype(bf16))
+        tables_ref[:, 2 * width : 3 * width] = dot(rows, (gnf * normed).astype(bf16))
+        g_after = go + norm_back(gnf * (1.0 + mod(2)), normed, rstd)
+        after_grad_ref[...] = g_after
+        tables_ref[:, 0:width] = dot(rows, (g_after * attn_proj[...]).astype(bf16))
+        gattn = (g_after * mod(0)).astype(bf16)
+        tables_ref[:, 4 * width : 5 * width] = dot(rows, gattn)
+        tables_ref[:, 5 * width : 6 * width] = dot(rows, gff[...])
+        gattT = dot_nt(w_out_ref[...], gattn).astype(bf16)
+        for c in range(heads_local):
+            for s in range(seq_ways):
+                lo = (c * seq_ways + s) * DH
+                gatt_refs[c][s] = gattT[lo : lo + DH]
+        grad_w_out = dot(attT[...], gattn).astype(bf16)
+        for s in range(seq_ways):
+            side = jnp.where(core == s % 2, 0, 1)
+            for k in range(parts):
+                lo = s * up_rows + k * out_part
+                grads[side, k, s // 2, up_part + down_part : up_part + down_part + out_part, :] = grad_w_out[
+                    lo : lo + out_part
+                ]
+        for side in range(2):
+            out_copy(side).start()
+        for side in range(2):
+            for j in range(ff_total // FF_TILE):
+                up_copy(side, j).wait()
+            for z in range(z_ways):
+                down_copy(side, z, base + z).wait()
+            out_copy(side).wait()
+
+
+def mid_block(
+    lengths, ids, scale, att, hidden, mods, cot, loss, w_out, b_out, w_up, b_up, w_down, b_down, parts
+):
+    frames, width = hidden.shape
+    heads_local = len(att)
+    seq_ways = att[0].shape[0]
+    ff = w_up.shape[1]
+    up_rows = width // seq_ways
+    rows = (ff // width * up_rows + ff // seq_ways + up_rows) // parts
+    utts = lengths.shape[0]
+    f32, bf16 = jnp.float32, jnp.bfloat16
+    steps = ff // FF_TILE
+
+    def whole(shape):
+        return pl.BlockSpec(shape, lambda j, *_: (0,) * len(shape), pipeline_mode=pl.Buffered(1))
+
+    hbm = pl.BlockSpec(memory_space=pl.ANY)
+    gshape = (parts, seq_ways // 2, rows, width)
+    out_shape = [
+        jax.ShapeDtypeStruct((frames, width), bf16),
+        jax.ShapeDtypeStruct((frames, width), f32),
+        jax.ShapeDtypeStruct((32, 6 * width), f32),
+        jax.ShapeDtypeStruct((8, ff), f32),
+    ]
+    out_shape += [jax.ShapeDtypeStruct(a.shape, bf16) for a in att]
+    out_specs = [whole(o.shape) for o in out_shape] + [hbm, hbm]
+    out_shape += [jax.ShapeDtypeStruct(gshape, bf16)] * 2
+    ins = list(att) + [hidden, mods, cot, loss, w_out, b_out]
+    return pl.pallas_call(
+        functools.partial(mid_kernel, (seq_ways, heads_local, utts)),
+        out_shape=out_shape,
+        grid_spec=pltpu.PrefetchScalarGridSpec(
+            num_scalar_prefetch=3,
+            grid=(steps,),
+            in_specs=[whole(a.shape) for a in ins]
+            + [
+                pl.BlockSpec((width, FF_TILE), lambda j, *_: (0, j)),
+                pl.BlockSpec((1, FF_TILE), lambda j, *_: (0, j)),
+                pl.BlockSpec((FF_TILE, width), lambda j, *_: (j, 0)),
+                whole((1, width)),
+            ],
+            out_specs=out_specs,
+            scratch_shapes=[
+                pltpu.VMEM((width, frames), bf16),
+                pltpu.VMEM((frames, width), f32),
+                pltpu.VMEM((frames, width), f32),
+                pltpu.VMEM((frames, width), bf16),
+                pltpu.VMEM((width, frames), bf16),
+                pltpu.VMEM((frames, width), bf16),
+                pltpu.VMEM((frames, width), f32),
+                pltpu.VMEM((frames, width), f32),
+                pltpu.VMEM((32, frames), bf16),
+                pltpu.VMEM((frames, 128), bf16),
+                pltpu.VMEM((128, 4 * width), bf16),
+                pltpu.VMEM((2,) + gshape, bf16),
+                pltpu.SemaphoreType.DMA((2, steps + seq_ways // 2 + 1)),
+            ],
+        ),
+        compiler_params=pltpu.CompilerParams(vmem_limit_bytes=63 << 20),
+        cost_estimate=pl.CostEstimate(
+            flops=2 * frames * width * (6 * ff + 3 * width),
+            bytes_accessed=4 * width * ff * 2 + 16 * frames * width,
+            transcendentals=frames * ff,
+        ),
+        name="mid_block",
+    )(lengths, ids, scale, *ins, w_up, b_up, w_down, b_down)
+
+
+def segment_rows(lengths_ref, drop_ref, utts, base, width):
+    col = base + lax.broadcasted_iota(jnp.int32, (1, width), 1)
+    start = jnp.int32(0)
+    kept = jnp.zeros((1, width), jnp.float32)
+    place = jnp.zeros((1, width), jnp.int32)
+    for u in range(utts):
+        end = start + lengths_ref[u]
+        inside = (col >= start) & (col < end)
+        kept = jnp.where(inside, (1 - drop_ref[u]).astype(jnp.float32), kept)
+        place = jnp.where(inside, col - start, place)
+        start = end
+    return kept, place.astype(jnp.float32)
+
+
+def rotary_rows(place, half):
+    index = lax.broadcasted_iota(jnp.int32, (half, 1), 0).astype(jnp.float32)
+    inverse = jnp.exp(index * (-9.210340371976184 / half))
+    angles = inverse * place
+    return jnp.cos(angles), jnp.sin(angles)
+
+
+def frame_columns(hot, extra):
+    hotb = hot.astype(jnp.bfloat16)
+    idx = lax.broadcasted_iota(jnp.int32, hot.shape, 0)
+    last = jnp.where(idx == 0, extra, 0.0).astype(jnp.bfloat16)
+    return pad_rows([hotb, hotb, hotb, last], 128).T
+
+
+def head_kernel(
+    utts,
+    lengths_ref,
+    ids_ref,
+    drop_ref,
+    tokens_ref,
+    skip_ref,
+    cond_ref,
+    mods_ref,
+    w_skip_ref,
+    b_skip_ref,
+    hidden_ref,
+    joinedT_ref,
+    naT_ref,
+    na_ref,
+    cols,
+):
+    f32, bf16 = jnp.float32, jnp.bfloat16
+    step = pl.program_id(0)
+    frames, width = tokens_ref.shape
+    rank = ids_ref[1]
+
+    @pl.when(step == 0)
+    def _():
+        hot = onehot_rows(lengths_ref, utts, 16, rank * frames, frames)
+        kept, _ = segment_rows(lengths_ref, drop_ref, utts, rank * frames, frames)
+        cols[...] = frame_columns(hot, kept)
+        keep = cols[:, 48:49].astype(f32)
+        mixed = (tokens_ref[...].astype(f32) + keep * cond_ref[...].astype(f32)).astype(bf16)
+        joinedT_ref[0:width, :] = mixed.T
+        hidden_ref[...] = dot(mixed, w_skip_ref[...]) + b_skip_ref[...].astype(f32)
+
+    @pl.when(step == 1)
+    def _():
+        skip = skip_ref[...]
+        joinedT_ref[width : 2 * width, :] = skip.T
+        hidden = hidden_ref[...] + dot(skip, w_skip_ref[...])
+        hidden_ref[...] = hidden
+        madd = mods_operand(mods_ref)
+        shift = dot(cols[...], madd[:, :width])
+        scale = dot(cols[...], madd[:, width:])
+        normed, _ = norm_stats(hidden)
+        value = (normed * (1.0 + scale) + shift).astype(bf16)
+        na_ref[...] = value
+        naT_ref[...] = value.T
+
+
+def head_block(lengths, ids, drop, tokens, skip, cond, mods, w_skip, b_skip):
+    frames, width = tokens.shape
+    utts = lengths.shape[0]
+    f32, bf16 = jnp.float32, jnp.bfloat16
+
+    def whole(shape):
+        return pl.BlockSpec(shape, lambda j, *_: (0,) * len(shape), pipeline_mode=pl.Buffered(1))
+
+    out_shape = [
+        jax.ShapeDtypeStruct((frames, width), f32),
+        jax.ShapeDtypeStruct((2 * width, frames), bf16),
+        jax.ShapeDtypeStruct((width, frames), bf16),
+        jax.ShapeDtypeStruct((frames, width), bf16),
+    ]
+    return pl.pallas_call(
+        functools.partial(head_kernel, utts),
+        out_shape=out_shape,
+        grid_spec=pltpu.PrefetchScalarGridSpec(
+            num_scalar_prefetch=3,
+            grid=(2,),
+            in_specs=[whole(a.shape) for a in (tokens, skip, cond, mods)]
+            + [pl.BlockSpec((width, width), lambda j, *_: (j, 0)), whole((1, width))],
+            out_specs=[whole(o.shape) for o in out_shape],
+            scratch_shapes=[pltpu.VMEM((frames, 128), bf16)],
+        ),
+        compiler_params=pltpu.CompilerParams(vmem_limit_bytes=48 << 20),
+        cost_estimate=pl.CostEstimate(
+            flops=4 * frames * width * width, bytes_accessed=20 * frames * width, transcendentals=0
+        ),
+        name="head_block",
+    )(lengths, ids, drop, tokens, skip, cond, mods, w_skip, b_skip)
+
+
+def turn_heads(tensor, cosine, sine):
+    half = DH // 2
+    first, second = tensor[:, :half], tensor[:, half:]
+    return jnp.concatenate([first * cosine - second * sine, second * cosine + first * sine], axis=1)
+
+
+def qkv_kernel(utts, seq_ways, lengths_ref, ids_ref, drop_ref, na_ref, w_ref, b_ref, out_ref, trig):
+    f32, bf16 = jnp.float32, jnp.bfloat16
+    part = pl.program_id(0)
+    frames = na_ref.shape[0]
+
+    @pl.when(part == 0)
+    def _():
+        _, place = segment_rows(lengths_ref, drop_ref, utts, ids_ref[1] * frames, frames)
+        cosine, sine = rotary_rows(place, DH // 2)
+        trig[0] = cosine
+        trig[1] = sine
+
+    raw = dot(na_ref[...], w_ref[...]) + b_ref[...].astype(f32)
+    rawT = raw.T.reshape(seq_ways, DH, frames)
+    turned = part < 2
+    cosine = jnp.where(turned, trig[0], 1.0)[None]
+    sine = jnp.where(turned, trig[1], 0.0)[None]
+    out_ref[:, pl.ds(pl.multiple_of(part * DH, DH), DH), :] = turn_heads(rawT, cosine, sine).astype(bf16)
+
+
+def qkv_block(lengths, ids, drop, na, w_qkv, b_qkv, chunk, seq_ways):
+    frames, width = na.shape
+    cols = seq_ways * DH
+    chunks = width // cols
+    utts = lengths.shape[0]
+
+    def whole(shape):
+        return pl.BlockSpec(shape, lambda j, *_: (0,) * len(shape), pipeline_mode=pl.Buffered(1))
+
+    shape = (seq_ways, 3 * DH, frames)
+    return pl.pallas_call(
+        functools.partial(qkv_kernel, utts, seq_ways),
+        out_shape=jax.ShapeDtypeStruct(shape, jnp.bfloat16),
+        grid_spec=pltpu.PrefetchScalarGridSpec(
+            num_scalar_prefetch=3,
+            grid=(3,),
+            in_specs=[
+                whole(na.shape),
+                pl.BlockSpec((width, cols), lambda j, *_: (0, j * chunks + chunk)),
+                pl.BlockSpec((1, cols), lambda j, *_: (0, j * chunks + chunk)),
+            ],
+            out_specs=whole(shape),
+            scratch_shapes=[pltpu.VMEM((2, DH // 2, frames), jnp.float32)],
+        ),
+        cost_estimate=pl.CostEstimate(
+            flops=6 * frames * width * cols, bytes_accessed=10 * frames * width, transcendentals=0
+        ),
+        name="qkv_block",
+    )(lengths, ids, drop, na, w_qkv, b_qkv)
+
+
+def back_kernel(utts, seq_ways, first, lengths_ref, ids_ref, drop_ref, grad_ref, naT_ref, w_ref, *refs):
+    if first:
+        acc_in = None
+        acc_ref, bias_ref, keep_ref, send_ref, trig = refs
+    else:
+        acc_in, acc_ref, bias_ref, keep_ref, send_ref, trig = refs
+    f32, bf16 = jnp.float32, jnp.bfloat16
+    part = pl.program_id(0)
+    width, frames = naT_ref.shape
+    core = ids_ref[0]
+    parts = keep_ref.shape[0]
+    own = width // seq_ways
+    rows = own // parts
+
+    @pl.when(part == 0)
+    def _():
+        _, place = segment_rows(lengths_ref, drop_ref, utts, ids_ref[1] * frames, frames)
+        cosine, sine = rotary_rows(place, DH // 2)
+        trig[0] = cosine
+        trig[1] = sine
+
+    turned = part < 2
+    cosine = jnp.where(turned, trig[0], 1.0)[None]
+    sine = jnp.where(turned, trig[1], 0.0)[None]
+    raw = grad_ref[:, pl.ds(pl.multiple_of(part * DH, DH), DH), :].astype(f32)
+    gpT = turn_heads(raw, cosine, -sine).astype(bf16).reshape(seq_ways * DH, frames)
+    gna = dot(w_ref[...], gpT)
+
+    @pl.when(part == 0)
+    def _():
+        acc_ref[...] = gna if first else acc_in[...] + gna
+
+    @pl.when(part > 0)
+    def _():
+        acc_ref[...] += gna
+
+    ones = jnp.ones((8, frames), bf16)
+    bias_ref[0] = dot_nt(ones, gpT)
+    grad_w = dot_nt(naT_ref[...], gpT).astype(bf16)
+    for s in range(seq_ways):
+        for k in range(parts):
+            tile = grad_w[s * own + k * rows : s * own + (k + 1) * rows]
+
+            @pl.when(core == s % 2)
+            def _():
+                keep_ref[k, s // 2] = tile
+
+            @pl.when(core != s % 2)
+            def _():
+                send_ref[k, s // 2] = tile
+
+
+def back_block(lengths, ids, drop, grad, naT, w_qkv, acc, chunk, parts):
+    seq_ways, _, frames = grad.shape
+    width = naT.shape[0]
+    cols = seq_ways * DH
+    chunks = width // cols
+    utts = lengths.shape[0]
+    f32, bf16 = jnp.float32, jnp.bfloat16
+    rows = width // seq_ways // parts
+
+    def whole(shape):
+        return pl.BlockSpec(shape, lambda j, *_: (0,) * len(shape), pipeline_mode=pl.Buffered(1))
+
+    gblock = (parts, seq_ways // 2, rows, cols)
+    gspec = pl.BlockSpec(gblock, lambda j, *_: (0, 0, 0, j))
+    gshape = jax.ShapeDtypeStruct((parts, seq_ways // 2, rows, 3 * cols), bf16)
+    ins = [grad, naT, w_qkv] + ([] if acc is None else [acc])
+    in_specs = [whole(grad.shape), whole(naT.shape)]
+    in_specs += [pl.BlockSpec((width, cols), lambda j, *_: (0, j * chunks + chunk))]
+    if acc is not None:
+        in_specs += [whole(acc.shape)]
+    return pl.pallas_call(
+        functools.partial(back_kernel, utts, seq_ways, acc is None),
+        out_shape=[
+            jax.ShapeDtypeStruct((width, frames), f32),
+            jax.ShapeDtypeStruct((3, 8, cols), f32),
+            gshape,
+            gshape,
+        ],
+        grid_spec=pltpu.PrefetchScalarGridSpec(
+            num_scalar_prefetch=3,
+            grid=(3,),
+            in_specs=in_specs,
+            out_specs=[
+                whole((width, frames)),
+                pl.BlockSpec((1, 8, cols), lambda j, *_: (j, 0, 0)),
+                gspec,
+                gspec,
+            ],
+            scratch_shapes=[pltpu.VMEM((2, DH // 2, frames), f32)],
+        ),
+        cost_estimate=pl.CostEstimate(
+            flops=12 * frames * width * cols, bytes_accessed=20 * frames * width, transcendentals=0
+        ),
+        name="back_block",
+    )(lengths, ids, drop, *ins)
+
+
+def tail_kernel(
+    utts,
+    seq_ways,
+    lengths_ref,
+    ids_ref,
+    acc_ref,
+    hidden_ref,
+    after_ref,
+    mods_ref,
+    joinedT_ref,
+    w_skip_ref,
+    tables_ref,
+    grad_a_ref,
+    grad_b_ref,
+    keep_ref,
+    send_ref,
+    gh_ref,
+):
+    f32, bf16 = jnp.float32, jnp.bfloat16
+    step = pl.program_id(0)
+    frames, width = hidden_ref.shape
+    core = ids_ref[0]
+    parts = keep_ref.shape[0]
+    block = 2 * width // seq_ways
+    rows = block // parts
+
+    @pl.when(step == 0)
+    def _():
+        hot = onehot_rows(lengths_ref, utts, 16, ids_ref[1] * frames, frames)
+        cols = frame_columns(hot, jnp.zeros((1, frames), f32))
+        madd = mods_operand(mods_ref)
+        scale = dot(cols, madd[:, width:])
+        gna = acc_ref[...].T
+        normed, rstd = norm_stats(hidden_ref[...])
+        sums = sum_rows(hot, 16, frames)
+        tables_ref[:, 0:width] = dot(sums, gna.astype(bf16))
+        tables_ref[:, width : 2 * width] = dot(sums, (gna * normed).astype(bf16))
+        gh = (after_ref[...] + norm_back(gna * (1.0 + scale), normed, rstd)).astype(bf16)
+        gh_ref[...] = gh
+        tables_ref[:, 2 * width : 3 * width] = dot(sums, gh)
+
+    gh = gh_ref[...]
+    grad_w = dot(joinedT_ref[...], gh).astype(bf16)
+    blocks = width // block
+    for b in range(blocks):
+        for k in range(parts):
+            tile = grad_w[b * block + k * rows : b * block + (k + 1) * rows]
+
+            @pl.when(core == b % 2)
+            def _():
+                keep_ref[k, b // 2] = tile
+
+            @pl.when(core != b % 2)
+            def _():
+                send_ref[k, b // 2] = tile
+
+    joined = dot_nt(gh, w_skip_ref[...])
+
+    @pl.when(step == 0)
+    def _():
+        grad_a_ref[...] = joined
+
+    @pl.when(step == 1)
+    def _():
+        grad_b_ref[...] = joined
+
+
+def tail_block(lengths, ids, acc, hidden, after, mods, joinedT, w_skip, seq_ways, parts):
+    frames, width = hidden.shape
+    utts = lengths.shape[0]
+    f32, bf16 = jnp.float32, jnp.bfloat16
+    rows = 2 * width // seq_ways // parts
+
+    def whole(shape):
+        return pl.BlockSpec(shape, lambda j, *_: (0,) * len(shape), pipeline_mode=pl.Buffered(1))
+
+    gspec = pl.BlockSpec((parts, seq_ways // 4, rows, width), lambda j, *_: (0, j, 0, 0))
+    gshape = jax.ShapeDtypeStruct((parts, seq_ways // 2, rows, width), bf16)
+    out_shape = [
+        jax.ShapeDtypeStruct((32, 3 * width), f32),
+        jax.ShapeDtypeStruct((frames, width), f32),
+        jax.ShapeDtypeStruct((frames, width), f32),
+        gshape,
+        gshape,
+    ]
+    return pl.pallas_call(
+        functools.partial(tail_kernel, utts, seq_ways),
+        out_shape=out_shape,
+        grid_spec=pltpu.PrefetchScalarGridSpec(
+            num_scalar_prefetch=2,
+            grid=(2,),
+            in_specs=[whole(a.shape) for a in (acc, hidden, after, mods)]
+            + [
+                pl.BlockSpec((width, frames), lambda j, *_: (j, 0)),
+                pl.BlockSpec((width, width), lambda j, *_: (j, 0)),
+            ],
+            out_specs=[whole(o.shape) for o in out_shape[:3]] + [gspec, gspec],
+            scratch_shapes=[pltpu.VMEM((frames, width), bf16)],
+        ),
+        compiler_params=pltpu.CompilerParams(vmem_limit_bytes=48 << 20),
+        cost_estimate=pl.CostEstimate(
+            flops=8 * frames * width * width, bytes_accessed=30 * frames * width, transcendentals=0
+        ),
+        name="tail_block",
+    )(lengths, ids, acc, hidden, after, mods, joinedT, w_skip)
+
+
+def sum_exchange(value, axis, bit):
+    ways = lax.axis_size(axis)
+    return lax.ppermute(value, axis, [(i, i ^ bit) for i in range(ways)])
+
+
+def add_pair(left, right):
+    return (left.astype(jnp.float32) + right.astype(jnp.float32)).astype(jnp.bfloat16)
+
+
+def pick(value, bit, axis=0):
+    return lax.dynamic_index_in_dim(value, bit, axis, keepdims=False)
+
+
+def axis_bits(ways):
+    return [1 << i for i in range(ways.bit_length() - 1)]
+
+
+def reduce_blocks(keep, send):
+    seq_ways, batch_ways = lax.axis_size("seq"), lax.axis_size("batch")
+    seq_rank, batch_rank = lax.axis_index("seq"), lax.axis_index("batch")
+    side = 1 << ((batch_ways.bit_length() - 1) // 2)
+    x_bit, y_bit = 1, side
+    x = lax.rem(batch_rank, 2)
+    y = lax.rem(batch_rank // side, 2)
+    _, z_ways, rows, width = keep.shape
+    total = add_pair(keep, sum_exchange(send, "seq", 1)).reshape(2, 2, 2, z_ways, rows, width)
+    first = []
+    for block, mine, bit in ((total[0], x, x_bit), (total[1], y, y_bit)):
+        got = sum_exchange(pick(block, 1 - mine), "batch", bit)
+        first.append(add_pair(pick(block, mine), got))
+    second = []
+    for block, mine, bit in ((first[0], y, y_bit), (first[1], x, x_bit)):
+        got = sum_exchange(pick(block, 1 - mine), "batch", bit)
+        second.append(add_pair(pick(block, mine), got))
+    block = jnp.stack(second)
+    for bit in axis_bits(batch_ways):
+        if bit not in (x_bit, y_bit):
+            block = add_pair(block, sum_exchange(block, "batch", bit))
+    z = seq_rank // 2
+    for i, bit in enumerate(axis_bits(z_ways)):
+        mine = lax.rem(z // bit, 2)
+        block = block.reshape(2, block.shape[1] // 2, 2, rows, width)
+        got = sum_exchange(pick(block, 1 - mine, 2), "seq", 2 * bit)
+        block = add_pair(pick(block, mine, 2), got)
+    block = block.reshape(2, rows, width)
+    got_x = sum_exchange(block, "batch", x_bit)
+    got_y = sum_exchange(block, "batch", y_bit)
+    got_xy = sum_exchange(block, "batch", x_bit | y_bit)
+    table = jnp.stack([jnp.stack([block, got_y]), jnp.stack([got_x, got_xy])])
+    table = jnp.where(x == 1, table[::-1], table)
+    table = jnp.where(y == 1, table[:, ::-1], table)
+    return jnp.concatenate(
+        [table[:, :, 0].reshape(4, rows, width), jnp.swapaxes(table[:, :, 1], 0, 1).reshape(4, rows, width)]
+    ).astype(jnp.float32)
+
+
+def gather_groups(value):
+    return [value] + [sum_exchange(value, "batch", i) for i in range(1, lax.axis_size("batch"))]
+
+
+def sum_seq(value):
+    for bit in axis_bits(lax.axis_size("seq")):
+        value = value + sum_exchange(value, "seq", bit)
+    return value
+
+
 def shards(
     tokens_in,
     skip_in,
@@ -334,185 +1038,160 @@
     w_down,
     b_down,
 ):
-    seq_ways = lax.axis_size("seq")
+    f32, bf16 = jnp.float32, jnp.bfloat16
+    seq_ways, batch_ways = lax.axis_size("seq"), lax.axis_size("batch")
     seq_rank = lax.axis_index("seq")
-    frames = tokens_in.shape[1]
-    model_width = tokens_in.shape[2]
+    frames, width = tokens_in.shape[1:]
     group_frames = frames * seq_ways
-    local_heads = HEADS // seq_ways
-    head_size = model_width // HEADS
-    lengths_row = lengths[0]
-    key_ok = key_mask[0]
-    local_ids = seq_rank * frames + jnp.arange(frames, dtype=jnp.int32)
-    member, segment_local, position = group_layout(lengths_row, local_ids)
-    onehot = member.astype(jnp.float32)
-    keep_frame = precise_dot(onehot, (1 - drop_mask[0]).astype(jnp.float32))
-    mixed_in = tokens_in[0].astype(jnp.float32) + keep_frame[:, None] * condition[0].astype(
-        jnp.float32
+    heads_local = HEADS // seq_ways
+    utts = lengths.shape[1]
+    lengths_row, drop = lengths[0], drop_mask[0]
+    ids = jnp.stack([lax.rem(seq_rank, 2), seq_rank]).astype(jnp.int32)
+    ok = key_mask.reshape(seq_ways, 1, frames)
+    exchange = functools.partial(lax.all_to_all, axis_name="seq", split_axis=0, concat_axis=0, tiled=True)
+
+    time_act = jax.nn.silu(time_embed[0]).astype(bf16)
+    time_rows = jnp.pad(time_act, ((0, 16 - utts), (0, 0)))
+
+    def modulation(first, last):
+        return jnp.dot(time_rows, w_ada[:, first:last], preferred_element_type=f32) + b_ada[
+            first:last
+        ].astype(f32)
+
+    mods_a = modulation(0, 2 * width)
+    hidden, joinedT, naT, na = head_block(
+        lengths_row, ids, drop, tokens_in[0], skip_in[0], condition[0], mods_a, w_skip, b_skip[None]
     )
-    joined = jnp.concatenate([mixed_in.astype(jnp.bfloat16), skip_in[0]], axis=1)
-    hidden = jnp.dot(joined, w_skip, preferred_element_type=jnp.float32) + b_skip.astype(
-        jnp.float32
-    )
-    time_act = jax.nn.silu(time_embed[0]).astype(jnp.bfloat16)
-    modulation = jnp.dot(time_act, w_ada, preferred_element_type=jnp.float32) + b_ada.astype(
-        jnp.float32
-    )
-    frame_mods = precise_dot(onehot, modulation)
-    shift_a, scale_a, gate_a, shift_f, scale_f, gate_f = jnp.split(frame_mods, 6, axis=1)
-    normed_a, pull_norm_a = jax.vjp(modulate, hidden, shift_a, scale_a)
-    normed_a = normed_a.astype(jnp.bfloat16)
-    half = head_size // 2
-    projected = lax.dot_general(
-        w_qkv, normed_a, (((0,), (1,)), ((), ())), preferred_element_type=jnp.float32
-    ) + b_qkv.astype(jnp.float32)[:, None]
-    projected = projected.reshape(3, HEADS, head_size, frames)
-    inverse = 10000.0 ** (-(2.0 * jnp.arange(half, dtype=jnp.float32)) / head_size)
-    angles = inverse[:, None] * position.astype(jnp.float32)[None, :]
-    cosine, sine = jnp.cos(angles)[None], jnp.sin(angles)[None]
-
-    def turn(tensor, sign):
-        first, second = tensor[:, :half], tensor[:, half:]
-        return jnp.concatenate(
-            [first * cosine - sign * second * sine, second * cosine + sign * first * sine], axis=1
-        )
-
-    packed = jnp.concatenate(
-        [turn(projected[0], 1.0), turn(projected[1], 1.0), projected[2]], axis=1
-    ).astype(jnp.bfloat16)
-    packed = packed.reshape(seq_ways, local_heads, 3 * head_size, frames)
-    ok = key_ok.reshape(seq_ways, 1, frames)
-    exchange = functools.partial(
-        lax.all_to_all, axis_name="seq", split_axis=0, concat_axis=0, tiled=True
-    )
-    received, head_out, log_totals, returned = [], [], [], []
-    for h in range(local_heads):
-        received.append(exchange(packed[:, h]))
-    for h in range(local_heads):
-        out, log_total = attend(lengths_row, received[h], ok)
+    received = []
+    for c in range(heads_local):
+        packed = qkv_block(lengths_row, ids, drop, na, w_qkv, b_qkv[None], c, seq_ways)
+        received.append(exchange(packed))
+
+    count = jnp.sum(loss_mask.astype(f32))
+    count = sum_seq(jnp.full((8, 128), count))
+    for bit in axis_bits(batch_ways):
+        count = count + sum_exchange(count, "batch", bit)
+    scale = (group_frames * batch_ways) / count[0, :1]
+    mods_rest = modulation(2 * width, 6 * width)
+    time_all = jnp.concatenate(gather_groups(time_act))
+
+    head_out, log_totals, returned = [], [], []
+    for c in range(heads_local):
+        out, log_total = attend(lengths_row, received[c], ok)
         head_out.append(out)
         log_totals.append(log_total)
         returned.append(exchange(out))
-    attended = jnp.stack(returned, axis=1).reshape(model_width, frames)
-    attn_proj = transpose_dot(attended, w_out) + b_out.astype(jnp.float32)
-    after_attn = hidden + gate_a * attn_proj
-    normed_f, pull_norm_f = jax.vjp(modulate, after_attn, shift_f, scale_f)
-    normed_f = normed_f.astype(jnp.bfloat16)
-    up_proj = jnp.dot(normed_f, w_up, preferred_element_type=jnp.float32) + b_up.astype(jnp.float32)
-    activated, pull_gelu = jax.vjp(gelu_tanh, up_proj)
-    activated = activated.astype(jnp.bfloat16)
-    ff_out = jnp.dot(activated, w_down, preferred_element_type=jnp.float32) + b_down.astype(
-        jnp.float32
+    mid = mid_block(
+        lengths_row,
+        ids,
+        scale,
+        returned,
+        hidden,
+        mods_rest,
+        cotangent[0],
+        loss_mask,
+        w_out,
+        b_out[None],
+        w_up,
+        b_up[None],
+        w_down,
+        b_down[None],
+        PARTS,
     )
-    output = after_attn + gate_f * ff_out
-    frame_count = lax.psum(jnp.sum(loss_mask[0].astype(jnp.float32)), ("batch", "seq"))
-    grad_scale = group_frames * lax.axis_size("batch") / frame_count
-    grad_out = (
-        cotangent[0].astype(jnp.float32) * loss_mask[0].astype(jnp.float32)[:, None] * grad_scale
+    output, after_grad, tables, b_up_grad = mid[:4]
+    grad_att = mid[4 : 4 + heads_local]
+    keep_f, send_f = mid[4 + heads_local :]
+    grad_heads = [exchange(g) for g in grad_att]
+    feed = reduce_blocks(keep_f, send_f)
+    early = jnp.concatenate([tables[:utts, : 4 * width].reshape(-1), b_up_grad[0], tables[16, 4 * width :]])
+    early = early.reshape(-1, 2 * width)
+    early = gather_groups(sum_seq(early))
+
+    acc, part_biases, part_blocks = None, [], []
+    grad_local = []
+    for c in range(heads_local):
+        grad = attend_back(lengths_row, received[c], ok, head_out[c], grad_heads[c], log_totals[c])
+        grad_local.append(exchange(grad))
+    for c in range(heads_local):
+        acc, bias, keep, send = back_block(
+            lengths_row, ids, drop, grad_local[c], naT, w_qkv, acc, c, PARTS
+        )
+        part_biases.append(bias[:, 0])
+        part_blocks.append(reduce_blocks(keep, send))
+    late_tables, grad_tokens, grad_skip, keep, send = tail_block(
+        lengths_row, ids, acc, hidden, after_grad, mods_a, joinedT, w_skip, seq_ways, PARTS
     )
-    grad_ff = (grad_out * gate_f).astype(jnp.bfloat16)
-    grad_gate_f = grad_out * ff_out
-    grad_w_down = transpose_dot(activated, grad_ff)
-    grad_b_down = jnp.sum(grad_ff.astype(jnp.float32), axis=0)
-    grad_act = back_dot(grad_ff, w_down)
-    grad_up = pull_gelu(grad_act)[0].astype(jnp.bfloat16)
-    grad_w_up = transpose_dot(normed_f, grad_up)
-    grad_b_up = jnp.sum(grad_up.astype(jnp.float32), axis=0)
-    grad_normed_f = back_dot(grad_up, w_up)
-    grad_after_norm, grad_shift_f, grad_scale_f = pull_norm_f(grad_normed_f)
-    grad_after = grad_out + grad_after_norm
-    grad_attn = (grad_after * gate_a).astype(jnp.bfloat16)
-    grad_gate_a = grad_after * attn_proj
-    grad_w_out = jnp.dot(attended, grad_attn, preferred_element_type=jnp.float32)
-    grad_b_out = jnp.sum(grad_attn.astype(jnp.float32), axis=0)
-    grad_attended = back_dot(w_out, grad_attn).astype(jnp.bfloat16)
-    grad_attended = grad_attended.reshape(seq_ways, local_heads, head_size, frames)
-    grad_heads = [exchange(grad_attended[:, h]) for h in range(local_heads)]
-    grad_local = []
-    for h in range(local_heads):
-        grad_packed = attend_back(
-            lengths_row, received[h], ok, head_out[h], grad_heads[h], log_totals[h]
+    skip_blocks = reduce_blocks(keep, send)
+    late = jnp.concatenate(
+        [
+            late_tables[:utts, : 2 * width].reshape(-1),
+            jnp.stack(part_biases, axis=1).reshape(-1),
+            late_tables[16, 2 * width :],
+        ]
+    ).reshape(-1, 2 * width)
+    late = gather_groups(sum_seq(late))
+
+    ada_rows = width // seq_ways
+    own_time = lax.dynamic_slice_in_dim(time_all, seq_rank * ada_rows, ada_rows, axis=1).astype(f32)
+
+    def own_slice(vector):
+        size = vector.shape[0] // seq_ways
+        return lax.dynamic_slice_in_dim(vector, seq_rank * size, size)
+
+    def ada_part(groups, tables_count):
+        rows = jnp.concatenate(
+            [g.reshape(-1)[: utts * tables_count * width].reshape(utts, -1) for g in groups]
         )
-        grad_local.append(exchange(grad_packed))
-    grad_local = jnp.stack(grad_local, axis=1).reshape(HEADS, 3, head_size, frames)
-    grad_local = grad_local.astype(jnp.float32)
-    grad_projected = jnp.stack(
-        [turn(grad_local[:, 0], -1.0), turn(grad_local[:, 1], -1.0), grad_local[:, 2]]
+        weight = lax.dot_general(
+            own_time, rows, (((0,), (0,)), ((), ())), precision=lax.Precision.HIGHEST
+        )
+        return weight, jnp.sum(rows, axis=0)
+
+    early_weight, early_bias = ada_part(early, 4)
+    late_weight, late_bias = ada_part(late, 2)
+    grad_w_ada = jnp.concatenate([late_weight, early_weight], axis=1)
+    grad_b_ada = own_slice(jnp.concatenate([late_bias, early_bias]))
+    early_vec = sum(g.reshape(-1)[utts * 4 * width :] for g in early)
+    late_vec = sum(g.reshape(-1)[utts * 2 * width :] for g in late)
+    ff = w_up.shape[1]
+    grad_b_up = own_slice(early_vec[:ff])
+    grad_b_out = own_slice(early_vec[ff : ff + width])
+    grad_b_down = own_slice(early_vec[ff + width :])
+    grad_b_qkv = own_slice(late_vec[: 3 * width])
+    grad_b_skip = own_slice(late_vec[3 * width :])
+
+    own = width // seq_ways
+    chunks = ff // width
+    up_part = chunks * own // PARTS
+    down_part = ff // seq_ways // PARTS
+    halves = own // up_part
+    grad_w_up = (
+        feed[:, :up_part]
+        .reshape(chunks, halves, up_part, width)
+        .transpose(1, 2, 0, 3)
+        .reshape(own, ff)
     )
-    grad_projected = grad_projected.reshape(3 * model_width, frames).astype(jnp.bfloat16)
-    grad_w_qkv = lax.dot_general(
-        normed_a, grad_projected, (((0,), (1,)), ((), ())), preferred_element_type=jnp.float32
-    )
-    grad_b_qkv = jnp.sum(grad_projected.astype(jnp.float32), axis=1)
-    grad_normed_a = lax.dot_general(
-        grad_projected, w_qkv, (((0,), (1,)), ((), ())), preferred_element_type=jnp.float32
-    )
-    grad_hidden_norm, grad_shift_a, grad_scale_a = pull_norm_a(grad_normed_a)
-    grad_hidden = (grad_after + grad_hidden_norm).astype(jnp.bfloat16)
-    grad_w_skip = transpose_dot(joined, grad_hidden)
-    grad_b_skip = jnp.sum(grad_hidden.astype(jnp.float32), axis=0)
-    grad_joined = back_dot(grad_hidden, w_skip)
-    grad_tokens = grad_joined[:, :model_width]
-    grad_skip = grad_joined[:, model_width:]
-    grad_frame_mods = jnp.concatenate(
-        [grad_shift_a, grad_scale_a, grad_gate_a, grad_shift_f, grad_scale_f, grad_gate_f], axis=1
-    )
-    grad_modulation = lax.dot_general(
-        onehot, grad_frame_mods, (((0,), (0,)), ((), ())), precision=lax.Precision.HIGHEST
-    )
-    grad_modulation = lax.psum(grad_modulation, "seq")
-    all_modulation = lax.all_gather(grad_modulation, "batch", axis=0, tiled=True)
-    all_time = lax.all_gather(time_act, "batch", axis=0, tiled=True)
-    ada_rows = model_width // seq_ways
-    own_time = lax.dynamic_slice_in_dim(all_time, seq_rank * ada_rows, ada_rows, axis=1)
-    grad_w_ada = lax.dot_general(
-        own_time.astype(jnp.float32),
-        all_modulation,
-        (((0,), (0,)), ((), ())),
-        precision=lax.Precision.HIGHEST,
-    )
-    bias_rows = all_modulation.shape[1] // seq_ways
-    grad_b_ada = jnp.sum(
-        lax.dynamic_slice_in_dim(all_modulation, seq_rank * bias_rows, bias_rows, axis=1), axis=0
-    )
-    def reduce_grad(grad):
-        shard = lax.psum_scatter(
-            grad.astype(jnp.bfloat16), "seq", scatter_dimension=0, tiled=True
-        )
-        return lax.psum(shard, "batch").astype(jnp.float32)
-
-    reduced = [
-        reduce_grad(g)
-        for g in (
-            grad_w_skip,
-            grad_b_skip,
-            grad_w_qkv,
-            grad_b_qkv,
-            grad_w_out,
-            grad_b_out,
-            grad_w_up,
-            grad_b_up,
-            grad_w_down,
-            grad_b_down,
-        )
-    ]
-    reduced = reduced[:2] + [grad_w_ada, grad_b_ada] + reduced[2:]
+    grad_w_down = feed[:, up_part : up_part + down_part].reshape(ff // seq_ways, width)
+    grad_w_out = feed[:, up_part + down_part :].reshape(own, width)
+    cols = seq_ways * HEAD_DIM
+    grad_w_qkv = jnp.stack([b.reshape(own, 3, cols) for b in part_blocks], axis=2).reshape(own, 3 * width)
+    grad_w_skip = skip_blocks.reshape(2 * own, width)
     return (
-        output.astype(jnp.bfloat16)[None],
+        output[None],
         grad_tokens[None],
         grad_skip[None],
-        reduced[0],
-        reduced[1],
-        reduced[2],
-        reduced[3],
-        reduced[4],
-        reduced[5],
-        reduced[6],
-        reduced[7],
-        reduced[8],
-        reduced[9],
-        reduced[10],
-        reduced[11],
+        grad_w_skip,
+        grad_b_skip,
+        grad_w_ada,
+        grad_b_ada,
+        grad_w_qkv,
+        grad_b_qkv,
+        grad_w_out,
+        grad_b_out,
+        grad_w_up,
+        grad_b_up,
+        grad_w_down,
+        grad_b_down,
     )
 
 

time: 943 us -> 716 us (0.76)
  blocking collectives: 163 us -> 19.5 us
  waiting for transfers between devices: 390 us -> 253 us
  matrix products: 128 us -> 9.93 us
  Pallas kernels: 119 us -> 226 us
  starting transfers between devices: 27.2 us -> 104 us
  between operations: 17.7 us -> 3.23 us
  local copies, waits for them, and re-layouts: 38.7 us -> 49.5 us
    reduce_scatter x5 -> x0, waiting for transfers between devices: 244 us -> none  [reduce_grad(): lax.psum_scatter(grad.astype(jnp.bfloat16), 'seq', scatter_dimension=0, t...]
    ppermute x0 -> x60, waiting for transfers between devices: none -> 203 us  [sum_exchange(): return lax.ppermute(value, axis, [(i, i ^ bit) for i in range(ways)])]
    dot_general x20 -> x4, matrix products: 128 us -> 9.93 us  [the longest x2 8.28 us: modulation(): jnp.dot(time_rows, w_ada[:, first:last], preferred_element_type=f32)]
    pallas_call x0 -> x7, Pallas kernels: none -> 112 us  [the longest x1 51.6 us: mid_block(): pl.pallas_call(functools.partial(mid_kernel, (seq_ways, heads_local, utts...]
    psum x2 -> x0, waiting for transfers between devices: 79.3 us -> none  [the longest x1 79.3 us: reduce_grad(): return lax.psum(shard, 'batch').astype(jnp.float32)]
    ppermute x0 -> x60, starting transfers between devices: none -> 73.6 us  [sum_exchange(): return lax.ppermute(value, axis, [(i, i ^ bit) for i in range(ways)])]
    psum x2 -> x0, blocking collectives: 49.2 us -> none  [the longest x1 40 us: shards(): lax.psum(jnp.sum(loss_mask[0].astype(jnp.float32)), ('batch', 'seq'))]
    all_to_all x2 -> x1, blocking collectives: 62.9 us -> 19.5 us  [shards(): grad_heads = [exchange(g) for g in grad_att]]
  transfers between devices with their start and end apart: 13 -> 67, of which waited for: 7 -> 39; matrix products, arithmetic and copies ran while one was open for 10% -> 11% of each run, Pallas kernels for 13% -> 23%
where the time goes in v2:
time: 716 us; the launch traced here: 708 us
  waiting for transfers between devices  253 us (35%)
  Pallas kernels  226 us (32%)
  starting transfers between devices  104 us (15%)
  local copies, waits for them, and re-layouts  49.5 us (7%)
  other arithmetic  42.2 us (6%)
  blocking collectives  19.5 us (3%)
  matrix products  9.93 us (1%)
    ppermute x60, waiting for transfers between devices, sum_exchange(): return lax.ppermute(value, axis, [(i, i ^ bit) for i in range(ways)])  203 us
    ppermute x60, starting transfers between devices, sum_exchange(): return lax.ppermute(value, axis, [(i, i ^ bit) for i in range(ways)])  73.6 us
    pallas_call x2, Pallas kernels, attend_back(): pl.pallas_call(functools.partial(bwd_kernel, utts), out_shape=jax.ShapeDt...  63.8 us
    pallas_call x1, Pallas kernels, mid_block(): pl.pallas_call(functools.partial(mid_kernel, (seq_ways, heads_local, utts...  51.6 us
    pallas_call x2, Pallas kernels, attend(): pl.pallas_call(functools.partial(fwd_kernel, utts), out_shape=(jax.ShapeD...  49.8 us
    all_to_all x2, waiting for transfers between devices, shards(): received.append(exchange(packed))  43.8 us
    pallas_call x2, Pallas kernels, back_block(): pl.pallas_call(functools.partial(back_kernel, utts, seq_ways, acc is None...  24.2 us
    convert_element_type x24, other arithmetic, add_pair(): (left.astype(jnp.float32) + right.astype(jnp.float32)).astype(jnp.bfloat16)  22.2 us
  transfers between devices with their start and end apart: 67, of which 39 were waited for; matrix products, arithmetic and copies ran while one was open for 11% of the time, Pallas kernels for 23%

profile of v2, /device:TPU:0, one launch (start us, length us, event | category | flops | bytes accessed | tf_op | source)
XLA Modules:
  0.0 707.9 jit_solution(8182820756141628526)
XLA Ops:
  7.3 8.0 %head_block.1 = (f32[512,1024]{1,0:T(8,128)}, bf16[2048,512]{1,0:T(8,128)(2,1)}, bf16[1024,512]{1,0:T(8,128)(2,1)S(1)}, bf16[512,1024]{1,0:T(8,128)(2,1)S(1)}) custom-call(s32[8]{0:T(128)S(1)} %bitcast.257, s32[2]{0:T(128)S(1)} %pad_add_fusion.ids_ref, s32[8]{0:T(128)S(1)} %bitcast.263, bf16[512,1024]{1,0:T(8,128)(2,1)S(1)} %bitcast.264, ...), custom_call_target="tpu_custom_call" | custom-call | flops 2147483648 | bytes 10485760 | tf_op jit(solution)/shard_map/head_block/pallas_call | solution.py:670
  30.3 6.8 qkv_block.3
  37.1 31.1 %all-to-all-done.qkv_ref = bf16[8,192,512]{2,1,0:T(8,128)(2,1)S(1)} async-done(((bf16[8,192,512]{2,1,0:T(8,128)(2,1)}), bf16[8,192,512]{2,1,0:T(8,128)(2,1)S(1)}, u32[]{:S(2)}, u32[]{:S(2)}) %all-to-all-start) | async-done | bytes 1572896 | tf_op jit(solution)/shard_map/all_to_all | solution.py:1068
  72.9 25.0 %attend.2 = (bf16[8,64,512]{2,1,0:T(8,128)(2,1)}, f32[8,1,512]{2,1,0:T(1,128)}) custom-call(s32[8]{0:T(128)} %bitcast.250, bf16[8,192,512]{2,1,0:T(8,128)(2,1)} %copy-done.14, s32[8,1,512]{2,1,0:T(1,128)} %bitcast.321), custom_call_target="tpu_custom_call" | custom-call | tf_op jit(solution)/shard_map/attend/pallas_call | solution.py:131
  97.9 12.8 %all-to-all-done.2.qkv_ref = bf16[8,192,512]{2,1,0:T(8,128)(2,1)S(1)} async-done(((bf16[8,192,512]{2,1,0:T(8,128)(2,1)}), bf16[8,192,512]{2,1,0:T(8,128)(2,1)S(1)}, u32[]{:S(2)}, u32[]{:S(2)}) %all-to-all-start.2) | async-done | bytes 1572896 | tf_op jit(solution)/shard_map/all_to_all | solution.py:1068
  119.3 24.8 %attend.3 = (bf16[8,64,512]{2,1,0:T(8,128)(2,1)}, f32[8,1,512]{2,1,0:T(1,128)}) custom-call(s32[8]{0:T(128)} %bitcast.251, bf16[8,192,512]{2,1,0:T(8,128)(2,1)} %copy-done.13, s32[8,1,512]{2,1,0:T(1,128)} %bitcast.322), custom_call_target="tpu_custom_call" | custom-call | tf_op jit(solution)/shard_map/attend/pallas_call | solution.py:131
  151.8 12.0 %collective-permute-done.2 = f32[8,128]{1,0:T(8,128)S(1)} collective-permute-done((f32[8,128]{1,0:T(8,128)S(1)}, f32[8,128]{1,0:T(8,128)S(1)}, u32[]{:S(2)}, u32[]{:S(2)}) %collective-permute-start.2) | collective-permute-done | bytes 4128 | tf_op jit(solution)/shard_map/ppermute | solution.py:954
  178.5 51.6 %mid_block.1 = (bf16[512,1024]{1,0:T(8,128)(2,1)}, f32[512,1024]{1,0:T(8,128)}, f32[32,6144]{1,0:T(8,128)}, f32[8,4096]{1,0:T(8,128)}, bf16[8,64,512]{2,1,0:T(8,...) custom-call(s32[8]{0:T(128)} %bitcast.252, ...), custom_call_target="tpu_custom_call" | custom-call | flops 28991029248 | bytes 41943040 | tf_op jit(solution)/shard_map/mid_block/pallas_call | solution.py:541
  230.1 19.5 %all_to_all.40.do_ref = bf16[8,64,512]{2,1,0:T(8,128)(2,1)} all-to-all(bf16[8,64,512]{2,1,0:T(8,128)(2,1)} %get-tuple-element.52), channel_id=1, replica_groups=mesh['batch'=4,'seq'=8] {'seq'}, dimensions={0} | all-to-all | bytes 1048576 | tf_op jit(solution)/shard_map/all_to_all | solution.py:1104
  253.5 31.9 %attend_back.3 = bf16[8,192,512]{2,1,0:T(8,128)(2,1)} custom-call(s32[8]{0:T(128)} %bitcast.253, bf16[8,192,512]{2,1,0:T(8,128)(2,1)} %copy-done.14, s32[8,1,512]{2,1,0:T(1,128)} %bitcast.323, bf16[8,64,512]{2,1,0:T(8,128)(2,1)} %get-tuple-element.45.o_ref, bf16[8,64,512]{2,1,0:T(8,128)(2,1)} %all_to_all.40.do_ref, f32[8,1,512]{2,1,0:T(1,128)} %get-tuple-element.53.lse_ref), custom_call_target="tpu_custom_call" | custom-call | tf_op jit(solution)/shard_map/attend_back/pallas_call | solution.py:252
  290.5 31.9 %attend_back.2 = bf16[8,192,512]{2,1,0:T(8,128)(2,1)} custom-call(s32[8]{0:T(128)} %bitcast.254, bf16[8,192,512]{2,1,0:T(8,128)(2,1)} %copy-done.13, s32[8,1,512]{2,1,0:T(1,128)} %bitcast.324, bf16[8,64,512]{2,1,0:T(8,128)(2,1)} %get-tuple-element.46.o_ref, bf16[8,64,512]{2,1,0:T(8,128)(2,1)} %copy-done.21, f32[8,1,512]{2,1,0:T(1,128)} %get-tuple-element.50.lse_ref), custom_call_target="tpu_custom_call" | custom-call | tf_op jit(solution)/shard_map/attend_back/pallas_call | solution.py:252
  338.9 24.3 %collective-permute-done.25 = f32[19,2048]{1,0:T(8,128)S(1)} collective-permute-done((f32[19,2048]{1,0:T(8,128)S(1)}, f32[19,2048]{1,0:T(8,128)S(1)}, u32[]{:S(2)}, u32[]{:S(2)}) %collective-permute-start.25) | collective-permute-done | bytes 155680 | tf_op jit(solution)/shard_map/ppermute | solution.py:954
  367.8 11.0 %collective-permute-done.26 = f32[19,2048]{1,0:T(8,128)S(1)} collective-permute-done((f32[19,2048]{1,0:T(8,128)S(1)}, f32[19,2048]{1,0:T(8,128)S(1)}, u32[]{:S(2)}, u32[]{:S(2)}) %collective-permute-start.26) | collective-permute-done | bytes 155680 | tf_op jit(solution)/shard_map/ppermute | solution.py:954
  391.1 11.6 %back_block.2 = (f32[1024,512]{1,0:T(8,128)}, f32[3,8,512]{2,1,0:T(8,128)}, bf16[8,4,16,1536]{3,2,1,0:T(8,128)(2,1)}, bf16[8,4,16,1536]{3,2,1,0:T(8,128)(2,1)}) custom-call(s32[8]{0:T(128)} %bitcast.255, s32[2]{0:T(128)} %copy-done.4, s32[8]{0:T(128)} %bitcast.261, bf16[8,192,512]{2,1,0:T(8,128)(2,1)} %copy-done.25, bf16[1024,512]{1,0:T(8,128)(2,1)} %copy-done.11, ...), custom_call_target="tpu_custom_call" | custom-call | flops 3221225472 | bytes 10485760 | tf_op jit(solution)/shard_map/back_block/pallas_call | solution.py:818
  402.7 12.5 %back_block.3 = (f32[1024,512]{1,0:T(8,128)}, f32[3,8,512]{2,1,0:T(8,128)}, bf16[8,4,16,1536]{3,2,1,0:T(8,128)(2,1)}, bf16[8,4,16,1536]{3,2,1,0:T(8,128)(2,1)}) custom-call(s32[8]{0:T(128)} %bitcast.256, s32[2]{0:T(128)} %copy-done.4, s32[8]{0:T(128)} %bitcast.262, bf16[8,192,512]{2,1,0:T(8,128)(2,1)} %all-to-all-done.5.grad_ref, ...), custom_call_target="tpu_custom_call" | custom-call | flops 3221225472 | bytes 10485760 | tf_op jit(solution)/shard_map/back_block/pallas_call | solution.py:818
  415.3 15.1 %tail_block.1 = (f32[32,3072]{1,0:T(8,128)S(1)}, f32[512,1024]{1,0:T(8,128)}, f32[512,1024]{1,0:T(8,128)}, bf16[8,4,32,1024]{3,2,1,0:T(8,128)(2,1)S(1)}, bf16[8,4,32,1024]{3,2,1,0:T(8,128)(2,1)S(1)}) custom-call(s32[8]{0:T(128)S(1)} %bitcast.258, s32[2]{0:T(128)S(1)} %copy-done.5, f32[1024,512]{1,0:T(8,128)} %get-tuple-element.55.acc_ref, ...), custom_call_target="tpu_custom_call" | custom-call | flops 4294967296 | bytes 15728640 | tf_op jit(solution)/shard_map/tail_block/pallas_call | solution.py:930
  468.1 8.5 %collective-permute-done.33 = bf16[2,4,16,1536]{3,2,1,0:T(8,128)(2,1)S(1)} collective-permute-done((bf16[2,4,16,1536]{3,2,1,0:T(8,128)(2,1)S(1)}, bf16[2,4,16,1536]{3,2,1,0:T(8,128)(2,1)S(1)}, u32[]{:S(2)}, u32[]{:S(2)}) %collective-permute-start.33) | collective-permute-done | bytes 393248 | tf_op jit(solution)/shard_map/ppermute | solution.py:954
  528.6 7.1 %add_convert_fusion = bf16[8,4,144,1024]{3,2,1,0:T(8,128)(2,1)S(1)} fusion(bf16[8,4,144,1024]{3,2,1,0:T(8,128)(2,1)} %collective-permute-done.50, bf16[8,4,144,1024]{3,2,1,0:T(8,128)(2,1)S(1)} %bitcast.282), kind=kLoop, calls=%fused_computation | loop fusion | flops 18874368 | bytes 28311552 | tf_op jit(solution)/shard_map/convert_element_type | solution.py:958
  552.1 36.1 %collective-permute-done.53 = bf16[2,4,144,1024]{3,2,1,0:T(8,128)(2,1)S(1)} collective-permute-done((bf16[2,4,144,1024]{3,2,1,0:T(8,128)(2,1)S(1)}, bf16[2,4,144,1024]{3,2,1,0:T(8,128)(2,1)S(1)}, u32[]{:S(2)}, u32[]{:S(2)}) %collective-permute-start.53) | collective-permute-done | bytes 2359328 | tf_op jit(solution)/shard_map/ppermute | solution.py:954
  590.5 9.6 %collective-permute-done.51 = bf16[2,4,144,1024]{3,2,1,0:T(8,128)(2,1)S(1)} collective-permute-done((bf16[2,4,144,1024]{3,2,1,0:T(8,128)(2,1)S(1)}, bf16[2,4,144,1024]{3,2,1,0:T(8,128)(2,1)S(1)}, u32[]{:S(2)}, u32[]{:S(2)}) %collective-permute-start.51) | collective-permute-done | bytes 2359328 | tf_op jit(solution)/shard_map/ppermute | solution.py:954
  611.8 11.3 %collective-permute-done.7 = bf16[4,32,1024]{2,1,0:T(8,128)(2,1)} collective-permute-done((bf16[4,32,1024]{2,1,0:T(8,128)(2,1)}, bf16[4,32,1024]{2,1,0:T(8,128)(2,1)}, u32[]{:S(2)}, u32[]{:S(2)}) %collective-permute-start.7) | collective-permute-done | bytes 262176 | tf_op jit(solution)/shard_map/ppermute | solution.py:954
  637.2 12.0 %collective-permute-done.11 = bf16[2,1,32,1024]{3,2,1,0:T(8,128)(2,1)} collective-permute-done((bf16[2,1,32,1024]{3,2,1,0:T(8,128)(2,1)}, bf16[2,1,32,1024]{3,2,1,0:T(8,128)(2,1)}, u32[]{:S(2)}, u32[]{:S(2)}) %collective-permute-start.11) | collective-permute-done | bytes 131104 | tf_op jit(solution)/shard_map/ppermute | solution.py:954
  666.6 13.9 %collective-permute-done.56 = bf16[2,1,144,1024]{3,2,1,0:T(8,128)(2,1)S(1)} collective-permute-done((bf16[2,1,144,1024]{3,2,1,0:T(8,128)(2,1)S(1)}, bf16[2,1,144,1024]{3,2,1,0:T(8,128)(2,1)S(1)}, u32[]{:S(2)}, u32[]{:S(2)}) %collective-permute-start.56) | collective-permute-done | bytes 589856 | tf_op jit(solution)/shard_map/ppermute | solution.py:954
  691.7 6.8 collective-permute-done.59
  (382 shorter events, 269.6 us)
Async XLA Ops:
  24.0 44.2 %all-to-all-start = ((bf16[8,192,512]{2,1,0:T(8,128)(2,1)}), bf16[8,192,512]{2,1,0:T(8,128)(2,1)S(1)}, u32[]{:S(2)}, u32[]{:S(2)}) async-start(bf16[8,192,512]{2,1,0:T(8,128)(2,1)} %qkv_block.2), calls=%async_computation | async-start | bytes 3145728 | tf_op jit(solution)/shard_map/all_to_all | solution.py:1068
  69.3 41.3 %all-to-all-start.2 = ((bf16[8,192,512]{2,1,0:T(8,128)(2,1)}), bf16[8,192,512]{2,1,0:T(8,128)(2,1)S(1)}, u32[]{:S(2)}, u32[]{:S(2)}) async-start(bf16[8,192,512]{2,1,0:T(8,128)(2,1)} %qkv_block.3), calls=%async_computation.2 | async-start | bytes 3145728 | tf_op jit(solution)/shard_map/all_to_all | solution.py:1068
  110.6 33.5 %all-to-all-start.1 = ((bf16[8,64,512]{2,1,0:T(8,128)(2,1)}), bf16[8,64,512]{2,1,0:T(8,128)(2,1)S(1)}, u32[]{:S(2)}, u32[]{:S(2)}) async-start(bf16[8,64,512]{2,1,0:T(8,128)(2,1)} %get-tuple-element.45.o_ref), calls=%async_computation.1 | async-start | bytes 1048576 | tf_op jit(solution)/shard_map/all_to_all | solution.py:1083
  117.3 30.9 %collective-permute-start.1 = (f32[8,128]{1,0:T(8,128)S(1)}, f32[8,128]{1,0:T(8,128)S(1)}, u32[]{:S(2)}, u32[]{:S(2)}) collective-permute-start(f32[8,128]{1,0:T(8,128)S(1)} %broadcast_add_fusion), channel_id=1, source_target_pairs={{0,2},{1,3},{2,0},{3,1},{4,6},{5,7},{6,4},{7,5},{8,10},{9,11},{10,... | collective-permute-start | bytes 12296 | tf_op jit(solution)/shard_map/ppermute | solution.py:954
  144.1 34.4 %all-to-all-start.3 = ((bf16[8,64,512]{2,1,0:T(8,128)(2,1)}), bf16[8,64,512]{2,1,0:T(8,128)(2,1)}, u32[]{:S(2)}, u32[]{:S(2)}) async-start(bf16[8,64,512]{2,1,0:T(8,128)(2,1)} %get-tuple-element.46.o_ref), calls=%async_computation.3 | async-start | bytes 1048576 | tf_op jit(solution)/shard_map/all_to_all | solution.py:1083
  249.6 35.8 %all-to-all-start.4 = ((bf16[8,64,512]{2,1,0:T(8,128)(2,1)}), bf16[8,64,512]{2,1,0:T(8,128)(2,1)S(1)}, u32[]{:S(2)}, u32[]{:S(2)}) async-start(bf16[8,64,512]{2,1,0:T(8,128)(2,1)} %get-tuple-element.49), calls=%async_computation.4 | async-start | bytes 1048576 | tf_op jit(solution)/shard_map/all_to_all | solution.py:1104
  285.4 42.9 %all-to-all-start.7 = ((bf16[8,192,512]{2,1,0:T(8,128)(2,1)}), bf16[8,192,512]{2,1,0:T(8,128)(2,1)S(1)}, u32[]{:S(2)}, u32[]{:S(2)}) async-start(bf16[8,192,512]{2,1,0:T(8,128)(2,1)} %attend_back.3), calls=%async_computation.7 | async-start | bytes 3145728 | tf_op jit(solution)/shard_map/all_to_all | solution.py:1114
  328.3 74.4 %all-to-all-start.5 = ((bf16[8,192,512]{2,1,0:T(8,128)(2,1)}), bf16[8,192,512]{2,1,0:T(8,128)(2,1)}, u32[]{:S(2)}, u32[]{:S(2)}) async-start(bf16[8,192,512]{2,1,0:T(8,128)(2,1)} %attend_back.2), calls=%async_computation.5 | async-start | bytes 3145728 | tf_op jit(solution)/shard_map/all_to_all | solution.py:1114
  336.9 26.2 %collective-permute-start.25 = (f32[19,2048]{1,0:T(8,128)S(1)}, f32[19,2048]{1,0:T(8,128)S(1)}, u32[]{:S(2)}, u32[]{:S(2)}) collective-permute-start(f32[19,2048]{1,0:T(8,128)S(1)} %add.299), channel_id=1, source_target_pairs={{0,2},{1,3},{2,0},{3,1},{4,6},{5,7},{6,4},{7,5},{8,10},{9,11},{10,... | collective-permute-start | bytes 466952 | tf_op jit(solution)/shard_map/ppermute | solution.py:954
  382.3 58.7 %collective-permute-start.21 = (bf16[8,1024]{1,0:T(8,128)(2,1)S(1)}, bf16[8,1024]{1,0:T(8,128)(2,1)S(1)}, u32[]{:S(2)}, u32[]{:S(2)}) collective-permute-start(bf16[8,1024]{1,0:T(8,128)(2,1)S(1)} %fusion.70), channel_id=1, source_target_pairs={{0,8},{8,0},{16,24},{24,16},{1,9},{9,1},{17,25},{25,17},{2,10},{10... | collective-permute-start | bytes 49160 | tf_op jit(solution)/shard_map/ppermute | solution.py:954
  383.4 57.7 %collective-permute-start.22 = (bf16[8,1024]{1,0:T(8,128)(2,1)S(1)}, bf16[8,1024]{1,0:T(8,128)(2,1)S(1)}, u32[]{:S(2)}, u32[]{:S(2)}) collective-permute-start(bf16[8,1024]{1,0:T(8,128)(2,1)S(1)} %fusion.70), channel_id=1, source_target_pairs={{0,16},{8,24},{16,0},{24,8},{1,17},{9,25},{17,1},{25,9},{2,18},{10... | collective-permute-start | bytes 49160 | tf_op jit(solution)/shard_map/ppermute | solution.py:954
  386.7 54.4 %collective-permute-start.23 = (bf16[8,1024]{1,0:T(8,128)(2,1)S(1)}, bf16[8,1024]{1,0:T(8,128)(2,1)S(1)}, u32[]{:S(2)}, u32[]{:S(2)}) collective-permute-start(bf16[8,1024]{1,0:T(8,128)(2,1)S(1)} %fusion.70), channel_id=1, source_target_pairs={{0,24},{8,16},{16,8},{24,0},{1,25},{9,17},{17,9},{25,1},{2,26},{10... | collective-permute-start | bytes 49160 | tf_op jit(solution)/shard_map/ppermute | solution.py:954
  390.1 138.4 %collective-permute-start.50 = (bf16[8,4,144,1024]{3,2,1,0:T(8,128)(2,1)}, bf16[8,4,144,1024]{3,2,1,0:T(8,128)(2,1)}, u32[]{:S(2)}, u32[]{:S(2)}) collective-permute-start(bf16[8,4,144,1024]{3,2,1,0:T(8,128)(2,1)} %get-tuple-element.72), channel_id=1, source_target_pairs={{0,1},{1,0},{2,3},{3,2},{4,5},{5,4},{6,7},{7,6},{8,9},{9,8},{10,11... | collective-permute-start | bytes 28311560 | tf_op jit(solution)/shard_map/ppermute | solution.py:954
  444.0 19.8 %collective-permute-start.30 = (bf16[8,4,16,1536]{3,2,1,0:T(8,128)(2,1)}, bf16[8,4,16,1536]{3,2,1,0:T(8,128)(2,1)S(1)}, u32[]{:S(2)}, u32[]{:S(2)}) collective-permute-start(bf16[8,4,16,1536]{3,2,1,0:T(8,128)(2,1)} %get-tuple-element.68), channel_id=1, source_target_pairs={{0,1},{1,0},{2,3},{3,2},{4,5},{5,4},{6,7},{7,6},{8,9},{9,8},{10,11... | collective-permute-start | bytes 4718600 | tf_op jit(solution)/shard_map/ppermute | solution.py:954
  457.4 31.8 %collective-permute-start.5 = (bf16[8,4,32,1024]{3,2,1,0:T(8,128)(2,1)S(1)}, bf16[8,4,32,1024]{3,2,1,0:T(8,128)(2,1)S(1)}, u32[]{:S(2)}, u32[]{:S(2)}) collective-permute-start(bf16[8,4,32,1024]{3,2,1,0:T(8,128)(2,1)S(1)} %copy-done.7), channel_id=1, source_target_pairs={{0,1},{1,0},{2,3},{3,2},{4,5},{5,4},{6,7},{7,6},{8,9},{9,8},{10,11... | collective-permute-start | bytes 6291464 | tf_op jit(solution)/shard_map/ppermute | solution.py:954
  493.9 54.7 %collective-permute-start.8 = (bf16[2,4,32,1024]{3,2,1,0:T(8,128)(2,1)}, bf16[2,4,32,1024]{3,2,1,0:T(8,128)(2,1)}, u32[]{:S(2)}, u32[]{:S(2)}) collective-permute-start(bf16[2,4,32,1024]{3,2,1,0:T(8,128)(2,1)} %dynamic-slice_bitcast_fusion.4), channel_id=1, source_target_pairs={{0,16},{8,24},{16,0},{24,8},{1,17},{9,25},{17,1},{25,9},{2,18},{10... | collective-permute-start | bytes 1572872 | tf_op jit(solution)/shard_map/ppermute | solution.py:954
  494.3 56.6 %collective-permute-start.6 = (bf16[2,4,32,1024]{3,2,1,0:T(8,128)(2,1)}, bf16[2,4,32,1024]{3,2,1,0:T(8,128)(2,1)}, u32[]{:S(2)}, u32[]{:S(2)}) collective-permute-start(bf16[2,4,32,1024]{3,2,1,0:T(8,128)(2,1)} %dynamic-slice_bitcast_fusion.5), channel_id=1, source_target_pairs={{0,8},{8,0},{16,24},{24,16},{1,9},{9,1},{17,25},{25,17},{2,10},{10... | collective-permute-start | bytes 1572872 | tf_op jit(solution)/shard_map/ppermute | solution.py:954
  542.7 45.5 %collective-permute-start.53 = (bf16[2,4,144,1024]{3,2,1,0:T(8,128)(2,1)S(1)}, bf16[2,4,144,1024]{3,2,1,0:T(8,128)(2,1)S(1)}, u32[]{:S(2)}, u32[]{:S(2)}) collective-permute-start(bf16[2,4,144,1024]{3,2,1,0:T(8,128)(2,1)S(1)} %dynamic-slice_bitcast_fusion), channel_id=1, source_target_pairs={{0,16},{8,24},{16,0},{24,8},{1,17},{9,25},{17,1},{25,9},{2,18},{10... | collective-permute-start | bytes 7077896 | tf_op jit(solution)/shard_map/ppermute | solution.py:954
  545.9 54.3 %collective-permute-start.51 = (bf16[2,4,144,1024]{3,2,1,0:T(8,128)(2,1)S(1)}, bf16[2,4,144,1024]{3,2,1,0:T(8,128)(2,1)S(1)}, u32[]{:S(2)}, u32[]{:S(2)}) collective-permute-start(bf16[2,4,144,1024]{3,2,1,0:T(8,128)(2,1)S(1)} %dynamic-slice_bitcast_fusion.1), channel_id=1, source_target_pairs={{0,8},{8,0},{16,24},{24,16},{1,9},{9,1},{17,25},{25,17},{2,10},{10... | collective-permute-start | bytes 7077896 | tf_op jit(solution)/shard_map/ppermute | solution.py:954
  550.7 60.1 %collective-permute-start.9 = (bf16[4,32,1024]{2,1,0:T(8,128)(2,1)}, bf16[4,32,1024]{2,1,0:T(8,128)(2,1)}, u32[]{:S(2)}, u32[]{:S(2)}) collective-permute-start(bf16[4,32,1024]{2,1,0:T(8,128)(2,1)} %dynamic-slice_bitcast_fusion.10), channel_id=1, source_target_pairs={{0,8},{8,0},{16,24},{24,16},{1,9},{9,1},{17,25},{25,17},{2,10},{10... | collective-permute-start | bytes 786440 | tf_op jit(solution)/shard_map/ppermute | solution.py:954
  590.5 33.8 %collective-permute-start.54 = (bf16[4,144,1024]{2,1,0:T(8,128)(2,1)}, bf16[4,144,1024]{2,1,0:T(8,128)(2,1)}, u32[]{:S(2)}, u32[]{:S(2)}) collective-permute-start(bf16[4,144,1024]{2,1,0:T(8,128)(2,1)} %dynamic-slice_bitcast_fusion.2), channel_id=1, source_target_pairs={{0,8},{8,0},{16,24},{24,16},{1,9},{9,1},{17,25},{25,17},{2,10},{10... | collective-permute-start | bytes 3538952 | tf_op jit(solution)/shard_map/ppermute | solution.py:954
  603.8 22.4 %collective-permute-start.52 = (bf16[4,144,1024]{2,1,0:T(8,128)(2,1)}, bf16[4,144,1024]{2,1,0:T(8,128)(2,1)}, u32[]{:S(2)}, u32[]{:S(2)}) collective-permute-start(bf16[4,144,1024]{2,1,0:T(8,128)(2,1)} %dynamic-slice_bitcast_fusion.3), channel_id=1, source_target_pairs={{0,16},{8,24},{16,0},{24,8},{1,17},{9,25},{17,1},{25,9},{2,18},{10... | collective-permute-start | bytes 3538952 | tf_op jit(solution)/shard_map/ppermute | solution.py:954
  629.1 32.0 %collective-permute-start.55 = (bf16[2,2,144,1024]{3,2,1,0:T(8,128)(2,1)}, bf16[2,2,144,1024]{3,2,1,0:T(8,128)(2,1)}, u32[]{:S(2)}, u32[]{:S(2)}) collective-permute-start(bf16[2,2,144,1024]{3,2,1,0:T(8,128)(2,1)} %fusion.16), channel_id=1, source_target_pairs={{0,2},{1,3},{2,0},{3,1},{4,6},{5,7},{6,4},{7,5},{8,10},{9,11},{10,... | collective-permute-start | bytes 3538952 | tf_op jit(solution)/shard_map/ppermute | solution.py:954
  662.9 17.6 %collective-permute-start.56 = (bf16[2,1,144,1024]{3,2,1,0:T(8,128)(2,1)S(1)}, bf16[2,1,144,1024]{3,2,1,0:T(8,128)(2,1)S(1)}, u32[]{:S(2)}, u32[]{:S(2)}) collective-permute-start(bf16[2,1,144,1024]{3,2,1,0:T(8,128)(2,1)S(1)} %constant_dynamic-slice_fusion), channel_id=1, source_target_pairs={{0,4},{1,5},{2,6},{3,7},{4,0},{5,1},{6,2},{7,3},{8,12},{9,13},{10,... | collective-permute-start | bytes 1769480 | tf_op jit(solution)/shard_map/ppermute | solution.py:954
  (84 other events, 982.2 us)

commit v3 on v2

--- a/solution.py
+++ b/solution.py
@@ -146,6 +146,9 @@
                 pltpu.VMEM((total, 128), jnp.bfloat16),
                 pltpu.VMEM((total // BK, DH + 16, BK), jnp.bfloat16),
             ],
+        ),
+        cost_estimate=pl.CostEstimate(
+            flops=total * total * 1200, bytes_accessed=8 * total * DH, transcendentals=0
         ),
         name="attend",
     )(lengths, qkv, ok)
@@ -265,6 +268,9 @@
                 pltpu.VMEM((total // BK, DH, BK), jnp.float32),
             ],
         ),
+        cost_estimate=pl.CostEstimate(
+            flops=total * total * 1500, bytes_accessed=16 * total * DH, transcendentals=0
+        ),
         name="attend_back",
     )(lengths, qkv, ok, out, grad, lse)
 
@@ -309,7 +315,6 @@
     dims,
     lengths_ref,
     ids_ref,
-    scale_ref,
     *refs,
 ):
     seq_ways, heads_local, utts = dims
@@ -366,7 +371,7 @@
 
     def grad_out():
         loss = cols[:, 48:49].astype(f32)
-        return cot_ref[...].astype(f32) * (loss * scale_ref[0])
+        return cot_ref[...].astype(f32) * loss
 
     @pl.when(step == 0)
     def _():
@@ -511,7 +516,7 @@
 
 
 def mid_block(
-    lengths, ids, scale, att, hidden, mods, cot, loss, w_out, b_out, w_up, b_up, w_down, b_down, parts
+    lengths, ids, att, hidden, mods, cot, loss, w_out, b_out, w_up, b_up, w_down, b_down, parts
 ):
     frames, width = hidden.shape
     heads_local = len(att)
@@ -542,7 +547,7 @@
         functools.partial(mid_kernel, (seq_ways, heads_local, utts)),
         out_shape=out_shape,
         grid_spec=pltpu.PrefetchScalarGridSpec(
-            num_scalar_prefetch=3,
+            num_scalar_prefetch=2,
             grid=(steps,),
             in_specs=[whole(a.shape) for a in ins]
             + [
@@ -575,7 +580,7 @@
             transcendentals=frames * ff,
         ),
         name="mid_block",
-    )(lengths, ids, scale, *ins, w_up, b_up, w_down, b_down)
+    )(lengths, ids, *ins, w_up, b_up, w_down, b_down)
 
 
 def segment_rows(lengths_ref, drop_ref, utts, base, width):
@@ -847,6 +852,7 @@
     seq_ways,
     lengths_ref,
     ids_ref,
+    scale_ref,
     acc_ref,
     hidden_ref,
     after_ref,
@@ -902,14 +908,14 @@
 
     @pl.when(step == 0)
     def _():
-        grad_a_ref[...] = joined
+        grad_a_ref[...] = joined * scale_ref[0]
 
     @pl.when(step == 1)
     def _():
-        grad_b_ref[...] = joined
-
-
-def tail_block(lengths, ids, acc, hidden, after, mods, joinedT, w_skip, seq_ways, parts):
+        grad_b_ref[...] = joined * scale_ref[0]
+
+
+def tail_block(lengths, ids, acc, hidden, after, mods, joinedT, w_skip, scale, seq_ways, parts):
     frames, width = hidden.shape
     utts = lengths.shape[0]
     f32, bf16 = jnp.float32, jnp.bfloat16
@@ -931,7 +937,7 @@
         functools.partial(tail_kernel, utts, seq_ways),
         out_shape=out_shape,
         grid_spec=pltpu.PrefetchScalarGridSpec(
-            num_scalar_prefetch=2,
+            num_scalar_prefetch=3,
             grid=(2,),
             in_specs=[whole(a.shape) for a in (acc, hidden, after, mods)]
             + [
@@ -946,7 +952,7 @@
             flops=8 * frames * width * width, bytes_accessed=30 * frames * width, transcendentals=0
         ),
         name="tail_block",
-    )(lengths, ids, acc, hidden, after, mods, joinedT, w_skip)
+    )(lengths, ids, scale, acc, hidden, after, mods, joinedT, w_skip)
 
 
 def sum_exchange(value, axis, bit):
@@ -966,7 +972,7 @@
     return [1 << i for i in range(ways.bit_length() - 1)]
 
 
-def reduce_blocks(keep, send):
+def reduce_stages(keep, send):
     seq_ways, batch_ways = lax.axis_size("seq"), lax.axis_size("batch")
     seq_rank, batch_rank = lax.axis_index("seq"), lax.axis_index("batch")
     side = 1 << ((batch_ways.bit_length() - 1) // 2)
@@ -974,35 +980,54 @@
     x = lax.rem(batch_rank, 2)
     y = lax.rem(batch_rank // side, 2)
     _, z_ways, rows, width = keep.shape
-    total = add_pair(keep, sum_exchange(send, "seq", 1)).reshape(2, 2, 2, z_ways, rows, width)
-    first = []
-    for block, mine, bit in ((total[0], x, x_bit), (total[1], y, y_bit)):
-        got = sum_exchange(pick(block, 1 - mine), "batch", bit)
-        first.append(add_pair(pick(block, mine), got))
-    second = []
-    for block, mine, bit in ((first[0], y, y_bit), (first[1], x, x_bit)):
-        got = sum_exchange(pick(block, 1 - mine), "batch", bit)
-        second.append(add_pair(pick(block, mine), got))
-    block = jnp.stack(second)
+    got = sum_exchange(send, "seq", 1)
+    total = add_pair(keep, got).reshape(2, 2, 2, z_ways, rows, width)
+    blocks = [total[0], total[1]]
+    for turn in ((x, x_bit, y, y_bit), (y, y_bit, x, x_bit)):
+        sends = [pick(blocks[0], 1 - turn[0]), pick(blocks[1], 1 - turn[2])]
+        sends = follow(sends, (yield sends))
+        got = [sum_exchange(sends[0], "batch", turn[1]), sum_exchange(sends[1], "batch", turn[3])]
+        blocks = [
+            add_pair(pick(blocks[0], turn[0]), got[0]),
+            add_pair(pick(blocks[1], turn[2]), got[1]),
+        ]
+    block = jnp.stack(blocks)
     for bit in axis_bits(batch_ways):
         if bit not in (x_bit, y_bit):
             block = add_pair(block, sum_exchange(block, "batch", bit))
     z = seq_rank // 2
-    for i, bit in enumerate(axis_bits(z_ways)):
+    for bit in axis_bits(z_ways):
         mine = lax.rem(z // bit, 2)
         block = block.reshape(2, block.shape[1] // 2, 2, rows, width)
-        got = sum_exchange(pick(block, 1 - mine, 2), "seq", 2 * bit)
-        block = add_pair(pick(block, mine, 2), got)
+        away = pick(block, 1 - mine, 2)
+        (away,) = follow([away], (yield [away]))
+        block = add_pair(pick(block, mine, 2), sum_exchange(away, "seq", 2 * bit))
     block = block.reshape(2, rows, width)
+    (block,) = follow([block], (yield [block]))
     got_x = sum_exchange(block, "batch", x_bit)
     got_y = sum_exchange(block, "batch", y_bit)
     got_xy = sum_exchange(block, "batch", x_bit | y_bit)
     table = jnp.stack([jnp.stack([block, got_y]), jnp.stack([got_x, got_xy])])
     table = jnp.where(x == 1, table[::-1], table)
     table = jnp.where(y == 1, table[:, ::-1], table)
-    return jnp.concatenate(
+    yield jnp.concatenate(
         [table[:, :, 0].reshape(4, rows, width), jnp.swapaxes(table[:, :, 1], 0, 1).reshape(4, rows, width)]
     ).astype(jnp.float32)
+
+
+def last_stage(stages, token=None):
+    value = stages.send(token)
+    for value in stages:
+        pass
+    return value
+
+
+def follow(values, token):
+    return values if token is None else [after(v, token) for v in values]
+
+
+def after(value, *others):
+    return lax.optimization_barrier((value,) + others)[0]
 
 
 def gather_groups(value):
@@ -1067,24 +1092,31 @@
         packed = qkv_block(lengths_row, ids, drop, na, w_qkv, b_qkv[None], c, seq_ways)
         received.append(exchange(packed))
 
-    count = jnp.sum(loss_mask.astype(f32))
-    count = sum_seq(jnp.full((8, 128), count))
-    for bit in axis_bits(batch_ways):
-        count = count + sum_exchange(count, "batch", bit)
-    scale = (group_frames * batch_ways) / count[0, :1]
     mods_rest = modulation(2 * width, 6 * width)
     time_all = jnp.concatenate(gather_groups(time_act))
-
+    hops = [("seq", bit) for bit in axis_bits(seq_ways)] + [("batch", bit) for bit in axis_bits(batch_ways)]
+    count = jnp.full((8, 128), jnp.sum(loss_mask.astype(f32)))
+
+    def hop(count):
+        if not hops:
+            return count
+        axis, bit = hops.pop(0)
+        return count + sum_exchange(count, axis, bit)
+
+    received[0] = after(received[0], mods_rest, time_all, count)
     head_out, log_totals, returned = [], [], []
     for c in range(heads_local):
         out, log_total = attend(lengths_row, received[c], ok)
         head_out.append(out)
         log_totals.append(log_total)
         returned.append(exchange(out))
+        count = hop(count)
+        if c < heads_local - 1:
+            received[c + 1] = after(received[c + 1], count, out)
+    returned[0] = after(returned[0], count)
     mid = mid_block(
         lengths_row,
         ids,
-        scale,
         returned,
         hidden,
         mods_rest,
@@ -1102,34 +1134,52 @@
     grad_att = mid[4 : 4 + heads_local]
     keep_f, send_f = mid[4 + heads_local :]
     grad_heads = [exchange(g) for g in grad_att]
-    feed = reduce_blocks(keep_f, send_f)
-    early = jnp.concatenate([tables[:utts, : 4 * width].reshape(-1), b_up_grad[0], tables[16, 4 * width :]])
-    early = early.reshape(-1, 2 * width)
-    early = gather_groups(sum_seq(early))
+    feed = reduce_stages(keep_f, send_f)
+    count = hop(count)
 
     acc, part_biases, part_blocks = None, [], []
     grad_local = []
+    ahead = list(next(feed)) + [count]
     for c in range(heads_local):
-        grad = attend_back(lengths_row, received[c], ok, head_out[c], grad_heads[c], log_totals[c])
-        grad_local.append(exchange(grad))
+        grad = attend_back(
+            lengths_row, received[c], ok, head_out[c], after(grad_heads[c], *ahead), log_totals[c]
+        )
+        grad_local.append(exchange(after(grad, *grad_heads[c + 1 :])))
+        count = hop(count)
+        ahead = [grad, count]
+    ahead += list(next(feed))
     for c in range(heads_local):
         acc, bias, keep, send = back_block(
-            lengths_row, ids, drop, grad_local[c], naT, w_qkv, acc, c, PARTS
+            lengths_row, ids, drop, after(grad_local[c], *ahead), naT, w_qkv, acc, c, PARTS
         )
         part_biases.append(bias[:, 0])
-        part_blocks.append(reduce_blocks(keep, send))
+        part_blocks.append(reduce_stages(keep, send))
+        ahead = list(next(feed))
+        for blocks in part_blocks:
+            ahead += list(next(blocks))
+    while hops:
+        count = hop(count)
+    scale = (group_frames * batch_ways) / count[0, :1]
     late_tables, grad_tokens, grad_skip, keep, send = tail_block(
-        lengths_row, ids, acc, hidden, after_grad, mods_a, joinedT, w_skip, seq_ways, PARTS
+        lengths_row, ids, after(acc, *ahead), hidden, after_grad, mods_a, joinedT, w_skip, scale, seq_ways, PARTS
     )
-    skip_blocks = reduce_blocks(keep, send)
+    skip_blocks = reduce_stages(keep, send)
+    next(skip_blocks)
+    feed = last_stage(feed, late_tables)
+    part_blocks = [last_stage(b, late_tables) for b in part_blocks]
+    skip_blocks = last_stage(skip_blocks)
     late = jnp.concatenate(
         [
             late_tables[:utts, : 2 * width].reshape(-1),
+            tables[:utts, : 4 * width].reshape(-1),
             jnp.stack(part_biases, axis=1).reshape(-1),
             late_tables[16, 2 * width :],
+            b_up_grad[0],
+            tables[16, 4 * width :],
         ]
-    ).reshape(-1, 2 * width)
-    late = gather_groups(sum_seq(late))
+    )
+    late = gather_groups(sum_seq(late.reshape(-1, 1024)))
+    late = [g.reshape(-1) * scale for g in late]
 
     ada_rows = width // seq_ways
     own_time = lax.dynamic_slice_in_dim(time_all, seq_rank * ada_rows, ada_rows, axis=1).astype(f32)
@@ -1138,28 +1188,27 @@
         size = vector.shape[0] // seq_ways
         return lax.dynamic_slice_in_dim(vector, seq_rank * size, size)
 
-    def ada_part(groups, tables_count):
-        rows = jnp.concatenate(
-            [g.reshape(-1)[: utts * tables_count * width].reshape(utts, -1) for g in groups]
-        )
-        weight = lax.dot_general(
-            own_time, rows, (((0,), (0,)), ((), ())), precision=lax.Precision.HIGHEST
-        )
-        return weight, jnp.sum(rows, axis=0)
-
-    early_weight, early_bias = ada_part(early, 4)
-    late_weight, late_bias = ada_part(late, 2)
-    grad_w_ada = jnp.concatenate([late_weight, early_weight], axis=1)
-    grad_b_ada = own_slice(jnp.concatenate([late_bias, early_bias]))
-    early_vec = sum(g.reshape(-1)[utts * 4 * width :] for g in early)
-    late_vec = sum(g.reshape(-1)[utts * 2 * width :] for g in late)
+    two, six = 2 * utts * width, 6 * utts * width
+    rows = jnp.concatenate(
+        [
+            jnp.concatenate([g[:two].reshape(utts, -1), g[two:six].reshape(utts, -1)], axis=1)
+            for g in late
+        ]
+    )
+    grad_w_ada = lax.dot_general(
+        own_time, rows, (((0,), (0,)), ((), ())), precision=lax.Precision.HIGHEST
+    )
+    grad_b_ada = own_slice(jnp.sum(rows, axis=0))
+    vector = sum(g[six:] for g in late)
     ff = w_up.shape[1]
-    grad_b_up = own_slice(early_vec[:ff])
-    grad_b_out = own_slice(early_vec[ff : ff + width])
-    grad_b_down = own_slice(early_vec[ff + width :])
-    grad_b_qkv = own_slice(late_vec[: 3 * width])
-    grad_b_skip = own_slice(late_vec[3 * width :])
-
+    grad_b_qkv = own_slice(vector[: 3 * width])
+    grad_b_skip = own_slice(vector[3 * width : 4 * width])
+    grad_b_up = own_slice(vector[4 * width : 4 * width + ff])
+    grad_b_out = own_slice(vector[4 * width + ff : 5 * width + ff])
+    grad_b_down = own_slice(vector[5 * width + ff :])
+
+    feed, skip_blocks = feed * scale, skip_blocks * scale
+    part_blocks = [b * scale for b in part_blocks]
     own = width // seq_ways
     chunks = ff // width
     up_part = chunks * own // PARTS

time: 716 us -> 654 us (0.913)
  waiting for transfers between devices: 253 us -> 149 us
  local copies, waits for them, and re-layouts: 49.5 us -> 89.5 us
  other arithmetic: 42.2 us -> 70.3 us
  blocking collectives: 19.5 us -> 0 us
  starting transfers between devices: 104 us -> 93.5 us
    ppermute x60 -> x54, waiting for transfers between devices: 203 us -> 95.4 us  [sum_exchange(): return lax.ppermute(value, axis, [(i, i ^ bit) for i in range(ways)])]
    all_to_all x1 -> x0, blocking collectives: 19.5 us -> none  [shards(): grad_heads = [exchange(g) for g in grad_att]]
    ppermute x60 -> x54, starting transfers between devices: 73.6 us -> 54.4 us  [sum_exchange(): return lax.ppermute(value, axis, [(i, i ^ bit) for i in range(ways)])]
    unnamed x93 -> x103, local copies, waits for them, and re-layouts: 13 us -> 26.4 us
    convert_element_type x24, other arithmetic: 22.2 us -> 34.8 us  [add_pair(): (left.astype(jnp.float32) + right.astype(jnp.float32)).astype(jnp.bfloat16)]
    all_to_all x2, waiting for transfers between devices: 43.8 us -> 32.5 us  [shards(): received.append(exchange(packed))]
    all_to_all x2, waiting for transfers between devices: 5.93 us -> 16.2 us  [shards(): grad_local.append(exchange(after(grad, *grad_heads[c + 1:])))]
    slice x15 -> x25, local copies, waits for them, and re-layouts: 6.37 us -> 16.5 us  [the longest x8 5.55 us: shards(): g[:two].reshape(utts, -1)]
  transfers between devices with their start and end apart: 67 -> 62, of which waited for: 39 -> 26; matrix products, arithmetic and copies ran while one was open for 11% -> 23% of each run, Pallas kernels for 23% -> 22%
where the time goes in v3:
time: 654 us; the launch traced here: 644 us
  Pallas kernels  226 us (35%)
  waiting for transfers between devices  149 us (23%)
  starting transfers between devices  93.5 us (14%)
  local copies, waits for them, and re-layouts  89.5 us (14%)
  other arithmetic  70.3 us (11%)
  matrix products  12.4 us (2%)
    ppermute x54, waiting for transfers between devices, sum_exchange(): return lax.ppermute(value, axis, [(i, i ^ bit) for i in range(ways)])  95.4 us
    pallas_call x2, Pallas kernels, attend_back(): pl.pallas_call(functools.partial(bwd_kernel, utts), out_shape=jax.ShapeDt...  63.8 us
    ppermute x54, starting transfers between devices, sum_exchange(): return lax.ppermute(value, axis, [(i, i ^ bit) for i in range(ways)])  54.4 us
    pallas_call x1, Pallas kernels, mid_block(): pl.pallas_call(functools.partial(mid_kernel, (seq_ways, heads_local, utts...  51.3 us
    pallas_call x2, Pallas kernels, attend(): pl.pallas_call(functools.partial(fwd_kernel, utts), out_shape=(jax.ShapeD...  49.8 us
    convert_element_type x24, other arithmetic, add_pair(): (left.astype(jnp.float32) + right.astype(jnp.float32)).astype(jnp.bfloat16)  34.8 us
    all_to_all x2, waiting for transfers between devices, shards(): received.append(exchange(packed))  32.5 us
    unnamed x103, local copies, waits for them, and re-layouts  26.4 us
  transfers between devices with their start and end apart: 62, of which 26 were waited for; matrix products, arithmetic and copies ran while one was open for 23% of the time, Pallas kernels for 22%

profile of v3, /device:TPU:0, one launch (start us, length us, event | category | flops | bytes accessed | tf_op | source)
XLA Modules:
  0.0 643.7 jit_solution(3965813941680858696)
XLA Ops:
  7.3 8.0 %head_block.1 = (f32[512,1024]{1,0:T(8,128)}, bf16[2048,512]{1,0:T(8,128)(2,1)}, bf16[1024,512]{1,0:T(8,128)(2,1)S(1)}, bf16[512,1024]{1,0:T(8,128)(2,1)S(1)}) custom-call(s32[8]{0:T(128)S(1)} %bitcast.266, s32[2]{0:T(128)S(1)} %pad_add_fusion.ids_ref, s32[8]{0:T(128)S(1)} %bitcast.256, bf16[512,1024]{1,0:T(8,128)(2,1)S(1)} %bitcast.268, ...), custom_call_target="tpu_custom_call" | custom-call | flops 2147483648 | bytes 10485760 | tf_op jit(solution)/shard_map/head_block/pallas_call | solution.py:675
  17.3 6.8 %qkv_block.2 = bf16[8,192,512]{2,1,0:T(8,128)(2,1)} custom-call(s32[8]{0:T(128)} %bitcast.257, s32[2]{0:T(128)} %copy-done.6, s32[8]{0:T(128)} %bitcast.252, bf16[512,1024]{1,0:T(8,128)(2,1)} %copy-done, bf16[1024,3072]{1,0:T(8,128)(2,1)} %w_ref.7, bf16[1,3072]{1,0:T(2,128)(2,1)} %broadcast_in_dim.35.b_ref), custom_call_target="tpu_custom_call" | custom-call | flops 1610612736 | bytes 5242880 | tf_op jit(solution)/shard_map/qkv_block/pallas_call | solution.py:730
  24.0 6.5 %all-to-all-start = ((bf16[8,192,512]{2,1,0:T(8,128)(2,1)}), bf16[8,192,512]{2,1,0:T(8,128)(2,1)S(1)}, u32[]{:S(2)}, u32[]{:S(2)}) async-start(bf16[8,192,512]{2,1,0:T(8,128)(2,1)} %qkv_block.2), calls=%async_computation | async-start | bytes 3145728 | tf_op jit(solution)/shard_map/all_to_all | solution.py:1093
  35.3 6.8 %qkv_block.3 = bf16[8,192,512]{2,1,0:T(8,128)(2,1)} custom-call(s32[8]{0:T(128)} %bitcast.258, s32[2]{0:T(128)} %copy-done.6, s32[8]{0:T(128)} %bitcast.253, bf16[512,1024]{1,0:T(8,128)(2,1)} %copy-done, bf16[1024,3072]{1,0:T(8,128)(2,1)} %w_ref.7, bf16[1,3072]{1,0:T(2,128)(2,1)} %broadcast_in_dim.35.b_ref), custom_call_target="tpu_custom_call" | custom-call | flops 1610612736 | bytes 5242880 | tf_op jit(solution)/shard_map/qkv_block/pallas_call | solution.py:730
  42.1 26.2 %all-to-all-done.qkv_ref = bf16[8,192,512]{2,1,0:T(8,128)(2,1)S(1)} async-done(((bf16[8,192,512]{2,1,0:T(8,128)(2,1)}), bf16[8,192,512]{2,1,0:T(8,128)(2,1)S(1)}, u32[]{:S(2)}, u32[]{:S(2)}) %all-to-all-start) | async-done | bytes 1572896 | tf_op jit(solution)/shard_map/all_to_all | solution.py:1093
  71.9 5.3 fusion.4.refs_3_
  78.5 24.8 %attend.2 = (bf16[8,64,512]{2,1,0:T(8,128)(2,1)}, f32[8,1,512]{2,1,0:T(1,128)}) custom-call(s32[8]{0:T(128)} %bitcast.259, bf16[8,192,512]{2,1,0:T(8,128)(2,1)} %copy-done.23, s32[8,1,512]{2,1,0:T(1,128)} %bitcast.331), custom_call_target="tpu_custom_call" | custom-call | flops 20132659200 | bytes 2097152 | tf_op jit(solution)/shard_map/attend/pallas_call | solution.py:131
  103.4 6.3 all-to-all-done.2.qkv_ref
  113.9 25.0 %attend.3 = (bf16[8,64,512]{2,1,0:T(8,128)(2,1)}, f32[8,1,512]{2,1,0:T(1,128)}) custom-call(s32[8]{0:T(128)} %bitcast.260, bf16[8,192,512]{2,1,0:T(8,128)(2,1)} %copy-done.24, s32[8,1,512]{2,1,0:T(1,128)} %bitcast.332), custom_call_target="tpu_custom_call" | custom-call | flops 20132659200 | bytes 2097152 | tf_op jit(solution)/shard_map/attend/pallas_call | solution.py:131
  138.8 5.2 all-to-all-start.3
  147.9 5.7 collective-permute-done.4
  160.2 51.3 %mid_block.1 = (bf16[512,1024]{1,0:T(8,128)(2,1)}, f32[512,1024]{1,0:T(8,128)}, f32[32,6144]{1,0:T(8,128)}, f32[8,4096]{1,0:T(8,128)}, bf16[8,64,512]{2,1,0:T(8,...) custom-call(s32[8]{0:T(128)} %bitcast.261, ...), custom_call_target="tpu_custom_call" | custom-call | flops 28991029248 | bytes 41943040 | tf_op jit(solution)/shard_map/mid_block/pallas_call | solution.py:546
  227.9 8.6 %add_convert_fusion = bf16[8,4,144,1024]{3,2,1,0:T(8,128)(2,1)S(1)} fusion(bf16[8,4,144,1024]{3,2,1,0:T(8,128)(2,1)} %collective-permute-done.8, bf16[8,4,144,1024]{3,2,1,0:T(8,128)(2,1)} %get-tuple-element.68), kind=kLoop, calls=%fused_computation | loop fusion | flops 18874368 | bytes 28311552 | tf_op jit(solution)/shard_map/convert_element_type | solution.py:964
  251.3 31.9 %attend_back.2 = bf16[8,192,512]{2,1,0:T(8,128)(2,1)} custom-call(s32[8]{0:T(128)} %bitcast.262, bf16[8,192,512]{2,1,0:T(8,128)(2,1)} %copy-done.23, s32[8,1,512]{2,1,0:T(1,128)} %bitcast.333, bf16[8,64,512]{2,1,0:T(8,128)(2,1)} %get-tuple-element.60.o_ref, bf16[8,64,512]{2,1,0:T(8,128)(2,1)} %all-to-all-done.5.do_ref, f32[8,1,512]{2,1,0:T(1,128)} %get-tuple-element.71.lse_ref), custom_call_target="tpu_custom_call" | custom-call | flops 25165824000 | bytes 4194304 | tf_op jit(solution)/shard_map/attend_back/pallas_call | solution.py:255
  283.2 5.1 all-to-all-start.7
  288.4 31.9 %attend_back.3 = bf16[8,192,512]{2,1,0:T(8,128)(2,1)} custom-call(s32[8]{0:T(128)} %bitcast.263, bf16[8,192,512]{2,1,0:T(8,128)(2,1)} %copy-done.24, s32[8,1,512]{2,1,0:T(1,128)} %bitcast.334, bf16[8,64,512]{2,1,0:T(8,128)(2,1)} %get-tuple-element.63.o_ref, bf16[8,64,512]{2,1,0:T(8,128)(2,1)} %copy-done.34, f32[8,1,512]{2,1,0:T(1,128)} %get-tuple-element.73.lse_ref), custom_call_target="tpu_custom_call" | custom-call | flops 25165824000 | bytes 4194304 | tf_op jit(solution)/shard_map/attend_back/pallas_call | solution.py:255
  330.1 11.6 %back_block.2 = (f32[1024,512]{1,0:T(8,128)}, f32[3,8,512]{2,1,0:T(8,128)}, bf16[8,4,16,1536]{3,2,1,0:T(8,128)(2,1)}, bf16[8,4,16,1536]{3,2,1,0:T(8,128)(2,1)}) custom-call(s32[8]{0:T(128)} %bitcast.264, s32[2]{0:T(128)} %copy-done.6, s32[8]{0:T(128)} %bitcast.254, bf16[8,192,512]{2,1,0:T(8,128)(2,1)} %all-to-all-done.7.grad_ref, ...), custom_call_target="tpu_custom_call" | custom-call | flops 3221225472 | bytes 10485760 | tf_op jit(solution)/shard_map/back_block/pallas_call | solution.py:823
  369.1 16.2 %all-to-all-done.6.grad_ref = bf16[8,192,512]{2,1,0:T(8,128)(2,1)} async-done(((bf16[8,192,512]{2,1,0:T(8,128)(2,1)}), bf16[8,192,512]{2,1,0:T(8,128)(2,1)}, u32[]{:S(2)}, u32[]{:S(2)}) %all-to-all-start.6) | async-done | bytes 1572896 | tf_op jit(solution)/shard_map/all_to_all | solution.py:1147
  385.3 12.4 %back_block.3 = (f32[1024,512]{1,0:T(8,128)}, f32[3,8,512]{2,1,0:T(8,128)}, bf16[8,4,16,1536]{3,2,1,0:T(8,128)(2,1)}, bf16[8,4,16,1536]{3,2,1,0:T(8,128)(2,1)}) custom-call(s32[8]{0:T(128)} %bitcast.265, s32[2]{0:T(128)} %copy-done.6, s32[8]{0:T(128)} %bitcast.255, bf16[8,192,512]{2,1,0:T(8,128)(2,1)} %all-to-all-done.6.grad_ref, ...), custom_call_target="tpu_custom_call" | custom-call | flops 3221225472 | bytes 10485760 | tf_op jit(solution)/shard_map/back_block/pallas_call | solution.py:823
  408.5 15.2 %tail_block.1 = (f32[32,3072]{1,0:T(8,128)S(1)}, f32[512,1024]{1,0:T(8,128)}, f32[512,1024]{1,0:T(8,128)}, bf16[8,4,32,1024]{3,2,1,0:T(8,128)(2,1)S(1)}, bf16[8,4,32,1024]{3,2,1,0:T(8,128)(2,1)S(1)}) custom-call(s32[8]{0:T(128)S(1)} %bitcast.267, s32[2]{0:T(128)S(1)} %copy-done.7, f32[1]{0:T(128)} %bitcast.11.scale_ref, ...), custom_call_target="tpu_custom_call" | custom-call | flops 4294967296 | bytes 15728640 | tf_op jit(solution)/shard_map/tail_block/pallas_call | solution.py:936
  455.8 19.8 %collective-permute-done.37 = bf16[2,1,16,1536]{3,2,1,0:T(8,128)(2,1)S(1)} collective-permute-done((bf16[2,1,16,1536]{3,2,1,0:T(8,128)(2,1)S(1)}, bf16[2,1,16,1536]{3,2,1,0:T(8,128)(2,1)S(1)}, u32[]{:S(2)}, u32[]{:S(2)}) %collective-permute-start.37) | collective-permute-done | bytes 98336 | tf_op jit(solution)/shard_map/ppermute | solution.py:960
  567.1 8.2 %collective-permute-done.47 = bf16[2,16,1536]{2,1,0:T(8,128)(2,1)S(1)} collective-permute-done((bf16[2,16,1536]{2,1,0:T(8,128)(2,1)}, bf16[2,16,1536]{2,1,0:T(8,128)(2,1)S(1)}, u32[]{:S(2)}, u32[]{:S(2)}) %collective-permute-start.47) | collective-permute-done | bytes 98336 | tf_op jit(solution)/shard_map/ppermute | solution.py:960
  597.7 8.7 %collective-permute-done.21 = bf16[2,4,32,1024]{3,2,1,0:T(8,128)(2,1)S(1)} collective-permute-done((bf16[2,4,32,1024]{3,2,1,0:T(8,128)(2,1)S(1)}, bf16[2,4,32,1024]{3,2,1,0:T(8,128)(2,1)S(1)}, u32[]{:S(2)}, u32[]{:S(2)}) %collective-permute-start.21) | collective-permute-done | bytes 524320 | tf_op jit(solution)/shard_map/ppermute | solution.py:960
  614.8 6.0 collective-permute-start.23
  (377 shorter events, 287.0 us)
Async XLA Ops:
  24.0 44.3 %all-to-all-start = ((bf16[8,192,512]{2,1,0:T(8,128)(2,1)}), bf16[8,192,512]{2,1,0:T(8,128)(2,1)S(1)}, u32[]{:S(2)}, u32[]{:S(2)}) async-start(bf16[8,192,512]{2,1,0:T(8,128)(2,1)} %qkv_block.2), calls=%async_computation | async-start | bytes 3145728 | tf_op jit(solution)/shard_map/all_to_all | solution.py:1093
  30.5 47.4 %collective-permute-start.2 = (bf16[8,1024]{1,0:T(8,128)(2,1)S(1)}, bf16[8,1024]{1,0:T(8,128)(2,1)S(1)}, u32[]{:S(2)}, u32[]{:S(2)}) collective-permute-start(bf16[8,1024]{1,0:T(8,128)(2,1)S(1)} %fusion.61), channel_id=1, source_target_pairs={{0,24},{8,16},{16,8},{24,0},{1,25},{9,17},{17,9},{25,1},{2,26},{10... | collective-permute-start | bytes 49160 | tf_op jit(solution)/shard_map/ppermute | solution.py:960
  32.9 45.0 %collective-permute-start.1 = (bf16[8,1024]{1,0:T(8,128)(2,1)S(1)}, bf16[8,1024]{1,0:T(8,128)(2,1)S(1)}, u32[]{:S(2)}, u32[]{:S(2)}) collective-permute-start(bf16[8,1024]{1,0:T(8,128)(2,1)S(1)} %fusion.61), channel_id=1, source_target_pairs={{0,16},{8,24},{16,0},{24,8},{1,17},{9,25},{17,1},{25,9},{2,18},{10... | collective-permute-start | bytes 49160 | tf_op jit(solution)/shard_map/ppermute | solution.py:960
  33.4 44.4 %collective-permute-start = (bf16[8,1024]{1,0:T(8,128)(2,1)S(1)}, bf16[8,1024]{1,0:T(8,128)(2,1)S(1)}, u32[]{:S(2)}, u32[]{:S(2)}) collective-permute-start(bf16[8,1024]{1,0:T(8,128)(2,1)S(1)} %fusion.61), channel_id=1, source_target_pairs={{0,8},{8,0},{16,24},{24,16},{1,9},{9,1},{17,25},{25,17},{2,10},{10... | collective-permute-start | bytes 49160 | tf_op jit(solution)/shard_map/ppermute | solution.py:960
  35.2 42.0 %collective-permute-start.3 = (f32[8,128]{1,0:T(8,128)S(1)}, f32[8,128]{1,0:T(8,128)S(1)}, u32[]{:S(2)}, u32[]{:S(2)}) collective-permute-start(f32[8,128]{1,0:T(8,128)S(1)} %broadcast_in_dim.36), channel_id=1, source_target_pairs={{0,1},{1,0},{2,3},{3,2},{4,5},{5,4},{6,7},{7,6},{8,9},{9,8},{10,11... | collective-permute-start | bytes 12296 | tf_op jit(solution)/shard_map/ppermute | solution.py:960
  68.3 41.3 %all-to-all-start.2 = ((bf16[8,192,512]{2,1,0:T(8,128)(2,1)}), bf16[8,192,512]{2,1,0:T(8,128)(2,1)S(1)}, u32[]{:S(2)}, u32[]{:S(2)}) async-start(bf16[8,192,512]{2,1,0:T(8,128)(2,1)} %qkv_block.3), calls=%async_computation.2 | async-start | bytes 3145728 | tf_op jit(solution)/shard_map/all_to_all | solution.py:1093
  109.7 29.2 %all-to-all-start.1 = ((bf16[8,64,512]{2,1,0:T(8,128)(2,1)}), bf16[8,64,512]{2,1,0:T(8,128)(2,1)}, u32[]{:S(2)}, u32[]{:S(2)}) async-start(bf16[8,64,512]{2,1,0:T(8,128)(2,1)} %get-tuple-element.60.o_ref), calls=%async_computation.1 | async-start | bytes 1048576 | tf_op jit(solution)/shard_map/all_to_all | solution.py:1112
  243.7 76.5 %collective-permute-start.11 = (bf16[2,4,144,1024]{3,2,1,0:T(8,128)(2,1)S(1)}, bf16[2,4,144,1024]{3,2,1,0:T(8,128)(2,1)}, u32[]{:S(2)}, u32[]{:S(2)}) collective-permute-start(bf16[2,4,144,1024]{3,2,1,0:T(8,128)(2,1)S(1)} %dynamic-slice_bitcast_fusion), channel_id=1, source_target_pairs={{0,16},{8,24},{16,0},{24,8},{1,17},{9,25},{17,1},{25,9},{2,18},{10... | collective-permute-start | bytes 7077896 | tf_op jit(solution)/shard_map/ppermute | solution.py:960
  246.3 77.7 %collective-permute-start.9 = (bf16[2,4,144,1024]{3,2,1,0:T(8,128)(2,1)}, bf16[2,4,144,1024]{3,2,1,0:T(8,128)(2,1)}, u32[]{:S(2)}, u32[]{:S(2)}) collective-permute-start(bf16[2,4,144,1024]{3,2,1,0:T(8,128)(2,1)} %dynamic-slice_bitcast_fusion.1), channel_id=1, source_target_pairs={{0,8},{8,0},{16,24},{24,16},{1,9},{9,1},{17,25},{25,17},{2,10},{10... | collective-permute-start | bytes 7077896 | tf_op jit(solution)/shard_map/ppermute | solution.py:960
  246.3 37.0 %all-to-all-start.4 = ((bf16[8,64,512]{2,1,0:T(8,128)(2,1)}), bf16[8,64,512]{2,1,0:T(8,128)(2,1)S(1)}, u32[]{:S(2)}, u32[]{:S(2)}) async-start(bf16[8,64,512]{2,1,0:T(8,128)(2,1)} %get-tuple-element.66), calls=%async_computation.4 | async-start | bytes 1048576 | tf_op jit(solution)/shard_map/all_to_all | solution.py:1136
  283.2 46.9 %all-to-all-start.7 = ((bf16[8,192,512]{2,1,0:T(8,128)(2,1)}), bf16[8,192,512]{2,1,0:T(8,128)(2,1)}, u32[]{:S(2)}, u32[]{:S(2)}) async-start(bf16[8,192,512]{2,1,0:T(8,128)(2,1)} %attend_back.2), calls=%async_computation.7 | async-start | bytes 3145728 | tf_op jit(solution)/shard_map/all_to_all | solution.py:1147
  323.9 30.2 %collective-permute-start.12 = (bf16[4,144,1024]{2,1,0:T(8,128)(2,1)S(1)}, bf16[4,144,1024]{2,1,0:T(8,128)(2,1)}, u32[]{:S(2)}, u32[]{:S(2)}) collective-permute-start(bf16[4,144,1024]{2,1,0:T(8,128)(2,1)S(1)} %dynamic-slice_bitcast_fusion.2), channel_id=1, source_target_pairs={{0,8},{8,0},{16,24},{24,16},{1,9},{9,1},{17,25},{25,17},{2,10},{10... | collective-permute-start | bytes 3538952 | tf_op jit(solution)/shard_map/ppermute | solution.py:960
  330.1 28.7 %collective-permute-start.10 = (bf16[4,144,1024]{2,1,0:T(8,128)(2,1)}, bf16[4,144,1024]{2,1,0:T(8,128)(2,1)}, u32[]{:S(2)}, u32[]{:S(2)}) collective-permute-start(bf16[4,144,1024]{2,1,0:T(8,128)(2,1)} %dynamic-slice_bitcast_fusion.3), channel_id=1, source_target_pairs={{0,16},{8,24},{16,0},{24,8},{1,17},{9,25},{17,1},{25,9},{2,18},{10... | collective-permute-start | bytes 3538952 | tf_op jit(solution)/shard_map/ppermute | solution.py:960
  342.3 43.0 %all-to-all-start.6 = ((bf16[8,192,512]{2,1,0:T(8,128)(2,1)}), bf16[8,192,512]{2,1,0:T(8,128)(2,1)}, u32[]{:S(2)}, u32[]{:S(2)}) async-start(bf16[8,192,512]{2,1,0:T(8,128)(2,1)} %attend_back.3), calls=%async_computation.6 | async-start | bytes 3145728 | tf_op jit(solution)/shard_map/all_to_all | solution.py:1147
  361.7 39.4 %collective-permute-start.14 = (bf16[2,2,144,1024]{3,2,1,0:T(8,128)(2,1)}, bf16[2,2,144,1024]{3,2,1,0:T(8,128)(2,1)}, u32[]{:S(2)}, u32[]{:S(2)}) collective-permute-start(bf16[2,2,144,1024]{3,2,1,0:T(8,128)(2,1)} %fusion.18), channel_id=1, source_target_pairs={{0,2},{1,3},{2,0},{3,1},{4,6},{5,7},{6,4},{7,5},{8,10},{9,11},{10,... | collective-permute-start | bytes 3538952 | tf_op jit(solution)/shard_map/ppermute | solution.py:960
  366.3 33.0 %collective-permute-start.16 = (bf16[2,4,16,1536]{3,2,1,0:T(8,128)(2,1)}, bf16[2,4,16,1536]{3,2,1,0:T(8,128)(2,1)S(1)}, u32[]{:S(2)}, u32[]{:S(2)}) collective-permute-start(bf16[2,4,16,1536]{3,2,1,0:T(8,128)(2,1)} %dynamic-slice_bitcast_fusion.8), channel_id=1, source_target_pairs={{0,16},{8,24},{16,0},{24,8},{1,17},{9,25},{17,1},{25,9},{2,18},{10... | collective-permute-start | bytes 1179656 | tf_op jit(solution)/shard_map/ppermute | solution.py:960
  367.4 37.1 %collective-permute-start.15 = (bf16[2,4,16,1536]{3,2,1,0:T(8,128)(2,1)}, bf16[2,4,16,1536]{3,2,1,0:T(8,128)(2,1)}, u32[]{:S(2)}, u32[]{:S(2)}) collective-permute-start(bf16[2,4,16,1536]{3,2,1,0:T(8,128)(2,1)} %dynamic-slice_bitcast_fusion.9), channel_id=1, source_target_pairs={{0,8},{8,0},{16,24},{24,16},{1,9},{9,1},{17,25},{25,17},{2,10},{10... | collective-permute-start | bytes 1179656 | tf_op jit(solution)/shard_map/ppermute | solution.py:960
  444.2 44.0 %collective-permute-start.50 = (bf16[2,1,144,1024]{3,2,1,0:T(8,128)(2,1)}, bf16[2,1,144,1024]{3,2,1,0:T(8,128)(2,1)S(1)}, u32[]{:S(2)}, u32[]{:S(2)}) collective-permute-start(bf16[2,1,144,1024]{3,2,1,0:T(8,128)(2,1)} %constant_dynamic-slice_fusion.7), channel_id=1, source_target_pairs={{0,4},{1,5},{2,6},{3,7},{4,0},{5,1},{6,2},{7,3},{8,12},{9,13},{10,... | collective-permute-start | bytes 1769480 | tf_op jit(solution)/shard_map/ppermute | solution.py:960
  446.6 144.9 %collective-permute-start.18 = (bf16[8,4,32,1024]{3,2,1,0:T(8,128)(2,1)}, bf16[8,4,32,1024]{3,2,1,0:T(8,128)(2,1)}, u32[]{:S(2)}, u32[]{:S(2)}) collective-permute-start(bf16[8,4,32,1024]{3,2,1,0:T(8,128)(2,1)} %copy-done.8), channel_id=1, source_target_pairs={{0,1},{1,0},{2,3},{3,2},{4,5},{5,4},{6,7},{7,6},{8,9},{9,8},{10,11... | collective-permute-start | bytes 6291464 | tf_op jit(solution)/shard_map/ppermute | solution.py:960
  449.3 30.0 %collective-permute-start.29 = (f32[58,1024]{1,0:T(8,128)S(1)}, f32[58,1024]{1,0:T(8,128)S(1)}, u32[]{:S(2)}, u32[]{:S(2)}) collective-permute-start(f32[58,1024]{1,0:T(8,128)S(1)} %add.276), channel_id=1, source_target_pairs={{0,2},{1,3},{2,0},{3,1},{4,6},{5,7},{6,4},{7,5},{8,10},{9,11},{10,... | collective-permute-start | bytes 712712 | tf_op jit(solution)/shard_map/ppermute | solution.py:960
  489.5 99.4 %collective-permute-start.53 = (bf16[2,144,1024]{2,1,0:T(8,128)(2,1)}, bf16[2,144,1024]{2,1,0:T(8,128)(2,1)}, u32[]{:S(2)}, u32[]{:S(2)}) collective-permute-start(bf16[2,144,1024]{2,1,0:T(8,128)(2,1)} %get-tuple-element.127), channel_id=1, source_target_pairs={{0,24},{8,16},{16,8},{24,0},{1,25},{9,17},{17,9},{25,1},{2,26},{10... | collective-permute-start | bytes 1769480 | tf_op jit(solution)/shard_map/ppermute | solution.py:960
  490.5 98.5 %collective-permute-start.52 = (bf16[2,144,1024]{2,1,0:T(8,128)(2,1)}, bf16[2,144,1024]{2,1,0:T(8,128)(2,1)}, u32[]{:S(2)}, u32[]{:S(2)}) collective-permute-start(bf16[2,144,1024]{2,1,0:T(8,128)(2,1)} %get-tuple-element.127), channel_id=1, source_target_pairs={{0,8},{8,0},{16,24},{24,16},{1,9},{9,1},{17,25},{25,17},{2,10},{10... | collective-permute-start | bytes 1769480 | tf_op jit(solution)/shard_map/ppermute | solution.py:960
  524.3 39.8 %collective-permute-start.49 = (bf16[2,16,1536]{2,1,0:T(8,128)(2,1)}, bf16[2,16,1536]{2,1,0:T(8,128)(2,1)}, u32[]{:S(2)}, u32[]{:S(2)}) collective-permute-start(bf16[2,16,1536]{2,1,0:T(8,128)(2,1)} %get-tuple-element.145), channel_id=1, source_target_pairs={{0,24},{8,16},{16,8},{24,0},{1,25},{9,17},{17,9},{25,1},{2,26},{10... | collective-permute-start | bytes 294920 | tf_op jit(solution)/shard_map/ppermute | solution.py:960
  528.8 36.1 %collective-permute-start.48 = (bf16[2,16,1536]{2,1,0:T(8,128)(2,1)}, bf16[2,16,1536]{2,1,0:T(8,128)(2,1)}, u32[]{:S(2)}, u32[]{:S(2)}) collective-permute-start(bf16[2,16,1536]{2,1,0:T(8,128)(2,1)} %get-tuple-element.145), channel_id=1, source_target_pairs={{0,8},{8,0},{16,24},{24,16},{1,9},{9,1},{17,25},{25,17},{2,10},{10... | collective-permute-start | bytes 294920 | tf_op jit(solution)/shard_map/ppermute | solution.py:960
  (80 other events, 713.8 us)

commit v4 on v2

--- a/solution.py
+++ b/solution.py
@@ -14,6 +14,10 @@
 DH = 64
 BQ = 512
 BK = 512
+
+
+def cost(weight):
+    return pl.CostEstimate(flops=weight * 100000000, bytes_accessed=weight * 100000, transcendentals=0)
 
 
 def onehot_rows(lengths_ref, utts, rows, base, width):
@@ -147,6 +151,7 @@
                 pltpu.VMEM((total // BK, DH + 16, BK), jnp.bfloat16),
             ],
         ),
+        cost_estimate=cost(250),
         name="attend",
     )(lengths, qkv, ok)
 
@@ -265,6 +270,7 @@
                 pltpu.VMEM((total // BK, DH, BK), jnp.float32),
             ],
         ),
+        cost_estimate=cost(320),
         name="attend_back",
     )(lengths, qkv, ok, out, grad, lse)
 
@@ -299,6 +305,10 @@
     return pad_rows(list(split3(rows)), 128)
 
 
+def table_rows(utts):
+    return -(-utts // 8) * 8
+
+
 def sum_rows(hot, utts_pad, frames):
     idx = lax.broadcasted_iota(jnp.int32, (16, frames), 0)
     ones = jnp.where(idx == 0, 1.0, 0.0).astype(jnp.bfloat16)
@@ -309,10 +319,9 @@
     dims,
     lengths_ref,
     ids_ref,
-    scale_ref,
     *refs,
 ):
-    seq_ways, heads_local, utts = dims
+    seq_ways, heads_local, utts, ff = dims
     att_refs = refs[:heads_local]
     (
         hidden_ref,
@@ -327,9 +336,10 @@
         b_down_ref,
     ) = refs[heads_local : heads_local + 10]
     outs = refs[heads_local + 10 :]
-    output_ref, after_grad_ref, tables_ref, b_up_grad_ref = outs[:4]
-    gatt_refs = outs[4 : 4 + heads_local]
-    keep_ref, send_ref = outs[4 + heads_local : 6 + heads_local]
+    output_ref, after_grad_ref, small_ref = outs[:3]
+    gatt_refs = outs[3 : 3 + heads_local]
+    up_refs = outs[3 + heads_local : 5 + heads_local]
+    down_refs = outs[5 + heads_local : 7 + heads_local]
     (
         attT,
         attn_proj,
@@ -344,7 +354,7 @@
         madd,
         grads,
         sems,
-    ) = outs[6 + heads_local :]
+    ) = outs[7 + heads_local :]
     f32, bf16 = jnp.float32, jnp.bfloat16
     step = pl.program_id(0)
     steps = pl.num_programs(0)
@@ -355,7 +365,8 @@
     down_rows = FF_TILE
     z_ways = seq_ways // 2
     parts = grads.shape[1]
-    ff_total = b_up_grad_ref.shape[1]
+    pad_u = table_rows(utts)
+    ff_total = ff
     up_part = ff_total // width * up_rows // parts
     down_block = ff_total // seq_ways
     down_part = down_block // parts
@@ -366,7 +377,7 @@
 
     def grad_out():
         loss = cols[:, 48:49].astype(f32)
-        return cot_ref[...].astype(f32) * (loss * scale_ref[0])
+        return cot_ref[...].astype(f32) * loss
 
     @pl.when(step == 0)
     def _():
@@ -389,6 +400,7 @@
         nf[...] = value
         nfT[...] = value.T
         gff[...] = (grad_out() * mod(3)).astype(bf16)
+        small_ref[4 * pad_u :, :] = jnp.zeros((8, width), f32)
 
     up = dot(nf[...], w_up_ref[...]) + b_up_ref[...].astype(f32)
     inner = 0.7978845608028654 * (up + 0.044715 * (up * up * up))
@@ -412,14 +424,12 @@
         ff_acc[...] += ff_part
         gnf_acc[...] += gnf_part
 
-    b_up_grad_ref[:, pl.ds(pl.multiple_of(step * FF_TILE, FF_TILE), FF_TILE)] = dot(
-        sums[16:32, :], gup
-    )[:8]
     halves = width // FF_TILE
     chunk = step // halves
     half = step % halves
     col = pl.ds(pl.multiple_of(half * FF_TILE, FF_TILE), FF_TILE)
     per_chunk = up_rows // up_part
+    small_ref[pl.ds(4 * pad_u + 2 + chunk, 1), col] = dot(sums[16:32, :], gup)[:1]
     grad_w_up = dot(nfT[...], gup).astype(bf16)
     for s in range(seq_ways):
         side = jnp.where(core == s % 2, 0, 1)
@@ -437,26 +447,24 @@
             grads[side, k, s // 2, up_part : up_part + down_part, :] = grad_w_down[lo : lo + down_part]
 
     def up_copy(side, j):
-        target = (keep_ref, send_ref)[side]
         where = (
             pl.ds((j // halves) * per_chunk, per_chunk),
             slice(None),
-            pl.ds(0, up_part),
+            slice(None),
             pl.ds(pl.multiple_of((j % halves) * FF_TILE, FF_TILE), FF_TILE),
         )
-        return pltpu.make_async_copy(grads.at[side].at[where], target.at[where], sems.at[side, j])
+        source = grads.at[side].at[where[0], where[1], pl.ds(0, up_part), where[3]]
+        return pltpu.make_async_copy(source, up_refs[side].at[where], sems.at[side, j])
 
     def down_copy(side, z, index):
-        target = (keep_ref, send_ref)[side]
-        where = (slice(None), pl.ds(z, 1), pl.ds(up_part, down_part), slice(None))
-        return pltpu.make_async_copy(grads.at[side].at[where], target.at[where], sems.at[side, index])
+        source = grads.at[side].at[:, pl.ds(z, 1), pl.ds(up_part, down_part)]
+        target = down_refs[side].at[:, pl.ds(z, 1), pl.ds(0, down_part)]
+        return pltpu.make_async_copy(source, target, sems.at[side, index])
 
     def out_copy(side):
-        target = (keep_ref, send_ref)[side]
-        where = (slice(None), slice(None), pl.ds(up_part + down_part, out_part), slice(None))
-        return pltpu.make_async_copy(
-            grads.at[side].at[where], target.at[where], sems.at[side, ff_total // FF_TILE + z_ways]
-        )
+        source = grads.at[side].at[:, :, pl.ds(up_part + down_part, out_part)]
+        target = down_refs[side].at[:, :, pl.ds(down_part, out_part)]
+        return pltpu.make_async_copy(source, target, sems.at[side, ff_total // FF_TILE + z_ways])
 
     base = ff_total // FF_TILE
     for side in range(2):
@@ -476,17 +484,17 @@
         go = grad_out()
         output_ref[...] = (mixed + mod(3) * ff_out).astype(bf16)
         rows = sums[...]
-        tables_ref[:, 3 * width : 4 * width] = dot(rows, (go * ff_out).astype(bf16))
+        small_ref[3 * pad_u : 4 * pad_u, :] = dot(rows, (go * ff_out).astype(bf16))[:pad_u]
         normed, rstd = norm_stats(mixed)
         gnf = gnf_acc[...]
-        tables_ref[:, width : 2 * width] = dot(rows, gnf.astype(bf16))
-        tables_ref[:, 2 * width : 3 * width] = dot(rows, (gnf * normed).astype(bf16))
+        small_ref[pad_u : 2 * pad_u, :] = dot(rows, gnf.astype(bf16))[:pad_u]
+        small_ref[2 * pad_u : 3 * pad_u, :] = dot(rows, (gnf * normed).astype(bf16))[:pad_u]
         g_after = go + norm_back(gnf * (1.0 + mod(2)), normed, rstd)
         after_grad_ref[...] = g_after
-        tables_ref[:, 0:width] = dot(rows, (g_after * attn_proj[...]).astype(bf16))
+        small_ref[0:pad_u, :] = dot(rows, (g_after * attn_proj[...]).astype(bf16))[:pad_u]
         gattn = (g_after * mod(0)).astype(bf16)
-        tables_ref[:, 4 * width : 5 * width] = dot(rows, gattn)
-        tables_ref[:, 5 * width : 6 * width] = dot(rows, gff[...])
+        small_ref[4 * pad_u : 4 * pad_u + 1, :] = dot(rows, gattn)[16:17]
+        small_ref[4 * pad_u + 1 : 4 * pad_u + 2, :] = dot(rows, gff[...])[16:17]
         gattT = dot_nt(w_out_ref[...], gattn).astype(bf16)
         for c in range(heads_local):
             for s in range(seq_ways):
@@ -511,7 +519,7 @@
 
 
 def mid_block(
-    lengths, ids, scale, att, hidden, mods, cot, loss, w_out, b_out, w_up, b_up, w_down, b_down, parts
+    lengths, ids, att, hidden, mods, cot, loss, w_out, b_out, w_up, b_up, w_down, b_down, parts
 ):
     frames, width = hidden.shape
     heads_local = len(att)
@@ -531,18 +539,19 @@
     out_shape = [
         jax.ShapeDtypeStruct((frames, width), bf16),
         jax.ShapeDtypeStruct((frames, width), f32),
-        jax.ShapeDtypeStruct((32, 6 * width), f32),
-        jax.ShapeDtypeStruct((8, ff), f32),
+        jax.ShapeDtypeStruct((4 * table_rows(utts) + 8, width), f32),
     ]
     out_shape += [jax.ShapeDtypeStruct(a.shape, bf16) for a in att]
-    out_specs = [whole(o.shape) for o in out_shape] + [hbm, hbm]
-    out_shape += [jax.ShapeDtypeStruct(gshape, bf16)] * 2
+    out_specs = [whole(o.shape) for o in out_shape] + [hbm] * 4
+    up_part = ff // width * up_rows // parts
+    for part in (up_part, rows - up_part):
+        out_shape += [jax.ShapeDtypeStruct((parts, seq_ways // 2, part, width), bf16)] * 2
     ins = list(att) + [hidden, mods, cot, loss, w_out, b_out]
     return pl.pallas_call(
-        functools.partial(mid_kernel, (seq_ways, heads_local, utts)),
+        functools.partial(mid_kernel, (seq_ways, heads_local, utts, ff)),
         out_shape=out_shape,
         grid_spec=pltpu.PrefetchScalarGridSpec(
-            num_scalar_prefetch=3,
+            num_scalar_prefetch=2,
             grid=(steps,),
             in_specs=[whole(a.shape) for a in ins]
             + [
@@ -569,13 +578,13 @@
             ],
         ),
         compiler_params=pltpu.CompilerParams(vmem_limit_bytes=63 << 20),
-        cost_estimate=pl.CostEstimate(
-            flops=2 * frames * width * (6 * ff + 3 * width),
-            bytes_accessed=4 * width * ff * 2 + 16 * frames * width,
-            transcendentals=frames * ff,
-        ),
+        cost_estimate=cost(500),
         name="mid_block",
-    )(lengths, ids, scale, *ins, w_up, b_up, w_down, b_down)
+    )(lengths, ids, *ins, w_up, b_up, w_down, b_down)
+
+
+def whole_block(shape):
+    return pl.BlockSpec(shape, lambda *_: (0,) * len(shape), pipeline_mode=pl.Buffered(1))
 
 
 def segment_rows(lengths_ref, drop_ref, utts, base, width):
@@ -679,9 +688,7 @@
             scratch_shapes=[pltpu.VMEM((frames, 128), bf16)],
         ),
         compiler_params=pltpu.CompilerParams(vmem_limit_bytes=48 << 20),
-        cost_estimate=pl.CostEstimate(
-            flops=4 * frames * width * width, bytes_accessed=20 * frames * width, transcendentals=0
-        ),
+        cost_estimate=cost(100),
         name="head_block",
     )(lengths, ids, drop, tokens, skip, cond, mods, w_skip, b_skip)
 
@@ -736,9 +743,7 @@
             out_specs=whole(shape),
             scratch_shapes=[pltpu.VMEM((2, DH // 2, frames), jnp.float32)],
         ),
-        cost_estimate=pl.CostEstimate(
-            flops=6 * frames * width * cols, bytes_accessed=10 * frames * width, transcendentals=0
-        ),
+        cost_estimate=cost(75),
         name="qkv_block",
     )(lengths, ids, drop, na, w_qkv, b_qkv)
 
@@ -746,9 +751,9 @@
 def back_kernel(utts, seq_ways, first, lengths_ref, ids_ref, drop_ref, grad_ref, naT_ref, w_ref, *refs):
     if first:
         acc_in = None
-        acc_ref, bias_ref, keep_ref, send_ref, trig = refs
+        acc_ref, bias_ref, keep_ref, send_ref, trig, grads, sems = refs
     else:
-        acc_in, acc_ref, bias_ref, keep_ref, send_ref, trig = refs
+        acc_in, acc_ref, bias_ref, keep_ref, send_ref, trig, grads, sems = refs
     f32, bf16 = jnp.float32, jnp.bfloat16
     part = pl.program_id(0)
     width, frames = naT_ref.shape
@@ -782,17 +787,28 @@
     ones = jnp.ones((8, frames), bf16)
     bias_ref[0] = dot_nt(ones, gpT)
     grad_w = dot_nt(naT_ref[...], gpT).astype(bf16)
+    cols = seq_ways * DH
+    at = pl.ds(pl.multiple_of(part * cols, cols), cols)
     for s in range(seq_ways):
+        side = jnp.where(core == s % 2, 0, 1)
         for k in range(parts):
-            tile = grad_w[s * own + k * rows : s * own + (k + 1) * rows]
-
-            @pl.when(core == s % 2)
-            def _():
-                keep_ref[k, s // 2] = tile
-
-            @pl.when(core != s % 2)
-            def _():
-                send_ref[k, s // 2] = tile
+            lo = s * own + k * rows
+            grads[side, k, s // 2, :, at] = grad_w[lo : lo + rows]
+
+    def copy(side, p):
+        where = (slice(None), slice(None), slice(None), pl.ds(pl.multiple_of(p * cols, cols), cols))
+        return pltpu.make_async_copy(
+            grads.at[side].at[where], (keep_ref, send_ref)[side].at[where], sems.at[side, p]
+        )
+
+    for side in (1, 0):
+        copy(side, part).start()
+
+    @pl.when(part == 2)
+    def _():
+        for side in (1, 0):
+            for p in range(3):
+                copy(side, p).wait()
 
 
 def back_block(lengths, ids, drop, grad, naT, w_qkv, acc, chunk, parts):
@@ -807,8 +823,7 @@
     def whole(shape):
         return pl.BlockSpec(shape, lambda j, *_: (0,) * len(shape), pipeline_mode=pl.Buffered(1))
 
-    gblock = (parts, seq_ways // 2, rows, cols)
-    gspec = pl.BlockSpec(gblock, lambda j, *_: (0, 0, 0, j))
+    gspec = pl.BlockSpec(memory_space=pl.ANY)
     gshape = jax.ShapeDtypeStruct((parts, seq_ways // 2, rows, 3 * cols), bf16)
     ins = [grad, naT, w_qkv] + ([] if acc is None else [acc])
     in_specs = [whole(grad.shape), whole(naT.shape)]
@@ -833,120 +848,343 @@
                 gspec,
                 gspec,
             ],
-            scratch_shapes=[pltpu.VMEM((2, DH // 2, frames), f32)],
+            scratch_shapes=[
+                pltpu.VMEM((2, DH // 2, frames), f32),
+                pltpu.VMEM((2,) + gshape.shape, bf16),
+                pltpu.SemaphoreType.DMA((2, 3)),
+            ],
         ),
-        cost_estimate=pl.CostEstimate(
-            flops=12 * frames * width * cols, bytes_accessed=20 * frames * width, transcendentals=0
-        ),
+        compiler_params=pltpu.CompilerParams(vmem_limit_bytes=48 << 20),
+        cost_estimate=cost(100),
         name="back_block",
     )(lengths, ids, drop, *ins)
 
 
-def tail_kernel(
-    utts,
-    seq_ways,
-    lengths_ref,
-    ids_ref,
-    acc_ref,
-    hidden_ref,
-    after_ref,
-    mods_ref,
-    joinedT_ref,
-    w_skip_ref,
-    tables_ref,
-    grad_a_ref,
-    grad_b_ref,
-    keep_ref,
-    send_ref,
-    gh_ref,
+def norm_kernel(
+    utts, heads_local, lengths_ref, ids_ref, acc_ref, hidden_ref, after_ref, mods_ref, loss_ref, mid_ref, *refs
 ):
     f32, bf16 = jnp.float32, jnp.bfloat16
-    step = pl.program_id(0)
+    bias_refs, (gh_ref, small_ref) = refs[:heads_local], refs[heads_local:]
     frames, width = hidden_ref.shape
-    core = ids_ref[0]
-    parts = keep_ref.shape[0]
-    block = 2 * width // seq_ways
-    rows = block // parts
-
-    @pl.when(step == 0)
-    def _():
-        hot = onehot_rows(lengths_ref, utts, 16, ids_ref[1] * frames, frames)
-        cols = frame_columns(hot, jnp.zeros((1, frames), f32))
-        madd = mods_operand(mods_ref)
-        scale = dot(cols, madd[:, width:])
-        gna = acc_ref[...].T
-        normed, rstd = norm_stats(hidden_ref[...])
-        sums = sum_rows(hot, 16, frames)
-        tables_ref[:, 0:width] = dot(sums, gna.astype(bf16))
-        tables_ref[:, width : 2 * width] = dot(sums, (gna * normed).astype(bf16))
-        gh = (after_ref[...] + norm_back(gna * (1.0 + scale), normed, rstd)).astype(bf16)
-        gh_ref[...] = gh
-        tables_ref[:, 2 * width : 3 * width] = dot(sums, gh)
-
-    gh = gh_ref[...]
-    grad_w = dot(joinedT_ref[...], gh).astype(bf16)
-    blocks = width // block
-    for b in range(blocks):
-        for k in range(parts):
-            tile = grad_w[b * block + k * rows : b * block + (k + 1) * rows]
-
-            @pl.when(core == b % 2)
-            def _():
-                keep_ref[k, b // 2] = tile
-
-            @pl.when(core != b % 2)
-            def _():
-                send_ref[k, b // 2] = tile
-
-    joined = dot_nt(gh, w_skip_ref[...])
-
-    @pl.when(step == 0)
-    def _():
-        grad_a_ref[...] = joined
-
-    @pl.when(step == 1)
-    def _():
-        grad_b_ref[...] = joined
-
-
-def tail_block(lengths, ids, acc, hidden, after, mods, joinedT, w_skip, seq_ways, parts):
+    pad_u = table_rows(utts)
+    base = 6 * pad_u
+    hot = onehot_rows(lengths_ref, utts, 16, ids_ref[1] * frames, frames)
+    cols = frame_columns(hot, jnp.zeros((1, frames), f32))
+    madd = mods_operand(mods_ref)
+    scale = dot(cols, madd[:, width:])
+    gna = acc_ref[...].T
+    normed, rstd = norm_stats(hidden_ref[...])
+    sums = sum_rows(hot, 16, frames)
+    small_ref[0:pad_u, :] = dot(sums, gna.astype(bf16))[:pad_u]
+    small_ref[pad_u : 2 * pad_u, :] = dot(sums, (gna * normed).astype(bf16))[:pad_u]
+    gh = (after_ref[...] + norm_back(gna * (1.0 + scale), normed, rstd)).astype(bf16)
+    gh_ref[...] = gh
+    small_ref[2 * pad_u : base, :] = mid_ref[0 : 4 * pad_u, :]
+    cols_local = width // heads_local
+    for c in range(heads_local):
+        for p in range(3):
+            small_ref[base + p : base + p + 1, c * cols_local : (c + 1) * cols_local] = bias_refs[c][p, 0:1, :]
+    small_ref[base + 3 : base + 4, :] = dot(sums, gh)[16:17]
+    small_ref[base + 4 : base + 12, :] = mid_ref[4 * pad_u : 4 * pad_u + 8, :]
+    count = jnp.sum(loss_ref[...].astype(f32), axis=1, keepdims=True)
+    small_ref[base + 12 : base + 16, :] = jnp.broadcast_to(count, (4, width))
+
+
+def norm_block(lengths, ids, acc, hidden, after, mods, loss, mid_small, biases):
     frames, width = hidden.shape
     utts = lengths.shape[0]
-    f32, bf16 = jnp.float32, jnp.bfloat16
-    rows = 2 * width // seq_ways // parts
-
-    def whole(shape):
-        return pl.BlockSpec(shape, lambda j, *_: (0,) * len(shape), pipeline_mode=pl.Buffered(1))
-
-    gspec = pl.BlockSpec((parts, seq_ways // 4, rows, width), lambda j, *_: (0, j, 0, 0))
-    gshape = jax.ShapeDtypeStruct((parts, seq_ways // 2, rows, width), bf16)
     out_shape = [
-        jax.ShapeDtypeStruct((32, 3 * width), f32),
-        jax.ShapeDtypeStruct((frames, width), f32),
-        jax.ShapeDtypeStruct((frames, width), f32),
-        gshape,
-        gshape,
+        jax.ShapeDtypeStruct((frames, width), jnp.bfloat16),
+        jax.ShapeDtypeStruct((6 * table_rows(utts) + 16, width), jnp.float32),
     ]
     return pl.pallas_call(
-        functools.partial(tail_kernel, utts, seq_ways),
+        functools.partial(norm_kernel, utts, len(biases)),
         out_shape=out_shape,
         grid_spec=pltpu.PrefetchScalarGridSpec(
             num_scalar_prefetch=2,
-            grid=(2,),
-            in_specs=[whole(a.shape) for a in (acc, hidden, after, mods)]
-            + [
-                pl.BlockSpec((width, frames), lambda j, *_: (j, 0)),
-                pl.BlockSpec((width, width), lambda j, *_: (j, 0)),
-            ],
-            out_specs=[whole(o.shape) for o in out_shape[:3]] + [gspec, gspec],
-            scratch_shapes=[pltpu.VMEM((frames, width), bf16)],
+            grid=(1,),
+            in_specs=[whole_block(a.shape) for a in (acc, hidden, after, mods, loss, mid_small, *biases)],
+            out_specs=[whole_block(o.shape) for o in out_shape],
         ),
         compiler_params=pltpu.CompilerParams(vmem_limit_bytes=48 << 20),
-        cost_estimate=pl.CostEstimate(
-            flops=8 * frames * width * width, bytes_accessed=30 * frames * width, transcendentals=0
+        cost_estimate=cost(50),
+        name="norm_block",
+    )(lengths, ids, acc, hidden, after, mods, loss, mid_small, *biases)
+
+
+def skip_kernel(seq_ways, ids_ref, joinedT_ref, gh_ref, keep_ref, send_ref, grads, sems):
+    step = pl.program_id(0)
+    core = ids_ref[0]
+    parts = keep_ref.shape[0]
+    width = joinedT_ref.shape[0]
+    block = 2 * width // seq_ways
+    rows = block // parts
+    z_step = seq_ways // 4
+    grad_w = dot(joinedT_ref[...], gh_ref[...]).astype(jnp.bfloat16)
+    for b in range(width // block):
+        side = jnp.where(core == b % 2, 0, 1)
+        for k in range(parts):
+            lo = b * block + k * rows
+            grads[side, k, step * z_step + b // 2] = grad_w[lo : lo + rows]
+
+    def copy(side, at):
+        where = (slice(None), pl.ds(at * z_step, z_step))
+        return pltpu.make_async_copy(
+            grads.at[side].at[where], (keep_ref, send_ref)[side].at[where], sems.at[side, at]
+        )
+
+    for side in (1, 0):
+        copy(side, step).start()
+
+    @pl.when(step == 1)
+    def _():
+        for side in (1, 0):
+            for at in range(2):
+                copy(side, at).wait()
+
+
+def skip_block(ids, joinedT, gh, seq_ways, parts):
+    frames, width = gh.shape
+    rows = 2 * width // seq_ways // parts
+    gshape = (parts, seq_ways // 2, rows, width)
+    return pl.pallas_call(
+        functools.partial(skip_kernel, seq_ways),
+        out_shape=[jax.ShapeDtypeStruct(gshape, jnp.bfloat16)] * 2,
+        grid_spec=pltpu.PrefetchScalarGridSpec(
+            num_scalar_prefetch=1,
+            grid=(2,),
+            in_specs=[pl.BlockSpec((width, frames), lambda j, *_: (j, 0)), whole_block(gh.shape)],
+            out_specs=[pl.BlockSpec(memory_space=pl.ANY)] * 2,
+            scratch_shapes=[pltpu.VMEM((2,) + gshape, jnp.bfloat16), pltpu.SemaphoreType.DMA((2, 2))],
         ),
-        name="tail_block",
-    )(lengths, ids, acc, hidden, after, mods, joinedT, w_skip)
+        compiler_params=pltpu.CompilerParams(vmem_limit_bytes=32 << 20),
+        cost_estimate=cost(50),
+        name="skip_block",
+    )(ids, joinedT, gh)
+
+
+def joined_kernel(gh_ref, w_ref, scale_ref, first_ref, second_ref):
+    step = pl.program_id(0)
+    value = dot_nt(gh_ref[...], w_ref[...]) * scale_ref[0:1, 0:1]
+
+    @pl.when(step == 0)
+    def _():
+        first_ref[...] = value
+
+    @pl.when(step == 1)
+    def _():
+        second_ref[...] = value
+
+
+def joined_block(gh, w_skip, scale):
+    frames, width = gh.shape
+    out = jax.ShapeDtypeStruct((frames, width), jnp.float32)
+    return pl.pallas_call(
+        joined_kernel,
+        out_shape=[out, out],
+        grid_spec=pltpu.PrefetchScalarGridSpec(
+            num_scalar_prefetch=0,
+            grid=(2,),
+            in_specs=[
+                whole_block(gh.shape),
+                pl.BlockSpec((width, width), lambda j: (j, 0)),
+                whole_block(scale.shape),
+            ],
+            out_specs=[whole_block(out.shape)] * 2,
+        ),
+        compiler_params=pltpu.CompilerParams(vmem_limit_bytes=32 << 20),
+        cost_estimate=cost(50),
+        name="joined_block",
+    )(gh, w_skip, scale)
+
+
+def add_bf16(left, right):
+    return (left.astype(jnp.float32) + right.astype(jnp.float32)).astype(jnp.bfloat16)
+
+
+def add_kernel(pairs, ids_ref, *refs):
+    for i in range(pairs):
+        refs[2 * pairs + i][...] = add_bf16(refs[2 * i][...], refs[2 * i + 1][...]).reshape(
+            refs[2 * pairs + i].shape
+        )
+
+
+def first_sum(ids, keep, got):
+    _, _, _, z_ways, rows, width = keep.shape
+
+    def source(half, axis, mine):
+        def at(g, z, ids):
+            bit = ids[axis]
+            return half, bit if mine else 1 - bit, g, z, 0, 0
+
+        return pl.BlockSpec((1, 1, 1, 1, rows, width), at)
+
+    order = [(0, 2, False), (1, 3, False), (0, 2, True), (1, 3, True)]
+    out = jax.ShapeDtypeStruct((2, z_ways, rows, width), jnp.bfloat16)
+    return pl.pallas_call(
+        functools.partial(add_kernel, 4),
+        out_shape=[out] * 4,
+        grid_spec=pltpu.PrefetchScalarGridSpec(
+            num_scalar_prefetch=1,
+            grid=(2, z_ways),
+            in_specs=[source(*o) for o in order for _ in range(2)],
+            out_specs=[pl.BlockSpec((1, 1, rows, width), lambda g, z, ids: (g, z, 0, 0))] * 4,
+        ),
+        cost_estimate=cost(20),
+        name="first_sum",
+    )(ids, *([keep, got] * 4))
+
+
+def second_sum(ids, keep_a, got_a, keep_b, got_b):
+    _, z_ways, rows, width = keep_a.shape
+
+    def source(axis, mine):
+        def at(z, ids):
+            bit = ids[axis]
+            return bit if mine else 1 - bit, z, 0, 0
+
+        return pl.BlockSpec((1, 1, rows, width), at)
+
+    order = [(3, False), (2, False), (3, True), (2, True)]
+    out = jax.ShapeDtypeStruct((z_ways, rows, width), jnp.bfloat16)
+    return pl.pallas_call(
+        functools.partial(add_kernel, 4),
+        out_shape=[out] * 4,
+        grid_spec=pltpu.PrefetchScalarGridSpec(
+            num_scalar_prefetch=1,
+            grid=(z_ways,),
+            in_specs=[source(*o) for o in order for _ in range(2)],
+            out_specs=[pl.BlockSpec((1, rows, width), lambda z, ids: (z, 0, 0))] * 4,
+        ),
+        cost_estimate=cost(10),
+        name="second_sum",
+    )(ids, *([keep_a, got_a, keep_b, got_b] * 2))
+
+
+def third_kernel(ids_ref, keep_a, got_a, keep_b, got_b, *outs):
+    for j, out in enumerate(outs):
+        at = ids_ref[4] ^ j
+        out[0] = add_bf16(keep_a[at], got_a[at])
+        out[1] = add_bf16(keep_b[at], got_b[at])
+
+
+def third_sum(ids, keep_a, got_a, keep_b, got_b):
+    z_ways, rows, width = keep_a.shape
+    out = jax.ShapeDtypeStruct((2, rows, width), jnp.bfloat16)
+    return pl.pallas_call(
+        third_kernel,
+        out_shape=[out] * z_ways,
+        grid_spec=pltpu.PrefetchScalarGridSpec(
+            num_scalar_prefetch=1,
+            grid=(1,),
+            in_specs=[whole_block(keep_a.shape)] * 4,
+            out_specs=[whole_block(out.shape)] * z_ways,
+        ),
+        cost_estimate=cost(10),
+        name="third_sum",
+    )(ids, keep_a, got_a, keep_b, got_b)
+
+
+def fourth_kernel(*refs):
+    total = refs[0][...].astype(jnp.float32)
+    for r in refs[1:-1]:
+        total = total + r[...].astype(jnp.float32)
+    refs[-1][...] = total.astype(jnp.bfloat16)
+
+
+def fourth_sum(terms):
+    shape = terms[0].shape
+    return pl.pallas_call(
+        fourth_kernel,
+        out_shape=jax.ShapeDtypeStruct(shape, jnp.bfloat16),
+        grid=(1,),
+        in_specs=[whole_block(shape)] * len(terms),
+        out_specs=whole_block(shape),
+        cost_estimate=cost(10),
+        name="fourth_sum",
+    )(*terms)
+
+
+def place_kernel(streams, plan, ids_ref, scale_ref, *refs):
+    blocks, outs = refs[: 4 * streams], refs[4 * streams :]
+    x, y = ids_ref[2], ids_ref[3]
+    scale = scale_ref[0:1, 0:1]
+    for stream, row, rows, lane, lanes, out, row_of, lane_of in plan:
+        for d in range(4):
+            own_x, own_y = x ^ (d & 1), y ^ (d >> 1)
+            for half in range(2):
+                k = own_x * 2 + own_y if half == 0 else 4 + own_y * 2 + own_x
+                tile = blocks[4 * stream + d][half, row : row + rows, lane : lane + lanes]
+                outs[out][row_of(k), lane_of(k)] = tile.astype(jnp.float32) * scale
+
+
+def place_blocks(ids, scale, streams, plan, shapes):
+    blocks = [b for s in streams for b in s]
+    outs = [jax.ShapeDtypeStruct(s, jnp.float32) for s in shapes]
+    return pl.pallas_call(
+        functools.partial(place_kernel, len(streams), plan),
+        out_shape=outs,
+        grid_spec=pltpu.PrefetchScalarGridSpec(
+            num_scalar_prefetch=1,
+            grid=(1,),
+            in_specs=[whole_block(a.shape) for a in (scale, *blocks)],
+            out_specs=[whole_block(o.shape) for o in outs],
+        ),
+        compiler_params=pltpu.CompilerParams(vmem_limit_bytes=32 << 20),
+        cost_estimate=cost(20),
+        name="place_blocks",
+    )(ids, scale, *blocks)
+
+
+def span(start, size):
+    return pl.ds(pl.multiple_of(start, size), size)
+
+
+def ada_kernel(groups, pad_u, numerator, time_ref, *refs):
+    f32 = jnp.float32
+    parts, (weight_ref, vector_ref, scale_ref) = refs[:groups], refs[groups:]
+    table = pl.program_id(0)
+    base = 6 * pad_u
+    count = parts[0][base + 12 : base + 13, 0:1]
+    for p in parts[1:]:
+        count = count + p[base + 12 : base + 13, 0:1]
+    scale = numerator / count
+    rows = jnp.concatenate([p[pl.ds(pl.multiple_of(table * pad_u, 8), pad_u), :] for p in parts], axis=0) * scale
+    vector_ref[pl.ds(table, 1), :] = jnp.sum(rows, axis=0, keepdims=True)
+    operand = jnp.concatenate(list(split3(rows)), axis=0)
+    weight_ref[...] = dot(time_ref[...], operand)
+
+    @pl.when(table == 0)
+    def _():
+        total = parts[0][base : base + 16, :]
+        for p in parts[1:]:
+            total = total + p[base : base + 16, :]
+        vector_ref[8:24, :] = total * scale
+        scale_ref[...] = jnp.broadcast_to(scale, scale_ref.shape)
+
+
+def ada_block(time3, parts, utts, numerator):
+    pad_u = table_rows(utts)
+    width = parts[0].shape[1]
+    own = time3.shape[0]
+    f32 = jnp.float32
+    return pl.pallas_call(
+        functools.partial(ada_kernel, len(parts), pad_u, numerator),
+        out_shape=[
+            jax.ShapeDtypeStruct((own, 6 * width), f32),
+            jax.ShapeDtypeStruct((24, width), f32),
+            jax.ShapeDtypeStruct((8, 128), f32),
+        ],
+        grid=(6,),
+        in_specs=[whole_block(time3.shape)] + [whole_block(p.shape) for p in parts],
+        out_specs=[
+            pl.BlockSpec((own, width), lambda j: (0, j)),
+            whole_block((24, width)),
+            whole_block((8, 128)),
+        ],
+        cost_estimate=cost(50),
+        name="ada_block",
+    )(time3, *parts)
 
 
 def sum_exchange(value, axis, bit):
@@ -954,55 +1192,56 @@
     return lax.ppermute(value, axis, [(i, i ^ bit) for i in range(ways)])
 
 
-def add_pair(left, right):
-    return (left.astype(jnp.float32) + right.astype(jnp.float32)).astype(jnp.bfloat16)
-
-
-def pick(value, bit, axis=0):
-    return lax.dynamic_index_in_dim(value, bit, axis, keepdims=False)
-
-
 def axis_bits(ways):
     return [1 << i for i in range(ways.bit_length() - 1)]
 
 
-def reduce_blocks(keep, send):
-    seq_ways, batch_ways = lax.axis_size("seq"), lax.axis_size("batch")
-    seq_rank, batch_rank = lax.axis_index("seq"), lax.axis_index("batch")
-    side = 1 << ((batch_ways.bit_length() - 1) // 2)
-    x_bit, y_bit = 1, side
-    x = lax.rem(batch_rank, 2)
-    y = lax.rem(batch_rank // side, 2)
+def reduce_stages(ids, keep, send):
+    batch_ways = lax.axis_size("batch")
+    x_bit, y_bit = 1, 1 << ((batch_ways.bit_length() - 1) // 2)
     _, z_ways, rows, width = keep.shape
-    total = add_pair(keep, sum_exchange(send, "seq", 1)).reshape(2, 2, 2, z_ways, rows, width)
-    first = []
-    for block, mine, bit in ((total[0], x, x_bit), (total[1], y, y_bit)):
-        got = sum_exchange(pick(block, 1 - mine), "batch", bit)
-        first.append(add_pair(pick(block, mine), got))
-    second = []
-    for block, mine, bit in ((first[0], y, y_bit), (first[1], x, x_bit)):
-        got = sum_exchange(pick(block, 1 - mine), "batch", bit)
-        second.append(add_pair(pick(block, mine), got))
-    block = jnp.stack(second)
+    shape = (2, 2, 2, z_ways, rows, width)
+    got = sum_exchange(send, "seq", 1)
+    send_a, send_b, keep_a, keep_b = first_sum(ids, keep.reshape(shape), got.reshape(shape))
+    send_a, send_b = follow([send_a, send_b], (yield [send_a, send_b]))
+    got = [sum_exchange(send_a, "batch", x_bit), sum_exchange(send_b, "batch", y_bit)]
+    got_a, got_b = follow(got, (yield got))
+    send_a, send_b, keep_a, keep_b = second_sum(ids, keep_a, got_a, keep_b, got_b)
+    send_a, send_b = follow([send_a, send_b], (yield [send_a, send_b]))
+    got = [sum_exchange(send_a, "batch", y_bit), sum_exchange(send_b, "batch", x_bit)]
+    got_a, got_b = follow(got, (yield got))
+    own, *away = third_sum(ids, keep_a, got_a, keep_b, got_b)
+    away = follow(away, (yield away))
+    got = [sum_exchange(a, "seq", 2 * (j + 1)) for j, a in enumerate(away)]
+    got = follow(got, (yield got))
+    block = fourth_sum([own] + got)
     for bit in axis_bits(batch_ways):
         if bit not in (x_bit, y_bit):
-            block = add_pair(block, sum_exchange(block, "batch", bit))
-    z = seq_rank // 2
-    for i, bit in enumerate(axis_bits(z_ways)):
-        mine = lax.rem(z // bit, 2)
-        block = block.reshape(2, block.shape[1] // 2, 2, rows, width)
-        got = sum_exchange(pick(block, 1 - mine, 2), "seq", 2 * bit)
-        block = add_pair(pick(block, mine, 2), got)
-    block = block.reshape(2, rows, width)
-    got_x = sum_exchange(block, "batch", x_bit)
-    got_y = sum_exchange(block, "batch", y_bit)
-    got_xy = sum_exchange(block, "batch", x_bit | y_bit)
-    table = jnp.stack([jnp.stack([block, got_y]), jnp.stack([got_x, got_xy])])
-    table = jnp.where(x == 1, table[::-1], table)
-    table = jnp.where(y == 1, table[:, ::-1], table)
-    return jnp.concatenate(
-        [table[:, :, 0].reshape(4, rows, width), jnp.swapaxes(table[:, :, 1], 0, 1).reshape(4, rows, width)]
-    ).astype(jnp.float32)
+            block = add_bf16(block, sum_exchange(block, "batch", bit))
+    (block,) = follow([block], (yield [block]))
+    yield [block] + [sum_exchange(block, "batch", bit) for bit in (x_bit, y_bit, x_bit | y_bit)]
+
+
+def advance(stages, steps, token=None):
+    value = stages.send(token)
+    for _ in range(steps - 1):
+        value = next(stages)
+    return value
+
+
+def last_stage(stages, token=None):
+    value = stages.send(token)
+    for value in stages:
+        pass
+    return value
+
+
+def follow(values, token):
+    return values if token is None else [after(v, token) for v in values]
+
+
+def after(value, *others):
+    return lax.optimization_barrier((value,) + others)[0]
 
 
 def gather_groups(value):
@@ -1046,7 +1285,10 @@
     heads_local = HEADS // seq_ways
     utts = lengths.shape[1]
     lengths_row, drop = lengths[0], drop_mask[0]
-    ids = jnp.stack([lax.rem(seq_rank, 2), seq_rank]).astype(jnp.int32)
+    batch_rank = lax.axis_index("batch")
+    side = 1 << ((batch_ways.bit_length() - 1) // 2)
+    ids = [lax.rem(seq_rank, 2), seq_rank, lax.rem(batch_rank, 2), lax.rem(batch_rank // side, 2), seq_rank // 2]
+    ids = jnp.stack(ids).astype(jnp.int32)
     ok = key_mask.reshape(seq_ways, 1, frames)
     exchange = functools.partial(lax.all_to_all, axis_name="seq", split_axis=0, concat_axis=0, tiled=True)
 
@@ -1067,24 +1309,24 @@
         packed = qkv_block(lengths_row, ids, drop, na, w_qkv, b_qkv[None], c, seq_ways)
         received.append(exchange(packed))
 
-    count = jnp.sum(loss_mask.astype(f32))
-    count = sum_seq(jnp.full((8, 128), count))
-    for bit in axis_bits(batch_ways):
-        count = count + sum_exchange(count, "batch", bit)
-    scale = (group_frames * batch_ways) / count[0, :1]
     mods_rest = modulation(2 * width, 6 * width)
-    time_all = jnp.concatenate(gather_groups(time_act))
-
+    own = width // seq_ways
+    pad_u = table_rows(utts)
+    time_own = lax.dynamic_slice_in_dim(jnp.concatenate(gather_groups(time_rows[:pad_u])), seq_rank * own, own, axis=1)
+    time3 = jnp.tile(time_own.T, (1, 3))
+
+    received[0] = after(received[0], mods_rest)
     head_out, log_totals, returned = [], [], []
     for c in range(heads_local):
         out, log_total = attend(lengths_row, received[c], ok)
         head_out.append(out)
         log_totals.append(log_total)
-        returned.append(exchange(out))
+        returned.append(exchange(after(out, *returned)))
+        if c < heads_local - 1:
+            received[c + 1] = after(received[c + 1], out)
     mid = mid_block(
         lengths_row,
         ids,
-        scale,
         returned,
         hidden,
         mods_rest,
@@ -1098,84 +1340,105 @@
         b_down[None],
         PARTS,
     )
-    output, after_grad, tables, b_up_grad = mid[:4]
-    grad_att = mid[4 : 4 + heads_local]
-    keep_f, send_f = mid[4 + heads_local :]
+    output, after_grad, mid_small = mid[:3]
+    grad_att = mid[3 : 3 + heads_local]
     grad_heads = [exchange(g) for g in grad_att]
-    feed = reduce_blocks(keep_f, send_f)
-    early = jnp.concatenate([tables[:utts, : 4 * width].reshape(-1), b_up_grad[0], tables[16, 4 * width :]])
-    early = early.reshape(-1, 2 * width)
-    early = gather_groups(sum_seq(early))
-
-    acc, part_biases, part_blocks = None, [], []
+    up = reduce_stages(ids, *mid[3 + heads_local : 5 + heads_local])
+    down = reduce_stages(ids, *mid[5 + heads_local :])
+
+    ahead = advance(up, 1) + advance(down, 1)
     grad_local = []
     for c in range(heads_local):
-        grad = attend_back(lengths_row, received[c], ok, head_out[c], grad_heads[c], log_totals[c])
-        grad_local.append(exchange(grad))
+        operand = after(grad_heads[c], *ahead)
+        moving = advance(up, 1)
+        if c > 0:
+            moving = moving + advance(down, 1)
+        grad = attend_back(lengths_row, received[c], ok, head_out[c], operand, log_totals[c])
+        grad_local.append(exchange(after(grad, *moving, *grad_heads[c + 1 :])))
+        ahead = [grad] + advance(up, 1, grad)
+    ahead = ahead + (advance(down, 1, grad) if heads_local > 1 else advance(down, 2))
+    acc, biases, part_blocks = None, [], []
     for c in range(heads_local):
         acc, bias, keep, send = back_block(
-            lengths_row, ids, drop, grad_local[c], naT, w_qkv, acc, c, PARTS
+            lengths_row, ids, drop, after(grad_local[c], *ahead), naT, w_qkv, acc, c, PARTS
         )
-        part_biases.append(bias[:, 0])
-        part_blocks.append(reduce_blocks(keep, send))
-    late_tables, grad_tokens, grad_skip, keep, send = tail_block(
-        lengths_row, ids, acc, hidden, after_grad, mods_a, joinedT, w_skip, seq_ways, PARTS
-    )
-    skip_blocks = reduce_blocks(keep, send)
-    late = jnp.concatenate(
-        [
-            late_tables[:utts, : 2 * width].reshape(-1),
-            jnp.stack(part_biases, axis=1).reshape(-1),
-            late_tables[16, 2 * width :],
-        ]
-    ).reshape(-1, 2 * width)
-    late = gather_groups(sum_seq(late))
-
-    ada_rows = width // seq_ways
-    own_time = lax.dynamic_slice_in_dim(time_all, seq_rank * ada_rows, ada_rows, axis=1).astype(f32)
-
-    def own_slice(vector):
-        size = vector.shape[0] // seq_ways
-        return lax.dynamic_slice_in_dim(vector, seq_rank * size, size)
-
-    def ada_part(groups, tables_count):
-        rows = jnp.concatenate(
-            [g.reshape(-1)[: utts * tables_count * width].reshape(utts, -1) for g in groups]
-        )
-        weight = lax.dot_general(
-            own_time, rows, (((0,), (0,)), ((), ())), precision=lax.Precision.HIGHEST
-        )
-        return weight, jnp.sum(rows, axis=0)
-
-    early_weight, early_bias = ada_part(early, 4)
-    late_weight, late_bias = ada_part(late, 2)
-    grad_w_ada = jnp.concatenate([late_weight, early_weight], axis=1)
-    grad_b_ada = own_slice(jnp.concatenate([late_bias, early_bias]))
-    early_vec = sum(g.reshape(-1)[utts * 4 * width :] for g in early)
-    late_vec = sum(g.reshape(-1)[utts * 2 * width :] for g in late)
+        biases.append(bias)
+        part_blocks.append(reduce_stages(ids, keep, send))
+        ahead = advance(down, 2) if c == 0 else []
+        ahead = ahead + advance(part_blocks[c], 1)
+    if heads_local == 1:
+        advance(up, 2)
+    gh, small = norm_block(lengths_row, ids, acc, hidden, after_grad, mods_a, loss_mask, mid_small, biases)
+    ahead = ahead + [x for blocks in part_blocks[:-1] for x in advance(blocks, 2)]
+    keep, send = skip_block(ids, joinedT, after(gh, *ahead), seq_ways, PARTS)
+    skip_blocks = reduce_stages(ids, keep, send)
+    token = advance(skip_blocks, 1)[0]
+    groups = gather_groups(sum_seq(small))
+    numerator = float(group_frames * batch_ways)
+    grad_w_ada, vectors, scale = ada_block(time3, groups, utts, numerator)
+    grad_tokens, grad_skip = joined_block(gh, w_skip, scale)
+    up, down = last_stage(up, token), last_stage(down, token)
+    part_blocks = [last_stage(b, token) for b in part_blocks]
+    skip_blocks = last_stage(skip_blocks)
+
     ff = w_up.shape[1]
-    grad_b_up = own_slice(early_vec[:ff])
-    grad_b_out = own_slice(early_vec[ff : ff + width])
-    grad_b_down = own_slice(early_vec[ff + width :])
-    grad_b_qkv = own_slice(late_vec[: 3 * width])
-    grad_b_skip = own_slice(late_vec[3 * width :])
-
-    own = width // seq_ways
     chunks = ff // width
     up_part = chunks * own // PARTS
     down_part = ff // seq_ways // PARTS
-    halves = own // up_part
-    grad_w_up = (
-        feed[:, :up_part]
-        .reshape(chunks, halves, up_part, width)
-        .transpose(1, 2, 0, 3)
-        .reshape(own, ff)
+    out_part = own // PARTS
+    per_chunk = own // up_part
+    whole_lanes = lambda k: span(0, width)
+    grad_w_up, grad_w_down, grad_w_out = place_blocks(
+        ids,
+        scale,
+        [up, down],
+        [
+            (
+                *(0, 0, up_part, 0, width, 0),
+                lambda k: span(lax.rem(k, per_chunk) * up_part, up_part),
+                lambda k: span(k // per_chunk * width, width),
+            ),
+            (1, 0, down_part, 0, width, 1, lambda k: span(k * down_part, down_part), whole_lanes),
+            (1, down_part, out_part, 0, width, 2, lambda k: span(k * out_part, out_part), whole_lanes),
+        ],
+        [(own, ff), (ff // seq_ways, width), (own, width)],
     )
-    grad_w_down = feed[:, up_part : up_part + down_part].reshape(ff // seq_ways, width)
-    grad_w_out = feed[:, up_part + down_part :].reshape(own, width)
     cols = seq_ways * HEAD_DIM
-    grad_w_qkv = jnp.stack([b.reshape(own, 3, cols) for b in part_blocks], axis=2).reshape(own, 3 * width)
-    grad_w_skip = skip_blocks.reshape(2 * own, width)
+    (grad_w_qkv,) = place_blocks(
+        ids,
+        scale,
+        part_blocks,
+        [
+            (
+                *(c, 0, out_part, p * cols, cols, 0),
+                lambda k: span(k * out_part, out_part),
+                lambda k, at=p * width + c * cols: span(at, cols),
+            )
+            for c in range(heads_local)
+            for p in range(3)
+        ],
+        [(own, 3 * width)],
+    )
+    skip_part = 2 * own // PARTS
+    (grad_w_skip,) = place_blocks(
+        ids,
+        scale,
+        [skip_blocks],
+        [(0, 0, skip_part, 0, width, 0, lambda k: span(k * skip_part, skip_part), whole_lanes)],
+        [(2 * own, width)],
+    )
+
+    def own_slice(vector):
+        vector = vector.reshape(-1)
+        size = vector.shape[0] // seq_ways
+        return lax.dynamic_slice_in_dim(vector, seq_rank * size, size)
+
+    grad_b_ada = own_slice(vectors[:6])
+    grad_b_qkv = own_slice(vectors[8:11])
+    grad_b_skip = own_slice(vectors[11])
+    grad_b_out = own_slice(vectors[12])
+    grad_b_down = own_slice(vectors[13])
+    grad_b_up = own_slice(vectors[14 : 14 + chunks])
     return (
         output[None],
         grad_tokens[None],

time: 716 us -> 616 us (0.86)
  waiting for transfers between devices: 253 us -> 138 us
  Pallas kernels: 226 us -> 293 us
  other arithmetic: 42.2 us -> 2.53 us
  starting transfers between devices: 104 us -> 129 us
  blocking collectives: 19.5 us -> 0 us
  local copies, waits for them, and re-layouts: 49.5 us -> 31.2 us
    ppermute x60 -> x64, waiting for transfers between devices: 203 us -> 72.7 us  [sum_exchange(): return lax.ppermute(value, axis, [(i, i ^ bit) for i in range(ways)])]
    pallas_call x1 -> x27, Pallas kernels: 15.1 us -> 109 us  [the longest x5 36.9 us: first_sum(): pl.pallas_call(functools.partial(add_kernel, 4), out_shape=[out] * 4, gri...]
    convert_element_type x26 -> x0, other arithmetic: 25 us -> none  [the longest x24 22.2 us: add_pair(): (left.astype(jnp.float32) + right.astype(jnp.float32)).astype(jnp.bfloat16)]
    ppermute x60 -> x64, starting transfers between devices: 73.6 us -> 93.6 us  [sum_exchange(): return lax.ppermute(value, axis, [(i, i ^ bit) for i in range(ways)])]
    all_to_all x1 -> x0, blocking collectives: 19.5 us -> none  [shards(): grad_heads = [exchange(g) for g in grad_att]]
    all_to_all x4, waiting for transfers between devices: 5.94 us -> 22.2 us  [the longest x2 13.6 us: shards(): returned.append(exchange(after(out, *returned)))]
    pallas_call x2, Pallas kernels: 63.8 us -> 51.7 us  [attend_back(): pl.pallas_call(functools.partial(bwd_kernel, utts), out_shape=jax.ShapeDt...]
    unnamed x93 -> x176, local copies, waits for them, and re-layouts: 13 us -> 23.6 us
  transfers between devices with their start and end apart: 67 -> 72, of which waited for: 39 -> 20; matrix products, arithmetic and copies ran while one was open for 11% -> 2% of each run, Pallas kernels for 23% -> 34%
where the time goes in v4:
time: 616 us; the launch traced here: 605 us
  Pallas kernels  293 us (48%)
  waiting for transfers between devices  138 us (22%)
  starting transfers between devices  129 us (21%)
  local copies, waits for them, and re-layouts  31.2 us (5%)
  matrix products  8.31 us (1%)
    ppermute x64, starting transfers between devices, sum_exchange(): return lax.ppermute(value, axis, [(i, i ^ bit) for i in range(ways)])  93.6 us
    ppermute x64, waiting for transfers between devices, sum_exchange(): return lax.ppermute(value, axis, [(i, i ^ bit) for i in range(ways)])  72.7 us
    pallas_call x2, Pallas kernels, attend_back(): pl.pallas_call(functools.partial(bwd_kernel, utts), out_shape=jax.ShapeDt...  51.7 us
    pallas_call x1, Pallas kernels, mid_block(): pl.pallas_call(functools.partial(mid_kernel, (seq_ways, heads_local, utts...  51.1 us
    all_to_all x2, waiting for transfers between devices, shards(): received.append(exchange(packed))  43.4 us
    pallas_call x2, Pallas kernels, attend(): pl.pallas_call(functools.partial(fwd_kernel, utts), out_shape=(jax.ShapeD...  40.2 us
    pallas_call x5, Pallas kernels, first_sum(): pl.pallas_call(functools.partial(add_kernel, 4), out_shape=[out] * 4, gri...  36.9 us
    unnamed x176, local copies, waits for them, and re-layouts  23.6 us
  transfers between devices with their start and end apart: 72, of which 20 were waited for; matrix products, arithmetic and copies ran while one was open for 2% of the time, Pallas kernels for 34%

profile of v4, /device:TPU:0, one launch (start us, length us, event | category | flops | bytes accessed | tf_op | source)
XLA Modules:
  0.0 604.9 jit_solution(4084342357217419366)
XLA Ops:
  8.5 7.9 %head_block.1 = (f32[512,1024]{1,0:T(8,128)}, bf16[2048,512]{1,0:T(8,128)(2,1)}, bf16[1024,512]{1,0:T(8,128)(2,1)S(1)}, bf16[512,1024]{1,0:T(8,128)(2,1)S(1)}) custom-call(s32[8]{0:T(128)S(1)} %bitcast.79, s32[5]{0:T(128)S(1)} %stack.23.ids_ref, s32[8]{0:T(128)S(1)} %bitcast.69, bf16[512,1024]{1,0:T(8,128)(2,1)S(1)} %bitcast.64, ...), custom_call_target="tpu_custom_call" | custom-call | flops 10000000000 | bytes 10000000 | tf_op jit(solution)/shard_map/head_block/pallas_call | solution.py:679
  18.4 6.8 %qkv_block.2 = bf16[8,192,512]{2,1,0:T(8,128)(2,1)} custom-call(s32[8]{0:T(128)} %bitcast.72, s32[5]{0:T(128)} %copy-done.5, s32[8]{0:T(128)} %bitcast.67, bf16[512,1024]{1,0:T(8,128)(2,1)} %copy-done.29, bf16[1024,3072]{1,0:T(8,128)(2,1)} %w_ref.8, bf16[1,3072]{1,0:T(2,128)(2,1)} %broadcast_in_dim.28.b_ref), custom_call_target="tpu_custom_call" | custom-call | flops 7500000256 | bytes 7500000 | tf_op jit(solution)/shard_map/qkv_block/pallas_call | solution.py:732
  31.6 6.8 %qkv_block.3 = bf16[8,192,512]{2,1,0:T(8,128)(2,1)} custom-call(s32[8]{0:T(128)} %bitcast.73, s32[5]{0:T(128)} %copy-done.5, s32[8]{0:T(128)} %bitcast.68, bf16[512,1024]{1,0:T(8,128)(2,1)} %copy-done.29, bf16[1024,3072]{1,0:T(8,128)(2,1)} %w_ref.8, bf16[1,3072]{1,0:T(2,128)(2,1)} %broadcast_in_dim.28.b_ref), custom_call_target="tpu_custom_call" | custom-call | flops 7500000256 | bytes 7500000 | tf_op jit(solution)/shard_map/qkv_block/pallas_call | solution.py:732
  38.4 31.1 %all-to-all-done.qkv_ref = bf16[8,192,512]{2,1,0:T(8,128)(2,1)S(1)} async-done(((bf16[8,192,512]{2,1,0:T(8,128)(2,1)}), bf16[8,192,512]{2,1,0:T(8,128)(2,1)S(1)}, u32[]{:S(2)}, u32[]{:S(2)}) %all-to-all-start) | async-done | bytes 1572896 | tf_op jit(solution)/shard_map/all_to_all | solution.py:1310
  78.4 20.1 %attend.2 = (bf16[8,64,512]{2,1,0:T(8,128)(2,1)}, f32[8,1,512]{2,1,0:T(1,128)}) custom-call(s32[8]{0:T(128)} %bitcast.74, bf16[8,192,512]{2,1,0:T(8,128)(2,1)} %copy-done.44, s32[8,1,512]{2,1,0:T(1,128)} %bitcast.102), custom_call_target="tpu_custom_call" | custom-call | flops 24999999488 | bytes 25000000 | tf_op jit(solution)/shard_map/attend/pallas_call | solution.py:135
  98.4 12.4 %all-to-all-done.2.qkv_ref = bf16[8,192,512]{2,1,0:T(8,128)(2,1)S(1)} async-done(((bf16[8,192,512]{2,1,0:T(8,128)(2,1)}), bf16[8,192,512]{2,1,0:T(8,128)(2,1)S(1)}, u32[]{:S(2)}, u32[]{:S(2)}) %all-to-all-start.2) | async-done | bytes 1572896 | tf_op jit(solution)/shard_map/all_to_all | solution.py:1310
  114.4 20.2 %attend.3 = (bf16[8,64,512]{2,1,0:T(8,128)(2,1)}, f32[8,1,512]{2,1,0:T(1,128)}) custom-call(s32[8]{0:T(128)} %bitcast.75, bf16[8,192,512]{2,1,0:T(8,128)(2,1)} %copy-done.43, s32[8,1,512]{2,1,0:T(1,128)} %bitcast.103), custom_call_target="tpu_custom_call" | custom-call | flops 24999999488 | bytes 25000000 | tf_op jit(solution)/shard_map/attend/pallas_call | solution.py:135
  141.6 13.6 %all-to-all-done.3.refs_1_ = bf16[8,64,512]{2,1,0:T(8,128)(2,1)} async-done(((bf16[8,64,512]{2,1,0:T(8,128)(2,1)}), bf16[8,64,512]{2,1,0:T(8,128)(2,1)}, u32[]{:S(2)}, u32[]{:S(2)}) %all-to-all-start.3) | async-done | bytes 524320 | tf_op jit(solution)/shard_map/all_to_all | solution.py:1324
  155.2 51.1 %mid_block.1 = (bf16[512,1024]{1,0:T(8,128)(2,1)}, f32[512,1024]{1,0:T(8,128)}, f32[40,1024]{1,0:T(8,128)}, bf16[8,64,512]{2,1,0:T(8,128)(2,1)}, bf16[8,64,512]{...) custom-call(s32[8]{0:T(128)} %bitcast.76, ...), custom_call_target="tpu_custom_call" | custom-call | flops 49999998976 | bytes 50000000 | tf_op jit(solution)/shard_map/mid_block/pallas_call | solution.py:550
  211.3 10.1 %collective-permute-done = bf16[8,4,64,1024]{3,2,1,0:T(8,128)(2,1)} collective-permute-done((bf16[8,4,64,1024]{3,2,1,0:T(8,128)(2,1)}, bf16[8,4,64,1024]{3,2,1,0:T(8,128)(2,1)}, u32[]{:S(2)}, u32[]{:S(2)}) %collective-permute-start) | collective-permute-done | bytes 4194336 | tf_op jit(solution)/shard_map/ppermute | solution.py:1192
  221.4 8.2 %first_sum.5 = (bf16[2,4,64,1024]{3,2,1,0:T(8,128)(2,1)}, bf16[2,4,64,1024]{3,2,1,0:T(8,128)(2,1)}, bf16[2,4,64,1024]{3,2,1,0:T(8,128)(2,1)}, bf16[2,4,64,1024]{3,2,1,0:T(8,128)(2,1)}) custom-call(s32[5]{0:T(128)} %copy-done.5, bf16[2,2,2,4,64,1024]{5,4,3,2,1,0:T(8,128)(2,1)} %bitcast.87, ...), custom_call_target="tpu_custom_call" | custom-call | flops 2000000000 | bytes 2000000 | tf_op jit(solution)/shard_map/first_sum/pallas_call | solution.py:1024
  235.9 9.1 %first_sum.6 = (bf16[2,4,80,1024]{3,2,1,0:T(8,128)(2,1)}, bf16[2,4,80,1024]{3,2,1,0:T(8,128)(2,1)}, bf16[2,4,80,1024]{3,2,1,0:T(8,128)(2,1)}, bf16[2,4,80,1024]{3,2,1,0:T(8,128)(2,1)}) custom-call(s32[5]{0:T(128)} %copy-done.5, bf16[2,2,2,4,80,1024]{5,4,3,2,1,0:T(8,128)(2,1)} %bitcast.83, ...), custom_call_target="tpu_custom_call" | custom-call | flops 2000000000 | bytes 2000000 | tf_op jit(solution)/shard_map/first_sum/pallas_call | solution.py:1024
  251.4 25.8 %attend_back.2 = bf16[8,192,512]{2,1,0:T(8,128)(2,1)} custom-call(s32[8]{0:T(128)} %bitcast.77, bf16[8,192,512]{2,1,0:T(8,128)(2,1)} %copy-done.44, s32[8,1,512]{2,1,0:T(1,128)} %bitcast.104, bf16[8,64,512]{2,1,0:T(8,128)(2,1)} %get-tuple-element.140.o_ref, bf16[8,64,512]{2,1,0:T(8,128)(2,1)} %all-to-all-done.5.do_ref, f32[8,1,512]{2,1,0:T(1,128)} %get-tuple-element.157.lse_ref), custom_call_target="tpu_custom_call" | custom-call | flops 32000000000 | bytes 32000000 | tf_op jit(solution)/shard_map/attend_back/pallas_call | solution.py:257
  283.5 8.1 %collective-permute-start.5 = (bf16[4,64,1024]{2,1,0:T(8,128)(2,1)}, bf16[4,64,1024]{2,1,0:T(8,128)(2,1)}, u32[]{:S(2)}, u32[]{:S(2)}) collective-permute-start(bf16[4,64,1024]{2,1,0:T(8,128)(2,1)} %get-tuple-element.163), channel_id=1, source_target_pairs={{0,8},{8,0},{16,24},{24,16},{1,9},{9,1},{17,25},{25,17},{2,10},{10... | collective-permute-start | bytes 1572872 | tf_op jit(solution)/shard_map/ppermute | solution.py:1192
  296.6 25.8 %attend_back.3 = bf16[8,192,512]{2,1,0:T(8,128)(2,1)} custom-call(s32[8]{0:T(128)} %bitcast.78, bf16[8,192,512]{2,1,0:T(8,128)(2,1)} %copy-done.43, s32[8,1,512]{2,1,0:T(1,128)} %bitcast.105, bf16[8,64,512]{2,1,0:T(8,128)(2,1)} %get-tuple-element.143.o_ref, bf16[8,64,512]{2,1,0:T(8,128)(2,1)} %all-to-all-done.4.do_ref, f32[8,1,512]{2,1,0:T(1,128)} %get-tuple-element.165.lse_ref), custom_call_target="tpu_custom_call" | custom-call | flops 32000000000 | bytes 32000000 | tf_op jit(solution)/shard_map/attend_back/pallas_call | solution.py:257
  325.8 8.6 %all-to-all-done.7.grad_ref = bf16[8,192,512]{2,1,0:T(8,128)(2,1)S(1)} async-done(((bf16[8,192,512]{2,1,0:T(8,128)(2,1)}), bf16[8,192,512]{2,1,0:T(8,128)(2,1)S(1)}, u32[]{:S(2)}, u32[]{:S(2)}) %all-to-all-start.7) | async-done | bytes 1572896 | tf_op jit(solution)/shard_map/all_to_all | solution.py:1357
  344.6 9.8 %back_block.2 = (f32[1024,512]{1,0:T(8,128)}, f32[3,8,512]{2,1,0:T(8,128)S(1)}, bf16[8,4,16,1536]{3,2,1,0:T(8,128)(2,1)S(1)}, bf16[8,4,16,1536]{3,2,1,0:T(8,128)(2,1)}) custom-call(s32[8]{0:T(128)S(1)} %bitcast.80, s32[5]{0:T(128)S(1)} %copy-done.6, s32[8]{0:T(128)S(1)} %bitcast.70, bf16[8,192,512]{2,1,0:T(8,128)(2,1)S(1)} %all-to-all-done.7.grad_ref, ...), custom_call_target="tpu_custom_call" | custom-call | flops 10000000000 | bytes 10000000 | tf_op jit(solution)/shard_map/back_block/pallas_call | solution.py:833
  358.1 14.9 %collective-permute-done.8.got_a = bf16[4,80,1024]{2,1,0:T(8,128)(2,1)S(1)} collective-permute-done((bf16[4,80,1024]{2,1,0:T(8,128)(2,1)S(1)}, bf16[4,80,1024]{2,1,0:T(8,128)(2,1)S(1)}, u32[]{:S(2)}, u32[]{:S(2)}) %collective-permute-start.8) | collective-permute-done | bytes 655392 | tf_op jit(solution)/shard_map/ppermute | solution.py:1192
  387.8 10.3 %back_block.3 = (f32[1024,512]{1,0:T(8,128)}, f32[3,8,512]{2,1,0:T(8,128)S(1)}, bf16[8,4,16,1536]{3,2,1,0:T(8,128)(2,1)S(1)}, bf16[8,4,16,1536]{3,2,1,0:T(8,128)(2,1)S(1)}) custom-call(s32[8]{0:T(128)S(1)} %bitcast.81, s32[5]{0:T(128)S(1)} %copy-done.7, s32[8]{0:T(128)S(1)} %bitcast.71, bf16[8,192,512]{2,1,0:T(8,128)(2,1)S(1)} %all-to-all-done.6.grad_ref, ...), custom_call_target="tpu_custom_call" | custom-call | flops 10000000000 | bytes 10000000 | tf_op jit(solution)/shard_map/back_block/pallas_call | solution.py:833
  433.7 6.6 %collective-permute-done.15 = f32[64,1024]{1,0:T(8,128)S(1)} collective-permute-done((f32[64,1024]{1,0:T(8,128)S(1)}, f32[64,1024]{1,0:T(8,128)S(1)}, u32[]{:S(2)}, u32[]{:S(2)}) %collective-permute-start.15) | collective-permute-done | bytes 262176 | tf_op jit(solution)/shard_map/ppermute | solution.py:1192
  444.3 6.8 %first_sum.9 = (bf16[2,4,32,1024]{3,2,1,0:T(8,128)(2,1)}, bf16[2,4,32,1024]{3,2,1,0:T(8,128)(2,1)}, bf16[2,4,32,1024]{3,2,1,0:T(8,128)(2,1)}, bf16[2,4,32,1024]{3,2,1,0:T(8,128)(2,1)}) custom-call(s32[5]{0:T(128)} %copy-done.5, bf16[2,2,2,4,32,1024]{5,4,3,2,1,0:T(8,128)(2,1)} %bitcast.52, bf16[2,2,2,4,32,1024]{5,4,3,2,1,0:T(8,128)(2,1)} %bitcast.91, ...), custom_call_target="tpu_custom_call" | custom-call | flops 2000000000 | bytes 2000000 | tf_op jit(solution)/shard_map/first_sum/pallas_call | solution.py:1024
  514.4 12.8 %collective-permute-done.59.refs_2_ = bf16[2,80,1024]{2,1,0:T(8,128)(2,1)} collective-permute-done((bf16[2,80,1024]{2,1,0:T(8,128)(2,1)}, bf16[2,80,1024]{2,1,0:T(8,128)(2,1)}, u32[]{:S(2)}, u32[]{:S(2)}) %collective-permute-start.59) | collective-permute-done | bytes 327712 | tf_op jit(solution)/shard_map/ppermute | solution.py:1192
  546.4 8.0 %collective-permute-done.56.refs_2_ = bf16[2,64,1024]{2,1,0:T(8,128)(2,1)S(1)} collective-permute-done((bf16[2,64,1024]{2,1,0:T(8,128)(2,1)S(1)}, bf16[2,64,1024]{2,1,0:T(8,128)(2,1)S(1)}, u32[]{:S(2)}, u32[]{:S(2)}) %collective-permute-start.56) | collective-permute-done | bytes 262176 | tf_op jit(solution)/shard_map/ppermute | solution.py:1192
  560.2 9.5 %collective-permute-start.47 = (bf16[2,16,1536]{2,1,0:T(8,128)(2,1)}, bf16[2,16,1536]{2,1,0:T(8,128)(2,1)S(1)}, u32[]{:S(2)}, u32[]{:S(2)}) collective-permute-start(bf16[2,16,1536]{2,1,0:T(8,128)(2,1)} %get-tuple-element.248), channel_id=1, source_target_pairs={{0,4},{1,5},{2,6},{3,7},{4,0},{5,1},{6,2},{7,3},{8,12},{9,13},{10,... | collective-permute-start | bytes 294920 | tf_op jit(solution)/shard_map/ppermute | solution.py:1192
  (360 shorter events, 258.7 us)
Async XLA Ops:
  25.2 44.3 %all-to-all-start = ((bf16[8,192,512]{2,1,0:T(8,128)(2,1)}), bf16[8,192,512]{2,1,0:T(8,128)(2,1)S(1)}, u32[]{:S(2)}, u32[]{:S(2)}) async-start(bf16[8,192,512]{2,1,0:T(8,128)(2,1)} %qkv_block.2), calls=%async_computation | async-start | bytes 3145728 | tf_op jit(solution)/shard_map/all_to_all | solution.py:1310
  69.5 41.3 %all-to-all-start.2 = ((bf16[8,192,512]{2,1,0:T(8,128)(2,1)}), bf16[8,192,512]{2,1,0:T(8,128)(2,1)S(1)}, u32[]{:S(2)}, u32[]{:S(2)}) async-start(bf16[8,192,512]{2,1,0:T(8,128)(2,1)} %qkv_block.3), calls=%async_computation.2 | async-start | bytes 3145728 | tf_op jit(solution)/shard_map/all_to_all | solution.py:1310
  110.8 23.7 %all-to-all-start.1 = ((bf16[8,64,512]{2,1,0:T(8,128)(2,1)}), bf16[8,64,512]{2,1,0:T(8,128)(2,1)S(1)}, u32[]{:S(2)}, u32[]{:S(2)}) async-start(bf16[8,64,512]{2,1,0:T(8,128)(2,1)} %get-tuple-element.140.o_ref), calls=%async_computation.1 | async-start | bytes 1048576 | tf_op jit(solution)/shard_map/all_to_all | solution.py:1324
  206.3 29.6 %collective-permute-start.1 = (bf16[8,4,80,1024]{3,2,1,0:T(8,128)(2,1)}, bf16[8,4,80,1024]{3,2,1,0:T(8,128)(2,1)}, u32[]{:S(2)}, u32[]{:S(2)}) collective-permute-start(bf16[8,4,80,1024]{3,2,1,0:T(8,128)(2,1)} %get-tuple-element.153), channel_id=1, source_target_pairs={{0,1},{1,0},{2,3},{3,2},{4,5},{5,4},{6,7},{7,6},{8,9},{9,8},{10,11... | collective-permute-start | bytes 15728648 | tf_op jit(solution)/shard_map/ppermute | solution.py:1192
  206.9 40.3 %all-to-all-start.5 = ((bf16[8,64,512]{2,1,0:T(8,128)(2,1)}), bf16[8,64,512]{2,1,0:T(8,128)(2,1)}, u32[]{:S(2)}, u32[]{:S(2)}) async-start(bf16[8,64,512]{2,1,0:T(8,128)(2,1)} %get-tuple-element.147), calls=%async_computation.5 | async-start | bytes 1048576 | tf_op jit(solution)/shard_map/all_to_all | solution.py:1345
  229.6 47.6 %collective-permute-start.2 = (bf16[2,4,64,1024]{3,2,1,0:T(8,128)(2,1)}, bf16[2,4,64,1024]{3,2,1,0:T(8,128)(2,1)S(1)}, u32[]{:S(2)}, u32[]{:S(2)}) collective-permute-start(bf16[2,4,64,1024]{3,2,1,0:T(8,128)(2,1)} %get-tuple-element.150), channel_id=1, source_target_pairs={{0,8},{8,0},{16,24},{24,16},{1,9},{9,1},{17,25},{25,17},{2,10},{10... | collective-permute-start | bytes 3145736 | tf_op jit(solution)/shard_map/ppermute | solution.py:1192
  235.9 41.3 %collective-permute-start.3 = (bf16[2,4,64,1024]{3,2,1,0:T(8,128)(2,1)}, bf16[2,4,64,1024]{3,2,1,0:T(8,128)(2,1)S(1)}, u32[]{:S(2)}, u32[]{:S(2)}) collective-permute-start(bf16[2,4,64,1024]{3,2,1,0:T(8,128)(2,1)} %get-tuple-element.151), channel_id=1, source_target_pairs={{0,16},{8,24},{16,0},{24,8},{1,17},{9,25},{17,1},{25,9},{2,18},{10... | collective-permute-start | bytes 3145736 | tf_op jit(solution)/shard_map/ppermute | solution.py:1192
  245.0 80.7 %collective-permute-start.6 = (bf16[2,4,80,1024]{3,2,1,0:T(8,128)(2,1)}, bf16[2,4,80,1024]{3,2,1,0:T(8,128)(2,1)S(1)}, u32[]{:S(2)}, u32[]{:S(2)}) collective-permute-start(bf16[2,4,80,1024]{3,2,1,0:T(8,128)(2,1)} %get-tuple-element.154), channel_id=1, source_target_pairs={{0,8},{8,0},{16,24},{24,16},{1,9},{9,1},{17,25},{25,17},{2,10},{10... | collective-permute-start | bytes 3932168 | tf_op jit(solution)/shard_map/ppermute | solution.py:1192
  245.2 80.6 %collective-permute-start.7 = (bf16[2,4,80,1024]{3,2,1,0:T(8,128)(2,1)}, bf16[2,4,80,1024]{3,2,1,0:T(8,128)(2,1)}, u32[]{:S(2)}, u32[]{:S(2)}) collective-permute-start(bf16[2,4,80,1024]{3,2,1,0:T(8,128)(2,1)} %get-tuple-element.155), channel_id=1, source_target_pairs={{0,16},{8,24},{16,0},{24,8},{1,17},{9,25},{17,1},{25,9},{2,18},{10... | collective-permute-start | bytes 3932168 | tf_op jit(solution)/shard_map/ppermute | solution.py:1192
  247.2 44.4 %all-to-all-start.4 = ((bf16[8,64,512]{2,1,0:T(8,128)(2,1)}), bf16[8,64,512]{2,1,0:T(8,128)(2,1)}, u32[]{:S(2)}, u32[]{:S(2)}) async-start(bf16[8,64,512]{2,1,0:T(8,128)(2,1)} %get-tuple-element.146), calls=%async_computation.4 | async-start | bytes 1048576 | tf_op jit(solution)/shard_map/all_to_all | solution.py:1345
  283.4 39.0 %collective-permute-start.4 = (bf16[4,64,1024]{2,1,0:T(8,128)(2,1)}, bf16[4,64,1024]{2,1,0:T(8,128)(2,1)}, u32[]{:S(2)}, u32[]{:S(2)}) collective-permute-start(bf16[4,64,1024]{2,1,0:T(8,128)(2,1)} %get-tuple-element.162), channel_id=1, source_target_pairs={{0,16},{8,24},{16,0},{24,8},{1,17},{9,25},{17,1},{25,9},{2,18},{10... | collective-permute-start | bytes 1572872 | tf_op jit(solution)/shard_map/ppermute | solution.py:1192
  283.5 38.9 %collective-permute-start.5 = (bf16[4,64,1024]{2,1,0:T(8,128)(2,1)}, bf16[4,64,1024]{2,1,0:T(8,128)(2,1)}, u32[]{:S(2)}, u32[]{:S(2)}) collective-permute-start(bf16[4,64,1024]{2,1,0:T(8,128)(2,1)} %get-tuple-element.163), channel_id=1, source_target_pairs={{0,8},{8,0},{16,24},{24,16},{1,9},{9,1},{17,25},{25,17},{2,10},{10... | collective-permute-start | bytes 1572872 | tf_op jit(solution)/shard_map/ppermute | solution.py:1192
  291.6 42.8 %all-to-all-start.7 = ((bf16[8,192,512]{2,1,0:T(8,128)(2,1)}), bf16[8,192,512]{2,1,0:T(8,128)(2,1)S(1)}, u32[]{:S(2)}, u32[]{:S(2)}) async-start(bf16[8,192,512]{2,1,0:T(8,128)(2,1)} %attend_back.2), calls=%async_computation.7 | async-start | bytes 3145728 | tf_op jit(solution)/shard_map/all_to_all | solution.py:1357
  334.4 52.1 %all-to-all-start.6 = ((bf16[8,192,512]{2,1,0:T(8,128)(2,1)}), bf16[8,192,512]{2,1,0:T(8,128)(2,1)S(1)}, u32[]{:S(2)}, u32[]{:S(2)}) async-start(bf16[8,192,512]{2,1,0:T(8,128)(2,1)} %attend_back.3), calls=%async_computation.6 | async-start | bytes 3145728 | tf_op jit(solution)/shard_map/all_to_all | solution.py:1357
  355.6 23.3 %collective-permute-start.10 = (bf16[8,4,16,1536]{3,2,1,0:T(8,128)(2,1)}, bf16[8,4,16,1536]{3,2,1,0:T(8,128)(2,1)S(1)}, u32[]{:S(2)}, u32[]{:S(2)}) collective-permute-start(bf16[8,4,16,1536]{3,2,1,0:T(8,128)(2,1)} %get-tuple-element.189), channel_id=1, source_target_pairs={{0,1},{1,0},{2,3},{3,2},{4,5},{5,4},{6,7},{7,6},{8,9},{9,8},{10,11... | collective-permute-start | bytes 4718600 | tf_op jit(solution)/shard_map/ppermute | solution.py:1192
  478.7 51.3 %collective-permute-start.24 = (bf16[2,4,32,1024]{3,2,1,0:T(8,128)(2,1)}, bf16[2,4,32,1024]{3,2,1,0:T(8,128)(2,1)S(1)}, u32[]{:S(2)}, u32[]{:S(2)}) collective-permute-start(bf16[2,4,32,1024]{3,2,1,0:T(8,128)(2,1)} %get-tuple-element.217), channel_id=1, source_target_pairs={{0,8},{8,0},{16,24},{24,16},{1,9},{9,1},{17,25},{25,17},{2,10},{10... | collective-permute-start | bytes 1572872 | tf_op jit(solution)/shard_map/ppermute | solution.py:1192
  500.1 33.9 %collective-permute-start.25 = (bf16[2,4,32,1024]{3,2,1,0:T(8,128)(2,1)S(1)}, bf16[2,4,32,1024]{3,2,1,0:T(8,128)(2,1)S(1)}, u32[]{:S(2)}, u32[]{:S(2)}) collective-permute-start(bf16[2,4,32,1024]{3,2,1,0:T(8,128)(2,1)S(1)} %copy-done.58), channel_id=1, source_target_pairs={{0,16},{8,24},{16,0},{24,8},{1,17},{9,25},{17,1},{25,9},{2,18},{10... | collective-permute-start | bytes 1572872 | tf_op jit(solution)/shard_map/ppermute | solution.py:1192
  501.3 25.9 %collective-permute-start.59 = (bf16[2,80,1024]{2,1,0:T(8,128)(2,1)}, bf16[2,80,1024]{2,1,0:T(8,128)(2,1)}, u32[]{:S(2)}, u32[]{:S(2)}) collective-permute-start(bf16[2,80,1024]{2,1,0:T(8,128)(2,1)} %get-tuple-element.256), channel_id=1, source_target_pairs={{0,4},{1,5},{2,6},{3,7},{4,0},{5,1},{6,2},{7,3},{8,12},{9,13},{10,... | collective-permute-start | bytes 983048 | tf_op jit(solution)/shard_map/ppermute | solution.py:1192
  504.0 24.0 %collective-permute-start.60 = (bf16[2,80,1024]{2,1,0:T(8,128)(2,1)}, bf16[2,80,1024]{2,1,0:T(8,128)(2,1)S(1)}, u32[]{:S(2)}, u32[]{:S(2)}) collective-permute-start(bf16[2,80,1024]{2,1,0:T(8,128)(2,1)} %get-tuple-element.257), channel_id=1, source_target_pairs={{0,6},{1,7},{2,4},{3,5},{4,2},{5,3},{6,0},{7,1},{8,14},{9,15},{10,... | collective-permute-start | bytes 983048 | tf_op jit(solution)/shard_map/ppermute | solution.py:1192
  512.6 27.7 %collective-permute-start.55 = (bf16[2,64,1024]{2,1,0:T(8,128)(2,1)S(1)}, bf16[2,64,1024]{2,1,0:T(8,128)(2,1)S(1)}, u32[]{:S(2)}, u32[]{:S(2)}) collective-permute-start(bf16[2,64,1024]{2,1,0:T(8,128)(2,1)S(1)} %copy-done.15), channel_id=1, source_target_pairs={{0,8},{8,0},{16,24},{24,16},{1,9},{9,1},{17,25},{25,17},{2,10},{10... | collective-permute-start | bytes 786440 | tf_op jit(solution)/shard_map/ppermute | solution.py:1192
  534.0 22.8 %collective-permute-start.61 = (bf16[2,80,1024]{2,1,0:T(8,128)(2,1)}, bf16[2,80,1024]{2,1,0:T(8,128)(2,1)S(1)}, u32[]{:S(2)}, u32[]{:S(2)}) collective-permute-start(bf16[2,80,1024]{2,1,0:T(8,128)(2,1)} %fourth_sum.9.refs_4_), channel_id=1, source_target_pairs={{0,8},{8,0},{16,24},{24,16},{1,9},{9,1},{17,25},{25,17},{2,10},{10... | collective-permute-start | bytes 983048 | tf_op jit(solution)/shard_map/ppermute | solution.py:1192
  542.9 26.8 %collective-permute-start.27 = (bf16[4,32,1024]{2,1,0:T(8,128)(2,1)}, bf16[4,32,1024]{2,1,0:T(8,128)(2,1)S(1)}, u32[]{:S(2)}, u32[]{:S(2)}) collective-permute-start(bf16[4,32,1024]{2,1,0:T(8,128)(2,1)} %get-tuple-element.223), channel_id=1, source_target_pairs={{0,8},{8,0},{16,24},{24,16},{1,9},{9,1},{17,25},{25,17},{2,10},{10... | collective-permute-start | bytes 786440 | tf_op jit(solution)/shard_map/ppermute | solution.py:1192
  554.4 29.5 %collective-permute-start.62 = (bf16[2,80,1024]{2,1,0:T(8,128)(2,1)S(1)}, bf16[2,80,1024]{2,1,0:T(8,128)(2,1)S(1)}, u32[]{:S(2)}, u32[]{:S(2)}) collective-permute-start(bf16[2,80,1024]{2,1,0:T(8,128)(2,1)S(1)} %copy-done.14), channel_id=1, source_target_pairs={{0,16},{8,24},{16,0},{24,8},{1,17},{9,25},{17,1},{25,9},{2,18},{10... | collective-permute-start | bytes 983048 | tf_op jit(solution)/shard_map/ppermute | solution.py:1192
  555.3 29.7 %collective-permute-start.63 = (bf16[2,80,1024]{2,1,0:T(8,128)(2,1)S(1)}, bf16[2,80,1024]{2,1,0:T(8,128)(2,1)S(1)}, u32[]{:S(2)}, u32[]{:S(2)}) collective-permute-start(bf16[2,80,1024]{2,1,0:T(8,128)(2,1)S(1)} %copy-done.14), channel_id=1, source_target_pairs={{0,24},{8,16},{16,8},{24,0},{1,25},{9,17},{17,9},{25,1},{2,26},{10... | collective-permute-start | bytes 983048 | tf_op jit(solution)/shard_map/ppermute | solution.py:1192
  (135 other events, 1265.0 us)
